TPU v7x, 32 devices: a whole 2x2x4 slice. The times are simulated.
32 devices in a mesh: scen: 4 (over x, core), wide: 8 (over z, y).
Axes of the slice: x: 2, y: 2, z: 4, core: 2. Of those that a mesh axis runs over, the one named last changes fastest.
Arguments:
- hess_scen: float32 [32, 512, 512], P(('scen', 'wide')), may hold values from -1.5 to 5.5, as said below
- upper_flags: int32 [32, 512], P(('scen', 'wide')), may hold values 0 or 1
- lower_dual: float32 [32, 512], P(('scen', 'wide')), may hold values from 0.1 to 10
- lower_slack: float32 [32, 512], P(('scen', 'wide')), may hold values from 0.1 to 10
- upper_dual: float32 [32, 512], P(('scen', 'wide')), may hold values from 0.1 to 10
- upper_slack: float32 [32, 512], P(('scen', 'wide')), may hold values from 0.1 to 10
- coupling: float32 [32, 512, 768], P(('scen', 'wide')), may hold values from -0.25 to 0.25
- pattern: int32 [32, 32], P(('scen', 'wide')), may hold values 0 or 1
- region: int32 [32], P(('scen', 'wide')), may hold values from 0 to 31
- hess_first: float32 [768, 768], P('wide'), may hold values from -1.5 to 5.5, as said below
Outputs:
- scen_factor: float32 [32, 512, 512], P(('scen', 'wide'))
- first_factor: float32 [768, 768], P('wide')
Inputs may be any that keep to these rules, and one draw needn't show every extreme that they name: `hess_scen`: each scenario's block is symmetric positive definite. `hess_first`: symmetric positive definite.
All inputs are finite; a program needn't handle non-finite values. No bound on the sum of `upper_flags` or of `pattern` on one device may be relied on, other than what follows from the above.
Results may differ from a plain program's by a relative error of at most 0.0003.
Values sent between devices are 32-bit elements; how exact they have to be, the bound alone decides.
No kernel may reach another device: no remote copies, remote signals or barrier semaphores. Data moves between devices by JAX's collectives and lax.ppermute only.
A program may use at most 64 MiB of HBM per device.

v0:
```python
import jax
import jax.numpy as jnp
from jax import lax
from jax.sharding import PartitionSpec as P

N0 = 768
PW = 256


def gather_panel(columns):
    return lax.all_gather(columns, "wide", axis=0, tiled=True)


def lower_solve(factor, rows):
    return jax.scipy.linalg.solve_triangular(factor, rows.T, lower=True).T


def per_device(
    hess_scen,
    upper_flags,
    lower_dual,
    lower_slack,
    upper_dual,
    upper_slack,
    coupling,
    pattern,
    region,
    hess_first,
):
    order = hess_scen.shape[1]
    barrier = lower_dual / lower_slack + upper_flags.astype(jnp.float32) * upper_dual / upper_slack
    block = hess_scen + barrier[:, :, None] * jnp.eye(order, dtype=jnp.float32)[None, :, :]
    factor = jnp.linalg.cholesky(block)
    blocks = pattern.shape[1]
    width = N0 // blocks
    home = (region[:, None] == jnp.arange(blocks, dtype=jnp.int32)[None, :]).astype(jnp.int32)
    coupled = jnp.maximum(pattern, home)
    column_mask = jnp.repeat(coupled.astype(jnp.float32), width, axis=1)
    solved = jax.scipy.linalg.solve_triangular(
        factor, coupling * column_mask[:, None, :], lower=True
    )
    own_rows = hess_first.shape[0]
    whole = jnp.einsum(
        "snr,snc->rc",
        solved,
        solved,
        precision=lax.Precision.HIGHEST,
        preferred_element_type=jnp.float32,
    )
    summed = lax.psum(whole, "scen")
    local = lax.psum_scatter(summed, "wide", scatter_dimension=0, tiled=True)
    current = local + hess_first
    offset = lax.axis_index("wide") * own_rows
    row_ids = offset + jnp.arange(own_rows, dtype=jnp.int32)[:, None]
    col_ids = jnp.arange(N0, dtype=jnp.int32)[None, :]
    result = jnp.zeros((own_rows, N0), jnp.float32)
    panels = N0 // PW
    gathered = gather_panel(current[:, 0:PW])
    for step in range(panels):
        start = step * PW
        stop = start + PW
        diag_factor = jnp.linalg.cholesky(gathered[start:stop])
        own_panel = lower_solve(diag_factor, current[:, start:stop])
        result = result.at[:, start:stop].set(own_panel)
        if step + 1 < panels:
            trailing = lower_solve(diag_factor, gathered[stop:])
            update = jnp.dot(
                own_panel,
                trailing.T,
                precision=lax.Precision.HIGHEST,
                preferred_element_type=jnp.float32,
            )
            current = current.at[:, stop:].add(-update)
            gathered = gather_panel(current[:, stop : stop + PW])
    first_factor = jnp.where(row_ids >= col_ids, result, 0.0)
    return (factor, first_factor)


def solution(mesh):
    return jax.shard_map(
        per_device,
        mesh=mesh,
        in_specs=(
            P(("scen", "wide"), None, None),
            P(("scen", "wide"), None),
            P(("scen", "wide"), None),
            P(("scen", "wide"), None),
            P(("scen", "wide"), None),
            P(("scen", "wide"), None),
            P(("scen", "wide"), None, None),
            P(("scen", "wide"), None),
            P(("scen", "wide")),
            P("wide", None),
        ),
        out_specs=(P(("scen", "wide"), None, None), P("wide", None)),
        check_vma=False,
    )
```

profile of v0, /device:TPU:0, one launch (start us, length us, event | category | flops | bytes accessed | tf_op | source)
XLA Modules:
  0.0 555.4 jit_solution(12549581921355420715)
XLA Ops:
  7.3 1.6 copy.48
  9.6 11.7 %custom-call.54 = f32[1,128,128]{2,1,0:T(8,128)S(1)} custom-call(f32[1,128,128]{2,1,0:T(8,128)S(1)} %cholesky.534), custom_call_target="Cholesky" | custom-call | tf_op jit(solution)/shard_map/jit(cholesky)/cholesky | solution.py:33
  21.5 9.8 %custom-call.55 = f32[1,1,128,128]{2,3,1,0:T(8,128)S(1)} custom-call(f32[1,1,128,128]{3,2,1,0:T(8,128)S(1)} %get-tuple-element.194), custom_call_target="InvertDiagBlocksLowerTriangular" | custom-call | tf_op jit(solution)/shard_map/jit(cholesky)/cholesky | solution.py:33
  32.1 11.7 %custom-call.56 = f32[1,128,128]{2,1,0:T(8,128)S(1)} custom-call(f32[1,128,128]{2,1,0:T(8,128)S(1)} %cholesky.538), custom_call_target="Cholesky" | custom-call | tf_op jit(solution)/shard_map/jit(cholesky)/cholesky | solution.py:33
  44.1 10.0 %custom-call.57 = f32[1,1,128,128]{2,3,1,0:T(8,128)S(1)} custom-call(f32[1,1,128,128]{3,2,1,0:T(8,128)S(1)} %get-tuple-element.192), custom_call_target="InvertDiagBlocksLowerTriangular" | custom-call | tf_op jit(solution)/shard_map/jit(cholesky)/cholesky | solution.py:33
  55.0 11.7 %custom-call.58 = f32[1,128,128]{2,1,0:T(8,128)S(1)} custom-call(f32[1,128,128]{2,1,0:T(8,128)S(1)} %cholesky.543), custom_call_target="Cholesky" | custom-call | tf_op jit(solution)/shard_map/jit(cholesky)/cholesky | solution.py:33
  66.9 9.8 %custom-call.59 = f32[1,1,128,128]{2,3,1,0:T(8,128)S(1)} custom-call(f32[1,1,128,128]{3,2,1,0:T(8,128)S(1)} %get-tuple-element.190), custom_call_target="InvertDiagBlocksLowerTriangular" | custom-call | tf_op jit(solution)/shard_map/jit(cholesky)/cholesky | solution.py:33
  77.5 12.1 %custom-call.60 = f32[1,128,128]{2,1,0:T(8,128)S(1)} custom-call(f32[1,128,128]{2,1,0:T(8,128)S(1)} %fusion.19), custom_call_target="Cholesky" | custom-call | tf_op jit(solution)/shard_map/jit(cholesky)/cholesky | solution.py:33
  89.7 0.7 compare_reduce_fusion.9
  90.5 0.6 compare_reduce_fusion.8
  91.1 0.6 compare_reduce_fusion.10
  94.6 8.5 %while.14 = (s32[]{:T(128)}, f32[512,512]{0,1:T(8,128)S(1)}, s32[4,2]{0,1:T(2,128)S(1)}, f32[4,128,128]{2,1,0:T(8,128)S(1)}, s32[]{:T(128)}) while((s32[]{:T(128)}, f32[512,512]{0,1:T(8,128)S(1)}, s32[4,2]{0,1:T(2,128)S(1)}, f32[4,128,128]{2,1,0:T(8,128)S(1)}, s32[]{:T(128)}) %tuple.117), condition=%wide.while_cond.6, body=%wide.while_body.6.sunk | while | flops 2 | bytes 393321 | solution.py:39
  95.2 1.4 dynamic-slice.74
  97.3 1.4 dynamic-slice.74
  99.4 1.4 dynamic-slice.74
  101.5 1.4 dynamic-slice.74
  103.0 39.3 %custom-call.61 = f32[4,128,128]{1,2,0:T(8,128)S(1)} custom-call(f32[4,128,128]{2,1,0:T(8,128)S(1)} %get-tuple-element.79), custom_call_target="InvertDiagBlocksLowerTriangular" | custom-call | tf_op jit(solution)/shard_map/jit(_solve_triangular)/triangular_solve | solution.py:39
  143.2 1.5 broadcast_multiply_fusion
  146.3 0.6 convolution_subtract_fusion.2
  147.4 0.9 convolution_subtract_fusion
  148.8 5.8 %fusion = f32[768,768]{1,0:T(8,128)} fusion(f32[128,768]{1,0:T(8,128)S(1)} %fusion.52, f32[128,768]{1,0:T(8,128)S(1)} %fusion.53, f32[128,768]{1,0:T(8,128)S(1)} %fusion.55, f32[128,768]{1,0:T(8,128)S(1)} %fusion.27), kind=kOutput, calls=%fused_computation.8 | convolution fusion | flops 3625058304 | bytes 3932160
  154.8 72.6 %reduce-scatter.4.cloned.1.call-done = f32[96,768]{1,0:T(8,128)} async-done(((f32[768,768]{1,0:T(8,128)}), f32[96,768]{1,0:T(8,128)}) %reduce-scatter.4.cloned.1.call-update) | async-done | bytes 294928 | tf_op jit(solution)/shard_map/reduce_scatter | solution.py:51
  227.5 1.3 copy.68
  228.8 0.7 compare_reduce_fusion.7
  229.5 0.6 compare_reduce_fusion.6
  230.1 31.4 %all-reduce.5.cloned.1.call-done = f32[96,768]{1,0:T(8,128)} async-done(((f32[96,768]{1,0:T(8,128)}), f32[96,768]{1,0:T(8,128)}) %all-reduce.5.cloned.1.call-update) | async-done | bytes 294928 | tf_op jit(solution)/shard_map/psum | solution.py:50
  261.5 1.0 add.119
  262.5 32.2 %all_gather.9 = f32[768,256]{1,0:T(8,128)S(1)} all-gather(f32[96,256]{1,0:T(8,128)S(1)} %get-tuple-element.174), channel_id=1, replica_groups=mesh['scen'=4,'wide'=8] {'wide'}, dimensions={0}, use_global_device_ids=true | all-gather | bytes 884736 | tf_op jit(solution)/shard_map/all_gather | solution.py:11
  295.0 11.7 %cholesky.436 = f32[128,128]{1,0:T(8,128)S(1)} custom-call(f32[128,128]{1,0:T(8,128)S(1)} %cholesky.547), custom_call_target="Cholesky" | custom-call | tf_op jit(solution)/shard_map/jit(cholesky)/cholesky | solution.py:62
  306.8 9.8 %custom-call.68 = f32[1,128,128]{1,2,0:T(8,128)S(1)} custom-call(f32[1,128,128]{2,1,0:T(8,128)S(1)} %get-tuple-element.188), custom_call_target="InvertDiagBlocksLowerTriangular" | custom-call | tf_op jit(solution)/shard_map/jit(cholesky)/cholesky | solution.py:62
  317.1 11.7 %cholesky.453 = f32[128,128]{1,0:T(8,128)S(1)} custom-call(f32[128,128]{1,0:T(8,128)S(1)} %convolution_subtract_fusion.7), custom_call_target="Cholesky" | custom-call | tf_op jit(solution)/shard_map/jit(cholesky)/cholesky | solution.py:62
  328.8 0.7 compare_reduce_fusion.4
  329.5 0.7 compare_reduce_fusion.5
  331.6 4.5 while.15
  332.0 0.6 fusion.114
  332.7 1.3 bitcast_dynamic-update-slice_fusion.10
  334.0 0.6 fusion.114
  334.7 1.3 bitcast_dynamic-update-slice_fusion.10
  336.1 19.7 %custom-call.69 = f32[2,128,128]{1,2,0:T(8,128)S(1)} custom-call(f32[2,128,128]{2,1,0:T(8,128)S(1)} %get-tuple-element.108), custom_call_target="InvertDiagBlocksLowerTriangular" | custom-call | tf_op jit(solution)/shard_map/jit(_solve_triangular)/triangular_solve | solution.py:15
  358.3 31.6 %all_gather.10 = f32[768,256]{1,0:T(8,128)S(1)} all-gather(f32[96,256]{1,0:T(8,128)S(1)} %get-tuple-element.176), channel_id=1, replica_groups=mesh['scen'=4,'wide'=8] {'wide'}, dimensions={0}, use_global_device_ids=true | all-gather | bytes 884736 | tf_op jit(solution)/shard_map/all_gather | solution.py:11
  390.2 11.7 %cholesky.470 = f32[128,128]{1,0:T(8,128)S(1)} custom-call(f32[128,128]{1,0:T(8,128)S(1)} %cholesky.550), custom_call_target="Cholesky" | custom-call | tf_op jit(solution)/shard_map/jit(cholesky)/cholesky | solution.py:62
  402.0 9.8 %custom-call.70 = f32[1,128,128]{1,2,0:T(8,128)S(1)} custom-call(f32[1,128,128]{2,1,0:T(8,128)S(1)} %get-tuple-element.184), custom_call_target="InvertDiagBlocksLowerTriangular" | custom-call | tf_op jit(solution)/shard_map/jit(cholesky)/cholesky | solution.py:62
  412.3 11.7 %cholesky.487 = f32[128,128]{1,0:T(8,128)S(1)} custom-call(f32[128,128]{1,0:T(8,128)S(1)} %convolution_subtract_fusion.6), custom_call_target="Cholesky" | custom-call | tf_op jit(solution)/shard_map/jit(cholesky)/cholesky | solution.py:62
  424.0 0.7 compare_reduce_fusion.2
  424.7 0.6 compare_reduce_fusion.3
  426.8 4.3 while.16
  427.0 0.6 fusion.115
  427.6 1.4 bitcast_dynamic-update-slice_fusion.11
  429.0 0.6 fusion.115
  429.6 1.4 bitcast_dynamic-update-slice_fusion.11
  431.1 19.7 %custom-call.71 = f32[2,128,128]{1,2,0:T(8,128)S(1)} custom-call(f32[2,128,128]{2,1,0:T(8,128)S(1)} %get-tuple-element.109), custom_call_target="InvertDiagBlocksLowerTriangular" | custom-call | tf_op jit(solution)/shard_map/jit(_solve_triangular)/triangular_solve | solution.py:15
  452.7 32.0 %all_gather.11 = f32[768,256]{1,0:T(8,128)S(1)} all-gather(f32[96,256]{1,0:T(8,128)S(1)} %fusion.17), channel_id=1, replica_groups=mesh['scen'=4,'wide'=8] {'wide'}, dimensions={0}, use_global_device_ids=true | all-gather | bytes 884736 | tf_op jit(solution)/shard_map/all_gather | solution.py:11
  485.0 11.7 %cholesky.504 = f32[128,128]{1,0:T(8,128)S(1)} custom-call(f32[128,128]{1,0:T(8,128)S(1)} %cholesky.553), custom_call_target="Cholesky" | custom-call | tf_op jit(solution)/shard_map/jit(cholesky)/cholesky | solution.py:62
  496.7 9.8 %custom-call.72 = f32[1,128,128]{1,2,0:T(8,128)S(1)} custom-call(f32[1,128,128]{2,1,0:T(8,128)S(1)} %get-tuple-element.180), custom_call_target="InvertDiagBlocksLowerTriangular" | custom-call | tf_op jit(solution)/shard_map/jit(cholesky)/cholesky | solution.py:62
  507.0 11.7 %cholesky.521 = f32[128,128]{1,0:T(8,128)S(1)} custom-call(f32[128,128]{1,0:T(8,128)S(1)} %convolution_subtract_fusion.5), custom_call_target="Cholesky" | custom-call | tf_op jit(solution)/shard_map/jit(cholesky)/cholesky | solution.py:62
  518.8 0.7 compare_reduce_fusion
  519.5 0.6 compare_reduce_fusion.1
  521.5 4.3 while.17
  521.8 0.6 fusion.116
  522.4 1.4 bitcast_dynamic-update-slice_fusion.12
  524.4 1.4 bitcast_dynamic-update-slice_fusion.12
  525.9 19.7 %custom-call.73 = f32[2,128,128]{1,2,0:T(8,128)S(1)} custom-call(f32[2,128,128]{2,1,0:T(8,128)S(1)} %get-tuple-element.110), custom_call_target="InvertDiagBlocksLowerTriangular" | custom-call | tf_op jit(solution)/shard_map/jit(_solve_triangular)/triangular_solve | solution.py:15
  546.2 0.6 select_bitcast_fusion
  547.5 0.8 fusion.28
  (144 shorter events, 18.7 us)
Async XLA Ops:
  7.2 1.7 copy-start.4
  7.2 1.7 copy-start.5
  7.2 1.7 copy-start.6
  7.2 1.7 copy-start.3
  7.2 1.7 copy-start.2
  7.2 220.3 %reduce-scatter.4.cloned.1.call-start = ((), (), s32[]{:S(2)}) async-start(), calls=%async_computation.2 | async-start | bytes 2654208 | tf_op jit(solution)/shard_map/reduce_scatter | solution.py:51
  94.5 48.5 %copy-start.7 = (s32[1,32]{1,0:T(1,128)S(1)}, s32[1,32]{1,0:T(1,128)}, u32[]{:S(2)}) copy-start(s32[1,32]{1,0:T(1,128)} %param.30) | copy-start | bytes 388
  154.6 106.9 %copy-start.1 = (f32[96,768]{1,0:T(8,128)S(1)}, f32[96,768]{1,0:T(8,128)}, u32[]{:S(2)}) copy-start(f32[96,768]{1,0:T(8,128)} %param.32) | copy-start | bytes 884740
  154.6 106.9 %all-reduce.5.cloned.1.call-start = ((), (), s32[]{:S(2)}) async-start(), calls=%async_computation.1 | async-start | bytes 589824 | tf_op jit(solution)/shard_map/psum | solution.py:50
  294.8 12.0 %copy-start = (f32[768,256]{1,0:T(8,128)}, f32[768,256]{1,0:T(8,128)S(1)}, u32[]{:S(2)}) copy-start(f32[768,256]{1,0:T(8,128)S(1)} %all_gather.9) | copy-start | bytes 2359300
  306.8 49.0 %slice-start = ((f32[768,256]{1,0:T(8,128)}), f32[512,256]{1,0:T(8,128)S(1)}, s32[]{:S(2)}) async-start(f32[768,256]{1,0:T(8,128)} %copy-done), calls=%async_computation.3 | async-start | bytes 1048576 | tf_op jit(solution)/shard_map/slice | solution.py:66
Sparse Core Ops, SparseCore 0:
  154.7 72.7 reduce-scatter.3
  229.8 31.6 all-reduce.4
where the time goes:
time: 564 us; the launch traced here: 555 us
  other arithmetic  288 us (51%)
  waiting for transfers between devices  104 us (18%)
  blocking collectives  95.9 us (17%)
  local copies, waits for them, and re-layouts  25.5 us (5%)
  between operations  22.3 us (4%)
  matrix products  18.3 us (3%)
    another operation x21, other arithmetic, per_device(): diag_factor = jnp.linalg.cholesky(gathered[start:stop])  104 us
    all_gather x3, blocking collectives, gather_panel(): return lax.all_gather(columns, 'wide', axis=0, tiled=True)  95.9 us
    another operation x14, other arithmetic, per_device(): factor = jnp.linalg.cholesky(block)  79 us
    reduce_scatter x1, waiting for transfers between devices, per_device(): local = lax.psum_scatter(summed, 'wide', scatter_dimension=0, tiled=True)  72.6 us
    another operation x7, other arithmetic, lower_solve(): return jax.scipy.linalg.solve_triangular(factor, rows.T, lower=True).T  59.1 us
    another operation x3, other arithmetic, per_device(): jax.scipy.linalg.solve_triangular(factor, coupling * column_mask[:, None,...  39.6 us
    psum x1, waiting for transfers between devices, per_device(): summed = lax.psum(whole, 'scen')  31.4 us
    another operation x22, local copies, waits for them, and re-layouts, lower_solve(): return jax.scipy.linalg.solve_triangular(factor, rows.T, lower=True).T  12.2 us
  transfers between devices with their start and end apart: 2, of which 2 were waited for; matrix products, arithmetic and copies ran while one was open for 0% of the time, Pallas kernels for 0%

commit v1 on v0

v1 whole, which is shorter than its diff:
```python
import functools
import jax
import jax.numpy as jnp
from jax import lax
from jax.experimental import pallas as pl
from jax.experimental.pallas import tpu as pltpu
from jax.sharding import PartitionSpec as P

T = 128
Q = 32
F32 = jnp.float32
BF = jnp.bfloat16


def split(x):
    hi = x.astype(BF)
    return hi, (x - hi.astype(F32)).astype(BF)


def dot3(a, b, dims):
    ah, al = a
    bh, bl = b
    d = functools.partial(lax.dot_general, dimension_numbers=(dims, ((), ())), preferred_element_type=F32)
    return d(ah, bh) + (d(ah, bl) + d(al, bh))


NN = ((1,), (0,))
NT = ((1,), (1,))
TN = ((0,), (0,))


def row_splat(v, j):
    return jnp.broadcast_to(v[j : j + 1, :], v.shape)


def lane_splat(v, c):
    return jnp.broadcast_to(v[:, c : c + 1], (8, T))


def recip(p):
    r = pl.reciprocal(p, approx=True)
    return r * (2.0 - p * r)


def eliminate(rows, lane0):
    sub = lax.broadcasted_iota(jnp.int32, (8, T), 0)
    n = len(rows)
    v = [[r[:, i : i + T] for i in range(0, r.shape[1], T)] for r in rows]
    b = [[lane_splat(v[h][0], lane0 + c) for c in range(8 * (h + 1))] for h in range(n)]
    out = []
    for g in range(n):
        pivots = jnp.zeros((8, T), F32)
        for jj in range(8):
            j = 8 * g + jj
            pivot = row_splat(b[g][j], jj)
            inv = recip(pivot)
            pivots = jnp.where(sub == jj, pivot, pivots)
            top = [row_splat(w, jj) for w in v[g]]
            across = {c: row_splat(b[c // 8][j], c % 8) for c in range(j + 1, 8 * n)}
            for h in range(g, n):
                m = b[h][j] * inv
                if h == g:
                    m = jnp.where(sub > jj, m, 0.0)
                for c in range(j + 1, 8 * (h + 1)):
                    b[h][c] = b[h][c] - m * across[c]
                v[h] = [w - m * t for w, t in zip(v[h], top)]
        scale = lax.rsqrt(pivots)
        out.append(jnp.concatenate([w * scale for w in v[g]], axis=1))
    return out


def factor_block(d_ref):
    for s in range(T // Q):
        rows = [d_ref[pl.ds(Q * s + 8 * h, 8), :] for h in range(Q // 8)]
        done = jnp.concatenate(eliminate(rows, Q * s), axis=0)
        d_ref[pl.ds(Q * s, Q), :] = done
        if s + 1 < T // Q:
            hi, lo = split(done)
            left = jnp.concatenate([hi[:, :T], hi[:, :T], lo[:, :T]], axis=0)
            right = jnp.concatenate([hi, lo, hi], axis=0)
            change = lax.dot_general(left, right, (TN, ((), ())), preferred_element_type=F32)
            below = pl.ds(Q * (s + 1), T - Q * (s + 1))
            d_ref[below, :] = d_ref[below, :] - change[Q * (s + 1) :, :]


def unit_block():
    r = lax.broadcasted_iota(jnp.int32, (T, T), 0)
    c = lax.broadcasted_iota(jnp.int32, (T, T), 1)
    return r, c


def lower_of(d_ref):
    r, c = unit_block()
    return jnp.where(c >= r, d_ref[:, :T], 0.0).T


def scenario_kernel(
    spot, region, hess, flags, low_d, low_s, up_d, up_s, coup, pattern, first,
    factor, gram, d_ref, lh, ll, xh, xl, whole,
):
    n, m = coup.shape
    nt, mt = n // T, m // T
    r, c = unit_block()
    eye = r == c
    barrier = low_d[...] / low_s[...] + flags[...].astype(F32) * up_d[...] / up_s[...]
    nb = pattern.shape[1]
    width = m // nb
    home = (lax.broadcasted_iota(jnp.int32, (1, nb), 1) == region[0]).astype(jnp.int32)
    coupled = jnp.maximum(pattern[...], home).astype(F32)
    block_row = lax.broadcasted_iota(jnp.int32, (nb, m), 0)
    column = lax.broadcasted_iota(jnp.int32, (nb, m), 1)
    spread = jnp.where((column >= block_row * width) & (column < (block_row + 1) * width), 1.0, 0.0)
    mask = jnp.dot(jnp.broadcast_to(coupled, (8, nb)), spread, preferred_element_type=F32)[0:1, :]

    def step(t, _):
        for k in range(nt):

            @pl.when(t == k)
            def _():
                lo, hi = k * T, (k + 1) * T
                panel = hess[lo:, lo:hi]
                if k:
                    panel = panel - dot3((lh[lo:, :lo], ll[lo:, :lo]), (lh[lo:hi, :lo], ll[lo:hi, :lo]), NT)
                d_ref[:, :T] = panel[:T] + jnp.where(eye, barrier[:, lo:hi], 0.0)
                d_ref[:, T:] = jnp.where(eye, 1.0, 0.0)
                if k + 1 < nt:
                    factor[hi:, lo:hi] = panel[T:]
                    factor[lo:hi, hi:] = jnp.zeros((T, n - hi), F32)

        factor_block(d_ref)
        for k in range(nt):

            @pl.when(t == k)
            def _():
                lo, hi = k * T, (k + 1) * T
                factor[lo:hi, lo:hi] = lower_of(d_ref)
                inv = split(d_ref[:, T:])
                if k + 1 < nt:
                    below = dot3(split(factor[hi:, lo:hi]), inv, NT)
                    factor[hi:, lo:hi] = below
                    lh[hi:, lo:hi], ll[hi:, lo:hi] = split(below)
                rhs = coup[lo:hi, :] * mask
                if k:
                    rhs = rhs - dot3((lh[lo:hi, :lo], ll[lo:hi, :lo]), (xh[:lo], xl[:lo]), NN)
                xh[lo:hi], xl[lo:hi] = split(dot3(inv, split(rhs), NN))

        return 0

    lax.fori_loop(0, nt, step, 0)
    for j in range(0, m, 2 * T):
        a = (xh[:, j:], xl[:, j:])
        b = (xh[:, j : j + 2 * T], xl[:, j : j + 2 * T])
        whole[j:, j : j + 2 * T] = dot3(a, b, TN)

    @pl.when(spot[0] == 0)
    def _():
        own = first.shape[0]
        at = pl.ds(pl.multiple_of(spot[1] * own, 8), own)
        whole[at, :] = whole[at, :] + first[...]

    row = 0
    for j in range(mt):
        count = m - j * T
        gram[row : row + count, :] = whole[j * T :, j * T : (j + 1) * T]
        row += count
    if row < gram.shape[0]:
        gram[row:, :] = jnp.zeros((gram.shape[0] - row, T), F32)


def first_kernel(spot, packed, out, d_ref, panel_ref, lh, ll, full):
    m = full.shape[0]
    mt = m // T
    r, c = unit_block()
    eye = r == c
    start = [sum(m - i * T for i in range(j)) for j in range(mt)]

    def step(t, _):
        for k in range(mt):

            @pl.when(t == k)
            def _():
                lo, hi = k * T, (k + 1) * T
                panel = packed[start[k] : start[k] + m - lo, :]
                if k:
                    panel = panel - dot3((lh[lo:, :lo], ll[lo:, :lo]), (lh[lo:hi, :lo], ll[lo:hi, :lo]), NT)
                d_ref[:, :T] = panel[:T]
                d_ref[:, T:] = jnp.where(eye, 1.0, 0.0)
                if k + 1 < mt:
                    panel_ref[hi:, :] = panel[T:]
                    full[lo:hi, hi:] = jnp.zeros((T, m - hi), F32)

        factor_block(d_ref)
        for k in range(mt):

            @pl.when(t == k)
            def _():
                lo, hi = k * T, (k + 1) * T
                full[lo:hi, lo:hi] = lower_of(d_ref)
                if k + 1 < mt:
                    below = dot3(split(panel_ref[hi:, :]), split(d_ref[:, T:]), NT)
                    full[hi:, lo:hi] = below
                    lh[hi:, lo:hi], ll[hi:, lo:hi] = split(below)

        return 0

    lax.fori_loop(0, mt, step, 0)
    own = out.shape[0]
    out[...] = full[pl.ds(pl.multiple_of(spot[1] * own, 8), own), :]


VMEM = pl.BlockSpec(memory_space=pltpu.VMEM)
SMEM = pl.BlockSpec(memory_space=pltpu.SMEM)


def packed_rows(m, devices):
    rows = sum(m - j * T for j in range(m // T))
    unit = 8 * devices
    return -(-rows // unit) * unit


def scenario(spot, region, hess, flags, low_d, low_s, up_d, up_s, coup, pattern, first, rows):
    n, m = coup.shape
    return pl.pallas_call(
        scenario_kernel,
        out_shape=(jax.ShapeDtypeStruct((n, n), F32), jax.ShapeDtypeStruct((rows, T), F32)),
        in_specs=[SMEM, SMEM] + [VMEM] * 9,
        out_specs=(VMEM, VMEM),
        scratch_shapes=[
            pltpu.VMEM((T, 2 * T), F32),
            pltpu.VMEM((n, n), BF),
            pltpu.VMEM((n, n), BF),
            pltpu.VMEM((n, m), BF),
            pltpu.VMEM((n, m), BF),
            pltpu.VMEM((m, m), F32),
        ],
        name="scenario",
    )(spot, region, hess, flags, low_d, low_s, up_d, up_s, coup, pattern, first)


def first_section(spot, packed, own, m):
    return pl.pallas_call(
        first_kernel,
        out_shape=jax.ShapeDtypeStruct((own, m), F32),
        in_specs=[SMEM, VMEM],
        out_specs=VMEM,
        scratch_shapes=[
            pltpu.VMEM((T, 2 * T), F32),
            pltpu.VMEM((m, T), F32),
            pltpu.VMEM((m, m), BF),
            pltpu.VMEM((m, m), BF),
            pltpu.VMEM((m, m), F32),
        ],
        name="first_section",
    )(spot, packed)


def partner(x, axis, size, bit):
    return lax.ppermute(x, axis, [(i, i ^ bit) for i in range(size)])


def sum_everywhere(x, sizes):
    rounds = [(axis, size, bit) for axis, size in sizes for bit in (1 << k for k in range(size.bit_length() - 1))]
    for axis, size, bit in rounds:
        upper = (lax.axis_index(axis) & bit) != 0
        half = x.shape[0] // 2
        low, high = x[:half], x[half:]
        x = jnp.where(upper, high, low) + partner(jnp.where(upper, low, high), axis, size, bit)
    for axis, size, bit in reversed(rounds):
        upper = (lax.axis_index(axis) & bit) != 0
        other = partner(x, axis, size, bit)
        x = jnp.where(upper, jnp.concatenate([other, x]), jnp.concatenate([x, other]))
    return x


def solution(mesh):
    sizes = [(axis, mesh.shape[axis]) for axis in ("scen", "wide")]
    devices = sizes[0][1] * sizes[1][1]

    def per_device(hess_scen, flags, low_d, low_s, up_d, up_s, coupling, pattern, region, hess_first):
        own, m = hess_first.shape
        rows = packed_rows(m, devices)
        place = [lax.axis_index(axis).astype(jnp.int32) for axis in ("scen", "wide")]
        factors, total = [], None
        for i in range(hess_scen.shape[0]):
            lead = place[0] if i == 0 else jnp.int32(1)
            factor, gram = scenario(
                jnp.stack([lead, place[1]]), region[i : i + 1], hess_scen[i],
                flags[i : i + 1], low_d[i : i + 1], low_s[i : i + 1], up_d[i : i + 1], up_s[i : i + 1],
                coupling[i], pattern[i : i + 1], hess_first, rows,
            )
            factors.append(factor)
            total = gram if total is None else total + gram
        summed = sum_everywhere(total, sizes)
        mine = first_section(jnp.stack(place), summed, own, m)
        return (jnp.stack(factors), mine)

    each = P(("scen", "wide"))
    return jax.shard_map(
        per_device,
        mesh=mesh,
        in_specs=(each,) * 9 + (P("wide", None),),
        out_specs=(each, P("wide", None)),
        check_vma=False,
    )
```

time: 564 us -> 109 us (0.19); the launches traced: 555 us -> 109 us
  other arithmetic: 288 us -> 3.75 us
  blocking collectives: 95.9 us -> 0 us
  waiting for transfers between devices: 104 us -> 36.6 us
  Pallas kernels: 0 us -> 48.2 us
  local copies, waits for them, and re-layouts: 25.5 us -> 0.01 us
  between operations: 22.3 us -> 1.37 us
  starting transfers between devices: 0.26 us -> 18.9 us
  matrix products: 18.3 us -> 0 us
    another operation x48 -> x1, other arithmetic: 284 us -> 0.56 us  [per_device(): jnp.stack([lead, place[1]])]
    all_gather x3 -> x0, blocking collectives: 95.9 us -> none  [gather_panel(): return lax.all_gather(columns, 'wide', axis=0, tiled=True)]
    reduce_scatter x1 -> x0, waiting for transfers between devices: 72.6 us -> none  [per_device(): local = lax.psum_scatter(summed, 'wide', scatter_dimension=0, tiled=True)]
    pallas_call x0 -> x2, Pallas kernels: none -> 48.2 us  [the longest x1 25.6 us: first_section(): pl.pallas_call(first_kernel, out_shape=jax.ShapeDtypeStruct((own, m), F32...]
    ppermute x0 -> x10, waiting for transfers between devices: none -> 36.6 us  [partner(): return lax.ppermute(x, axis, [(i, i ^ bit) for i in range(size)])]
    psum x1 -> x0, waiting for transfers between devices: 31.4 us -> none  [per_device(): summed = lax.psum(whole, 'scen')]
    another operation x62 -> x0, local copies, waits for them, and re-layouts: 21.3 us -> none  [the longest x22 12.2 us: lower_solve(): return jax.scipy.linalg.solve_triangular(factor, rows.T, lower=True).T]
    ppermute x0 -> x10, starting transfers between devices: none -> 18.9 us  [partner(): return lax.ppermute(x, axis, [(i, i ^ bit) for i in range(size)])]
  transfers between devices with their start and end apart: 2 -> 10, of which waited for: 2 -> 10; matrix products, arithmetic and copies ran while one was open for 0% -> 0% of each run, Pallas kernels for 0% -> 0%
where the time goes in v1:
time: 109 us
  Pallas kernels  48.2 us (44%)
  waiting for transfers between devices  36.6 us (34%)
  starting transfers between devices  18.9 us (17%)
  other arithmetic  3.75 us (3%)
  between operations  1.37 us (1%)
    ppermute x10, waiting for transfers between devices, partner(): return lax.ppermute(x, axis, [(i, i ^ bit) for i in range(size)])  36.6 us
    pallas_call x1, Pallas kernels, first_section(): pl.pallas_call(first_kernel, out_shape=jax.ShapeDtypeStruct((own, m), F32...  25.6 us
    pallas_call x1, Pallas kernels, scenario(): pl.pallas_call(scenario_kernel, out_shape=(jax.ShapeDtypeStruct((n, n), F...  22.5 us
    ppermute x10, starting transfers between devices, partner(): return lax.ppermute(x, axis, [(i, i ^ bit) for i in range(size)])  18.9 us
  transfers between devices with their start and end apart: 10, of which 10 were waited for; matrix products, arithmetic and copies ran while one was open for 0% of the time, Pallas kernels for 0%

profile of v1, /device:TPU:0, one launch (start us, length us, event | category | flops | bytes accessed | tf_op | source)
XLA Modules:
  0.0 108.8 jit_solution(253866027046060804)
XLA Ops:
  1.3 0.6 pad_add_fusion.spot
  1.8 22.5 %scenario.1 = (f32[512,512]{1,0:T(8,128)}, f32[2816,128]{1,0:T(8,128)}) custom-call(s32[2]{0:T(128)} %pad_add_fusion.spot, s32[1]{0:T(128)S(6)} %copy.12.region, f32[512,512]{1,0:T(8,128)} %bitcast.6, s32[1,512]{1,0:T(1,128)} %flags.1, f32[1,512]{1,0:T(1,128)} %low_d.1, f32[1,512]{1,0:T(1,128)} %low_s.1, f32[1,512]{1,0:T(1,128)} %up_d.1, f32[1,512]{1,0:T(1,128)} %up_s.1, ...), custom_call_target="tpu_custom_call" | custom-call | tf_op jit(solution)/shard_map/scenario/pallas_call | solution.py:223
  24.4 0.0 copy-start
  24.4 1.5 %slice_select_fusion = f32[1408,128]{1,0:T(8,128)S(1)} fusion(f32[2816,128]{1,0:T(8,128)} %get-tuple-element.5, pred[]{:T(512)S(6)} %ne.20), kind=kLoop, calls=%fused_computation.3 | loop fusion | flops 180224 | bytes 2162689 | tf_op jit(solution)/shard_map/jit(_where)/select_n | solution.py:267
  25.9 0.5 collective-permute-start
  26.4 1.8 %collective-permute-done = f32[1408,128]{1,0:T(8,128)S(1)} collective-permute-done((f32[1408,128]{1,0:T(8,128)S(1)}, f32[1408,128]{1,0:T(8,128)S(1)}, u32[]{:S(2)}, u32[]{:S(2)}) %collective-permute-start) | collective-permute-done | bytes 720928 | tf_op jit(solution)/shard_map/ppermute | solution.py:258
  28.2 0.0 copy-done
  28.2 0.1 select_add_fusion
  28.4 2.9 %collective-permute-start.1 = (f32[704,128]{1,0:T(8,128)S(1)}, f32[704,128]{1,0:T(8,128)S(1)}, u32[]{:S(2)}, u32[]{:S(2)}) collective-permute-start(f32[704,128]{1,0:T(8,128)S(1)} %slice_select_fusion.1), channel_id=1, source_target_pairs={{0,16},{8,24},{16,0},{24,8},{1,17},{9,25},{17,1},{25,9},{2,18},{10... | collective-permute-start | bytes 1081352 | tf_op jit(solution)/shard_map/ppermute | solution.py:258
  31.3 8.7 %collective-permute-done.1 = f32[704,128]{1,0:T(8,128)S(1)} collective-permute-done((f32[704,128]{1,0:T(8,128)S(1)}, f32[704,128]{1,0:T(8,128)S(1)}, u32[]{:S(2)}, u32[]{:S(2)}) %collective-permute-start.1) | collective-permute-done | bytes 360480 | tf_op jit(solution)/shard_map/ppermute | solution.py:258
  40.0 0.1 select_add_fusion.1
  40.1 1.9 %collective-permute-start.2 = (f32[352,128]{1,0:T(8,128)S(1)}, f32[352,128]{1,0:T(8,128)S(1)}, u32[]{:S(2)}, u32[]{:S(2)}) collective-permute-start(f32[352,128]{1,0:T(8,128)S(1)} %slice_select_fusion.2), channel_id=1, source_target_pairs={{0,1},{1,0},{2,3},{3,2},{4,5},{5,4},{6,7},{7,6},{8,9},{9,8},{10,11... | collective-permute-start | bytes 540680 | tf_op jit(solution)/shard_map/ppermute | solution.py:258
  42.0 4.2 %collective-permute-done.2 = f32[352,128]{1,0:T(8,128)S(1)} collective-permute-done((f32[352,128]{1,0:T(8,128)S(1)}, f32[352,128]{1,0:T(8,128)S(1)}, u32[]{:S(2)}, u32[]{:S(2)}) %collective-permute-start.2) | collective-permute-done | bytes 180256 | tf_op jit(solution)/shard_map/ppermute | solution.py:258
  46.2 1.6 %collective-permute-start.3 = (f32[176,128]{1,0:T(8,128)S(1)}, f32[176,128]{1,0:T(8,128)S(1)}, u32[]{:S(2)}, u32[]{:S(2)}) collective-permute-start(f32[176,128]{1,0:T(8,128)S(1)} %slice_select_fusion.3), channel_id=1, source_target_pairs={{0,2},{1,3},{2,0},{3,1},{4,6},{5,7},{6,4},{7,5},{8,10},{9,11},{10,... | collective-permute-start | bytes 270344 | tf_op jit(solution)/shard_map/ppermute | solution.py:258
  47.9 3.0 %collective-permute-done.3 = f32[176,128]{1,0:T(8,128)S(1)} collective-permute-done((f32[176,128]{1,0:T(8,128)S(1)}, f32[176,128]{1,0:T(8,128)S(1)}, u32[]{:S(2)}, u32[]{:S(2)}) %collective-permute-start.3) | collective-permute-done | bytes 90144 | tf_op jit(solution)/shard_map/ppermute | solution.py:258
  50.9 2.8 %collective-permute-start.4 = (f32[88,128]{1,0:T(8,128)S(1)}, f32[88,128]{1,0:T(8,128)S(1)}, u32[]{:S(2)}, u32[]{:S(2)}) collective-permute-start(f32[88,128]{1,0:T(8,128)S(1)} %slice_select_fusion.4), channel_id=1, source_target_pairs={{0,4},{1,5},{2,6},{3,7},{4,0},{5,1},{6,2},{7,3},{8,12},{9,13},{10,... | collective-permute-start | bytes 135176 | tf_op jit(solution)/shard_map/ppermute | solution.py:258
  53.7 2.2 %collective-permute-done.4 = f32[88,128]{1,0:T(8,128)S(1)} collective-permute-done((f32[88,128]{1,0:T(8,128)S(1)}, f32[88,128]{1,0:T(8,128)S(1)}, u32[]{:S(2)}, u32[]{:S(2)}) %collective-permute-start.4) | collective-permute-done | bytes 45088 | tf_op jit(solution)/shard_map/ppermute | solution.py:258
  55.9 3.3 %collective-permute-start.5 = (f32[88,128]{1,0:T(8,128)S(1)}, f32[88,128]{1,0:T(8,128)S(1)}, u32[]{:S(2)}, u32[]{:S(2)}) collective-permute-start(f32[88,128]{1,0:T(8,128)S(1)} %select_add_fusion.4), channel_id=1, source_target_pairs={{0,4},{1,5},{2,6},{3,7},{4,0},{5,1},{6,2},{7,3},{8,12},{9,13},{10,... | collective-permute-start | bytes 135176 | tf_op jit(solution)/shard_map/ppermute | solution.py:258
  59.2 2.0 %collective-permute-done.5 = f32[88,128]{1,0:T(8,128)S(1)} collective-permute-done((f32[88,128]{1,0:T(8,128)S(1)}, f32[88,128]{1,0:T(8,128)S(1)}, u32[]{:S(2)}, u32[]{:S(2)}) %collective-permute-start.5) | collective-permute-done | bytes 45088 | tf_op jit(solution)/shard_map/ppermute | solution.py:258
  61.2 2.7 %collective-permute-start.6 = (f32[176,128]{1,0:T(8,128)S(1)}, f32[176,128]{1,0:T(8,128)S(1)}, u32[]{:S(2)}, u32[]{:S(2)}) collective-permute-start(f32[176,128]{1,0:T(8,128)S(1)} %maximum_select_fusion.4), channel_id=1, source_target_pairs={{0,2},{1,3},{2,0},{3,1},{4,6},{5,7},{6,4},{7,5},{8,10},{9,11},{10,... | collective-permute-start | bytes 270344 | tf_op jit(solution)/shard_map/ppermute | solution.py:258
  63.9 2.5 %collective-permute-done.6 = f32[176,128]{1,0:T(8,128)S(1)} collective-permute-done((f32[176,128]{1,0:T(8,128)S(1)}, f32[176,128]{1,0:T(8,128)S(1)}, u32[]{:S(2)}, u32[]{:S(2)}) %collective-permute-start.6) | collective-permute-done | bytes 90144 | tf_op jit(solution)/shard_map/ppermute | solution.py:258
  66.4 1.6 %collective-permute-start.7 = (f32[352,128]{1,0:T(8,128)S(1)}, f32[352,128]{1,0:T(8,128)S(1)}, u32[]{:S(2)}, u32[]{:S(2)}) collective-permute-start(f32[352,128]{1,0:T(8,128)S(1)} %maximum_select_fusion.3), channel_id=1, source_target_pairs={{0,1},{1,0},{2,3},{3,2},{4,5},{5,4},{6,7},{7,6},{8,9},{9,8},{10,11... | collective-permute-start | bytes 540680 | tf_op jit(solution)/shard_map/ppermute | solution.py:258
  68.0 4.0 %collective-permute-done.7 = f32[352,128]{1,0:T(8,128)S(1)} collective-permute-done((f32[352,128]{1,0:T(8,128)S(1)}, f32[352,128]{1,0:T(8,128)S(1)}, u32[]{:S(2)}, u32[]{:S(2)}) %collective-permute-start.7) | collective-permute-done | bytes 180256 | tf_op jit(solution)/shard_map/ppermute | solution.py:258
  72.0 1.5 %collective-permute-start.8 = (f32[704,128]{1,0:T(8,128)S(1)}, f32[704,128]{1,0:T(8,128)S(1)}, u32[]{:S(2)}, u32[]{:S(2)}) collective-permute-start(f32[704,128]{1,0:T(8,128)S(1)} %maximum_select_fusion.2), channel_id=1, source_target_pairs={{0,16},{8,24},{16,0},{24,8},{1,17},{9,25},{17,1},{25,9},{2,18},{10... | collective-permute-start | bytes 1081352 | tf_op jit(solution)/shard_map/ppermute | solution.py:258
  73.6 5.9 %collective-permute-done.8 = f32[704,128]{1,0:T(8,128)S(1)} collective-permute-done((f32[704,128]{1,0:T(8,128)S(1)}, f32[704,128]{1,0:T(8,128)S(1)}, u32[]{:S(2)}, u32[]{:S(2)}) %collective-permute-start.8) | collective-permute-done | bytes 360480 | tf_op jit(solution)/shard_map/ppermute | solution.py:258
  79.6 0.1 collective-permute-start.9
  79.7 2.2 %collective-permute-done.9 = f32[1408,128]{1,0:T(8,128)S(1)} collective-permute-done((f32[1408,128]{1,0:T(8,128)S(1)}, f32[1408,128]{1,0:T(8,128)S(1)}, u32[]{:S(2)}, u32[]{:S(2)}) %collective-permute-start.9) | collective-permute-done | bytes 720928 | tf_op jit(solution)/shard_map/ppermute | solution.py:258
  81.8 1.3 %maximum_select_fusion.packed = f32[2816,128]{1,0:T(8,128)} fusion(f32[1408,128]{1,0:T(8,128)S(1)} %maximum_select_fusion.1, f32[1408,128]{1,0:T(8,128)S(1)} %collective-permute-done.9, pred[]{:T(512)S(6)} %ne.20), kind=kLoop, calls=%fused_computation | loop fusion | flops 1081344 | bytes 2883585 | tf_op jit(solution)/shard_map/jit(_where)/select_n | solution.py:271
  83.1 25.6 %first_section.1 = f32[96,768]{1,0:T(8,128)} custom-call(s32[2]{0:T(128)} %pad_add_fusion.spot, f32[2816,128]{1,0:T(8,128)} %maximum_select_fusion.packed), custom_call_target="tpu_custom_call" | custom-call | tf_op jit(solution)/shard_map/first_section/pallas_call | solution.py:241
  (11 shorter events, 0.2 us)
Async XLA Ops:
  24.4 3.9 %copy-start = (f32[2816,128]{1,0:T(8,128)S(1)}, f32[2816,128]{1,0:T(8,128)}, u32[]{:S(2)}) copy-start(f32[2816,128]{1,0:T(8,128)} %get-tuple-element.5) | copy-start | bytes 4325380
  25.9 2.4 %collective-permute-start = (f32[1408,128]{1,0:T(8,128)S(1)}, f32[1408,128]{1,0:T(8,128)S(1)}, u32[]{:S(2)}, u32[]{:S(2)}) collective-permute-start(f32[1408,128]{1,0:T(8,128)S(1)} %slice_select_fusion), channel_id=1, source_target_pairs={{0,8},{8,0},{16,24},{24,16},{1,9},{9,1},{17,25},{25,17},{2,10},{10... | collective-permute-start | bytes 2162696 | tf_op jit(solution)/shard_map/ppermute | solution.py:258
  28.4 11.6 %collective-permute-start.1 = (f32[704,128]{1,0:T(8,128)S(1)}, f32[704,128]{1,0:T(8,128)S(1)}, u32[]{:S(2)}, u32[]{:S(2)}) collective-permute-start(f32[704,128]{1,0:T(8,128)S(1)} %slice_select_fusion.1), channel_id=1, source_target_pairs={{0,16},{8,24},{16,0},{24,8},{1,17},{9,25},{17,1},{25,9},{2,18},{10... | collective-permute-start | bytes 1081352 | tf_op jit(solution)/shard_map/ppermute | solution.py:258
  40.1 6.1 %collective-permute-start.2 = (f32[352,128]{1,0:T(8,128)S(1)}, f32[352,128]{1,0:T(8,128)S(1)}, u32[]{:S(2)}, u32[]{:S(2)}) collective-permute-start(f32[352,128]{1,0:T(8,128)S(1)} %slice_select_fusion.2), channel_id=1, source_target_pairs={{0,1},{1,0},{2,3},{3,2},{4,5},{5,4},{6,7},{7,6},{8,9},{9,8},{10,11... | collective-permute-start | bytes 540680 | tf_op jit(solution)/shard_map/ppermute | solution.py:258
  46.2 4.6 %collective-permute-start.3 = (f32[176,128]{1,0:T(8,128)S(1)}, f32[176,128]{1,0:T(8,128)S(1)}, u32[]{:S(2)}, u32[]{:S(2)}) collective-permute-start(f32[176,128]{1,0:T(8,128)S(1)} %slice_select_fusion.3), channel_id=1, source_target_pairs={{0,2},{1,3},{2,0},{3,1},{4,6},{5,7},{6,4},{7,5},{8,10},{9,11},{10,... | collective-permute-start | bytes 270344 | tf_op jit(solution)/shard_map/ppermute | solution.py:258
  50.9 5.0 %collective-permute-start.4 = (f32[88,128]{1,0:T(8,128)S(1)}, f32[88,128]{1,0:T(8,128)S(1)}, u32[]{:S(2)}, u32[]{:S(2)}) collective-permute-start(f32[88,128]{1,0:T(8,128)S(1)} %slice_select_fusion.4), channel_id=1, source_target_pairs={{0,4},{1,5},{2,6},{3,7},{4,0},{5,1},{6,2},{7,3},{8,12},{9,13},{10,... | collective-permute-start | bytes 135176 | tf_op jit(solution)/shard_map/ppermute | solution.py:258
  55.9 5.3 %collective-permute-start.5 = (f32[88,128]{1,0:T(8,128)S(1)}, f32[88,128]{1,0:T(8,128)S(1)}, u32[]{:S(2)}, u32[]{:S(2)}) collective-permute-start(f32[88,128]{1,0:T(8,128)S(1)} %select_add_fusion.4), channel_id=1, source_target_pairs={{0,4},{1,5},{2,6},{3,7},{4,0},{5,1},{6,2},{7,3},{8,12},{9,13},{10,... | collective-permute-start | bytes 135176 | tf_op jit(solution)/shard_map/ppermute | solution.py:258
  61.2 5.2 %collective-permute-start.6 = (f32[176,128]{1,0:T(8,128)S(1)}, f32[176,128]{1,0:T(8,128)S(1)}, u32[]{:S(2)}, u32[]{:S(2)}) collective-permute-start(f32[176,128]{1,0:T(8,128)S(1)} %maximum_select_fusion.4), channel_id=1, source_target_pairs={{0,2},{1,3},{2,0},{3,1},{4,6},{5,7},{6,4},{7,5},{8,10},{9,11},{10,... | collective-permute-start | bytes 270344 | tf_op jit(solution)/shard_map/ppermute | solution.py:258
  66.4 5.6 %collective-permute-start.7 = (f32[352,128]{1,0:T(8,128)S(1)}, f32[352,128]{1,0:T(8,128)S(1)}, u32[]{:S(2)}, u32[]{:S(2)}) collective-permute-start(f32[352,128]{1,0:T(8,128)S(1)} %maximum_select_fusion.3), channel_id=1, source_target_pairs={{0,1},{1,0},{2,3},{3,2},{4,5},{5,4},{6,7},{7,6},{8,9},{9,8},{10,11... | collective-permute-start | bytes 540680 | tf_op jit(solution)/shard_map/ppermute | solution.py:258
  72.0 7.5 %collective-permute-start.8 = (f32[704,128]{1,0:T(8,128)S(1)}, f32[704,128]{1,0:T(8,128)S(1)}, u32[]{:S(2)}, u32[]{:S(2)}) collective-permute-start(f32[704,128]{1,0:T(8,128)S(1)} %maximum_select_fusion.2), channel_id=1, source_target_pairs={{0,16},{8,24},{16,0},{24,8},{1,17},{9,25},{17,1},{25,9},{2,18},{10... | collective-permute-start | bytes 1081352 | tf_op jit(solution)/shard_map/ppermute | solution.py:258
  79.6 2.3 %collective-permute-start.9 = (f32[1408,128]{1,0:T(8,128)S(1)}, f32[1408,128]{1,0:T(8,128)S(1)}, u32[]{:S(2)}, u32[]{:S(2)}) collective-permute-start(f32[1408,128]{1,0:T(8,128)S(1)} %maximum_select_fusion.1), channel_id=1, source_target_pairs={{0,8},{8,0},{16,24},{24,16},{1,9},{9,1},{17,25},{25,17},{2,10},{10... | collective-permute-start | bytes 2162696 | tf_op jit(solution)/shard_map/ppermute | solution.py:258

commit v2 on v1

--- a/solution.py
+++ b/solution.py
@@ -34,38 +34,58 @@
 
 
 def lane_splat(v, c):
-    return jnp.broadcast_to(v[:, c : c + 1], (8, T))
-
-
-def recip(p):
-    r = pl.reciprocal(p, approx=True)
-    return r * (2.0 - p * r)
+    return jnp.take_along_axis(v, jnp.full((8, T), c, jnp.int32), axis=1, mode="promise_in_bounds")
 
 
 def eliminate(rows, lane0):
     sub = lax.broadcasted_iota(jnp.int32, (8, T), 0)
     n = len(rows)
     v = [[r[:, i : i + T] for i in range(0, r.shape[1], T)] for r in rows]
-    b = [[lane_splat(v[h][0], lane0 + c) for c in range(8 * (h + 1))] for h in range(n)]
+    block = {}
+
+    def fetch(h, k):
+        block[h, k] = [lane_splat(v[h][0], lane0 + 8 * k + c) for c in range(8)]
+
+    for h in range(n):
+        fetch(h, 0)
+    fetch(1, 1)
     out = []
     for g in range(n):
+        for h in range(g + 1, n):
+            if (h, g) not in block:
+                fetch(h, g)
+        later = [key for key in block if key[1] > g]
+        own = block[g, g]
         pivots = jnp.zeros((8, T), F32)
-        for jj in range(8):
-            j = 8 * g + jj
-            pivot = row_splat(b[g][j], jj)
-            inv = recip(pivot)
-            pivots = jnp.where(sub == jj, pivot, pivots)
-            top = [row_splat(w, jj) for w in v[g]]
-            across = {c: row_splat(b[c // 8][j], c % 8) for c in range(j + 1, 8 * n)}
+        pivot = row_splat(own[0], 0)
+        for j in range(8):
+            pivots = jnp.where(sub == j, pivot, pivots)
+            inv = 1.0 / pivot
+            if j < 7:
+                side = row_splat(own[j], j + 1)
+                pivot = row_splat(own[j + 1], j + 1) - (side * side) * inv
+            top = [row_splat(w, j) for w in v[g]]
+            across = {c: row_splat(own[j], c) for c in range(j + 1, 8)}
+            far = {k: [row_splat(block[k, g][j], c) for c in range(8)] for k in sorted({key[1] for key in later})}
+            m = {}
             for h in range(g, n):
-                m = b[h][j] * inv
-                if h == g:
-                    m = jnp.where(sub > jj, m, 0.0)
-                for c in range(j + 1, 8 * (h + 1)):
-                    b[h][c] = b[h][c] - m * across[c]
-                v[h] = [w - m * t for w, t in zip(v[h], top)]
+                here = block[h, g]
+                m[h] = here[j] * inv
+                for c in range(j + 1, 8):
+                    here[c] = here[c] - m[h] * across[c]
+            for h, k in later:
+                there = block[h, k]
+                for c in range(8):
+                    there[c] = there[c] - m[h] * far[k][c]
+            for h in range(g, n):
+                part = jnp.where(sub > j, m[h], 0.0) if h == g else m[h]
+                v[h] = [w - part * t for w, t in zip(v[h], top)]
         scale = lax.rsqrt(pivots)
         out.append(jnp.concatenate([w * scale for w in v[g]], axis=1))
+        for h in range(g + 2, n):
+            for k in (g + 1, g + 2):
+                if k <= h and (h, k) not in block:
+                    fetch(h, k)
     return out
 
 
@@ -95,7 +115,7 @@
 
 
 def scenario_kernel(
-    spot, region, hess, flags, low_d, low_s, up_d, up_s, coup, pattern, first,
+    count, spot, region, hess, flags, low_d, low_s, up_d, up_s, coup, pattern, first,
     factor, gram, d_ref, lh, ll, xh, xl, whole,
 ):
     n, m = coup.shape
@@ -158,21 +178,28 @@
         at = pl.ds(pl.multiple_of(spot[1] * own, 8), own)
         whole[at, :] = whole[at, :] + first[...]
 
-    row = 0
-    for j in range(mt):
-        count = m - j * T
-        gram[row : row + count, :] = whole[j * T :, j * T : (j + 1) * T]
-        row += count
-    if row < gram.shape[0]:
-        gram[row:, :] = jnp.zeros((gram.shape[0] - row, T), F32)
-
-
-def first_kernel(spot, packed, out, d_ref, panel_ref, lh, ll, full):
+    chunk = gram.shape[0] // count
+    for l, at, rows, i, j in pieces(m, gram.shape[0], count):
+        to = pl.multiple_of((spot[2] ^ l) * chunk, 8) + at
+        if i is None:
+            gram[pl.ds(to, rows), :] = jnp.zeros((rows, T), F32)
+        else:
+            gram[pl.ds(to, rows), :] = whole[i : i + rows, j : j + T]
+
+
+def first_kernel(count, spot, *refs):
+    parts, (out, d_ref, panel_ref, lh, ll, full, packed) = refs[:-7], refs[-7:]
     m = full.shape[0]
     mt = m // T
     r, c = unit_block()
     eye = r == c
     start = [sum(m - i * T for i in range(j)) for j in range(mt)]
+    chunk = packed.shape[0] // count
+    each = count // len(parts)
+    for p in range(count):
+        to = pl.multiple_of((spot[2] ^ p) * chunk, 8)
+        at = (p % each) * chunk
+        packed[pl.ds(to, chunk), :] = parts[p // each][at : at + chunk, :]
 
     def step(t, _):
         for k in range(mt):
@@ -218,10 +245,19 @@
     return -(-rows // unit) * unit
 
 
-def scenario(spot, region, hess, flags, low_d, low_s, up_d, up_s, coup, pattern, first, rows):
+def pieces(m, total, count):
+    chunk = total // count
+    spans = [(i, j) for j in range(0, m, T) for i in range(j, m, T)]
+    cuts = sorted(set(range(0, total, chunk)) | set(range(0, len(spans) * T, T)) | {len(spans) * T, total})
+    for lo, hi in zip(cuts, cuts[1:]):
+        i, j = spans[lo // T] if lo < len(spans) * T else (None, None)
+        yield lo // chunk, lo % chunk, hi - lo, None if i is None else i + lo % T, j
+
+
+def scenario(spot, region, hess, flags, low_d, low_s, up_d, up_s, coup, pattern, first, rows, count):
     n, m = coup.shape
     return pl.pallas_call(
-        scenario_kernel,
+        functools.partial(scenario_kernel, count),
         out_shape=(jax.ShapeDtypeStruct((n, n), F32), jax.ShapeDtypeStruct((rows, T), F32)),
         in_specs=[SMEM, SMEM] + [VMEM] * 9,
         out_specs=(VMEM, VMEM),
@@ -237,11 +273,12 @@
     )(spot, region, hess, flags, low_d, low_s, up_d, up_s, coup, pattern, first)
 
 
-def first_section(spot, packed, own, m):
+def first_section(spot, parts, own, m, count):
+    rows = sum(part.shape[0] for part in parts)
     return pl.pallas_call(
-        first_kernel,
+        functools.partial(first_kernel, count),
         out_shape=jax.ShapeDtypeStruct((own, m), F32),
-        in_specs=[SMEM, VMEM],
+        in_specs=[SMEM] + [VMEM] * len(parts),
         out_specs=VMEM,
         scratch_shapes=[
             pltpu.VMEM((T, 2 * T), F32),
@@ -249,52 +286,73 @@
             pltpu.VMEM((m, m), BF),
             pltpu.VMEM((m, m), BF),
             pltpu.VMEM((m, m), F32),
+            pltpu.VMEM((rows, T), F32),
         ],
         name="first_section",
-    )(spot, packed)
-
-
-def partner(x, axis, size, bit):
-    return lax.ppermute(x, axis, [(i, i ^ bit) for i in range(size)])
-
-
-def sum_everywhere(x, sizes):
-    rounds = [(axis, size, bit) for axis, size in sizes for bit in (1 << k for k in range(size.bit_length() - 1))]
-    for axis, size, bit in rounds:
-        upper = (lax.axis_index(axis) & bit) != 0
-        half = x.shape[0] // 2
-        low, high = x[:half], x[half:]
-        x = jnp.where(upper, high, low) + partner(jnp.where(upper, low, high), axis, size, bit)
-    for axis, size, bit in reversed(rounds):
-        upper = (lax.axis_index(axis) & bit) != 0
-        other = partner(x, axis, size, bit)
-        x = jnp.where(upper, jnp.concatenate([other, x]), jnp.concatenate([x, other]))
-    return x
+    )(spot, *parts)
+
+
+AXES = ("scen", "wide")
+
+
+def swap(x, mask, count):
+    return lax.ppermute(x, AXES, [(i, i ^ mask) for i in range(count)])
+
+
+def rounds_of(sizes):
+    (_, scen), (_, wide) = sizes
+    bits = [wide << k for k in range(scen.bit_length() - 1)] + [1 << k for k in range(wide.bit_length() - 1)]
+    return [bits[:1]] + [bits[k : k + 2] for k in range(1, len(bits), 2)]
+
+
+def masks_of(bits):
+    return [sum(b for k, b in enumerate(bits) if d >> k & 1) for d in range(1 << len(bits))]
+
+
+def place_of(flat, rounds):
+    bits = [bit for group in reversed(rounds) for bit in group]
+    return sum(((flat // bit) % 2) << k for k, bit in enumerate(bits))
+
+
+def sum_everywhere(x, rounds, count):
+    for bits in rounds:
+        masks = masks_of(bits)
+        part = x.shape[0] // len(masks)
+        cut = [x[k * part : (k + 1) * part] for k in range(len(masks))]
+        got = [swap(c, mask, count) for c, mask in zip(cut[1:], masks[1:])]
+        x = functools.reduce(jnp.add, got, cut[0])
+    parts = [x]
+    for bits in reversed(rounds):
+        x = parts[0] if len(parts) == 1 else jnp.concatenate(parts)
+        parts = [x] + [swap(x, mask, count) for mask in masks_of(bits)[1:]]
+    return parts
 
 
 def solution(mesh):
-    sizes = [(axis, mesh.shape[axis]) for axis in ("scen", "wide")]
-    devices = sizes[0][1] * sizes[1][1]
+    sizes = [(axis, mesh.shape[axis]) for axis in AXES]
+    count = sizes[0][1] * sizes[1][1]
+    rounds = rounds_of(sizes)
 
     def per_device(hess_scen, flags, low_d, low_s, up_d, up_s, coupling, pattern, region, hess_first):
         own, m = hess_first.shape
-        rows = packed_rows(m, devices)
-        place = [lax.axis_index(axis).astype(jnp.int32) for axis in ("scen", "wide")]
+        rows = packed_rows(m, count)
+        scen, wide = [lax.axis_index(axis).astype(jnp.int32) for axis in AXES]
+        place = place_of(scen * sizes[1][1] + wide, rounds)
         factors, total = [], None
         for i in range(hess_scen.shape[0]):
-            lead = place[0] if i == 0 else jnp.int32(1)
+            lead = scen if i == 0 else jnp.int32(1)
             factor, gram = scenario(
-                jnp.stack([lead, place[1]]), region[i : i + 1], hess_scen[i],
+                jnp.stack([lead, wide, place]), region[i : i + 1], hess_scen[i],
                 flags[i : i + 1], low_d[i : i + 1], low_s[i : i + 1], up_d[i : i + 1], up_s[i : i + 1],
-                coupling[i], pattern[i : i + 1], hess_first, rows,
+                coupling[i], pattern[i : i + 1], hess_first, rows, count,
             )
             factors.append(factor)
             total = gram if total is None else total + gram
-        summed = sum_everywhere(total, sizes)
-        mine = first_section(jnp.stack(place), summed, own, m)
+        parts = sum_everywhere(total, rounds, count)
+        mine = first_section(jnp.stack([scen, wide, place]), parts, own, m, count)
         return (jnp.stack(factors), mine)
 
-    each = P(("scen", "wide"))
+    each = P(AXES)
     return jax.shard_map(
         per_device,
         mesh=mesh,

time: 109 us -> 85.8 us (0.79)
  Pallas kernels: 48.2 us -> 37.2 us
  waiting for transfers between devices: 36.6 us -> 26.6 us
  other arithmetic: 3.75 us -> 0.78 us
  local copies, waits for them, and re-layouts: 0.01 us -> 2.26 us
  starting transfers between devices: 18.9 us -> 17.3 us
    pallas_call x2, Pallas kernels: 48.2 us -> 37.2 us  [the longest x1 19.2 us: first_section(): pl.pallas_call(functools.partial(first_kernel, count), out_shape=jax.Shap...]
    ppermute x10 -> x14, waiting for transfers between devices: 36.6 us -> 26.6 us  [swap(): return lax.ppermute(x, AXES, [(i, i ^ mask) for i in range(count)])]
    select_n x10 -> x0, other arithmetic: 2.97 us -> none  [the longest x5 1.6 us: sum_everywhere(): jnp.where(upper, low, high)]
    ppermute x10 -> x14, starting transfers between devices: 18.9 us -> 17.3 us  [swap(): return lax.ppermute(x, AXES, [(i, i ^ mask) for i in range(count)])]
    slice x0 -> x3, local copies, waits for them, and re-layouts: none -> 1.32 us  [sum_everywhere(): cut = [x[k * part:(k + 1) * part] for k in range(len(masks))]]
  transfers between devices with their start and end apart: 10 -> 14, of which waited for: 10 -> 11; matrix products, arithmetic and copies ran while one was open for 0% -> 0% of each run, Pallas kernels for 0% -> 0%
where the time goes in v2:
time: 85.8 us; the launch traced here: 85.6 us
  Pallas kernels  37.2 us (43%)
  waiting for transfers between devices  26.6 us (31%)
  starting transfers between devices  17.3 us (20%)
  local copies, waits for them, and re-layouts  2.26 us (3%)
  between operations  1.49 us (2%)
    ppermute x14, waiting for transfers between devices, swap(): return lax.ppermute(x, AXES, [(i, i ^ mask) for i in range(count)])  26.6 us
    pallas_call x1, Pallas kernels, first_section(): pl.pallas_call(functools.partial(first_kernel, count), out_shape=jax.Shap...  19.2 us
    pallas_call x1, Pallas kernels, scenario(): pl.pallas_call(functools.partial(scenario_kernel, count), out_shape=(jax....  18 us
    ppermute x14, starting transfers between devices, swap(): return lax.ppermute(x, AXES, [(i, i ^ mask) for i in range(count)])  17.3 us
  transfers between devices with their start and end apart: 14, of which 11 were waited for; matrix products, arithmetic and copies ran while one was open for 0% of the time, Pallas kernels for 0%

profile of v2, /device:TPU:0, one launch (start us, length us, event | category | flops | bytes accessed | tf_op | source)
XLA Modules:
  0.0 85.6 jit_solution(8019271980294071876)
XLA Ops:
  1.4 0.6 pad_add_fusion.spot
  2.0 18.0 %scenario.1 = (f32[512,512]{1,0:T(8,128)}, f32[2816,128]{1,0:T(8,128)}) custom-call(s32[3]{0:T(128)} %pad_add_fusion.spot, s32[1]{0:T(128)S(6)} %copy.18.region, f32[512,512]{1,0:T(8,128)} %bitcast.7, s32[1,512]{1,0:T(1,128)} %flags.1, f32[1,512]{1,0:T(1,128)} %low_d.1, f32[1,512]{1,0:T(1,128)} %low_s.1, f32[1,512]{1,0:T(1,128)} %up_d.1, f32[1,512]{1,0:T(1,128)} %up_s.1, ...), custom_call_target="tpu_custom_call" | custom-call | tf_op jit(solution)/shard_map/scenario/pallas_call | solution.py:259
  20.0 0.0 copy-start
  20.0 1.3 %slice.31 = f32[1408,128]{1,0:T(8,128)S(1)} slice(f32[2816,128]{1,0:T(8,128)} %get-tuple-element.5), slice={[1408:2816], [0:128]} | slice | bytes 1441792 | tf_op jit(solution)/shard_map/slice | solution.py:321
  21.3 0.5 collective-permute-start
  21.8 1.8 %collective-permute-done = f32[1408,128]{1,0:T(8,128)S(1)} collective-permute-done((f32[1408,128]{1,0:T(8,128)S(1)}, f32[1408,128]{1,0:T(8,128)S(1)}, u32[]{:S(2)}, u32[]{:S(2)}) %collective-permute-start) | collective-permute-done | bytes 720928 | tf_op jit(solution)/shard_map/ppermute | solution.py:299
  23.6 0.0 copy-done
  23.6 0.1 slice_add_fusion
  23.8 2.9 %collective-permute-start.1 = (f32[352,128]{1,0:T(8,128)S(1)}, f32[352,128]{1,0:T(8,128)S(1)}, u32[]{:S(2)}, u32[]{:S(2)}) collective-permute-start(f32[352,128]{1,0:T(8,128)S(1)} %get-tuple-element.8), channel_id=1, source_target_pairs={{0,16},{1,17},{2,18},{3,19},{4,20},{5,21},{6,22},{7,23},{8,24},{9,... | collective-permute-start | bytes 540680 | tf_op jit(solution)/shard_map/ppermute | solution.py:299
  26.7 1.5 %collective-permute-start.3 = (f32[352,128]{1,0:T(8,128)S(1)}, f32[352,128]{1,0:T(8,128)S(1)}, u32[]{:S(2)}, u32[]{:S(2)}) collective-permute-start(f32[352,128]{1,0:T(8,128)S(1)} %get-tuple-element.9), channel_id=1, source_target_pairs={{0,17},{1,16},{2,19},{3,18},{4,21},{5,20},{6,23},{7,22},{8,25},{9,... | collective-permute-start | bytes 540680 | tf_op jit(solution)/shard_map/ppermute | solution.py:299
  28.2 0.0 collective-permute-start.2
  28.2 3.9 %collective-permute-done.1 = f32[352,128]{1,0:T(8,128)S(1)} collective-permute-done((f32[352,128]{1,0:T(8,128)S(1)}, f32[352,128]{1,0:T(8,128)S(1)}, u32[]{:S(2)}, u32[]{:S(2)}) %collective-permute-start.1) | collective-permute-done | bytes 180256 | tf_op jit(solution)/shard_map/ppermute | solution.py:299
  32.1 4.6 %collective-permute-done.3 = f32[352,128]{1,0:T(8,128)S(1)} collective-permute-done((f32[352,128]{1,0:T(8,128)S(1)}, f32[352,128]{1,0:T(8,128)S(1)}, u32[]{:S(2)}, u32[]{:S(2)}) %collective-permute-start.3) | collective-permute-done | bytes 180256 | tf_op jit(solution)/shard_map/ppermute | solution.py:299
  36.7 1.4 %collective-permute-done.2 = f32[352,128]{1,0:T(8,128)S(1)} collective-permute-done((f32[352,128]{1,0:T(8,128)S(1)}, f32[352,128]{1,0:T(8,128)S(1)}, u32[]{:S(2)}, u32[]{:S(2)}) %collective-permute-start.2) | collective-permute-done | bytes 180256 | tf_op jit(solution)/shard_map/ppermute | solution.py:299
  38.1 0.1 fusion.1
  38.2 1.6 %collective-permute-start.4 = (f32[88,128]{1,0:T(8,128)S(1)}, f32[88,128]{1,0:T(8,128)S(1)}, u32[]{:S(2)}, u32[]{:S(2)}) collective-permute-start(f32[88,128]{1,0:T(8,128)S(1)} %get-tuple-element.11), channel_id=1, source_target_pairs={{0,2},{1,3},{2,0},{3,1},{4,6},{5,7},{6,4},{7,5},{8,10},{9,11},{10,... | collective-permute-start | bytes 135176 | tf_op jit(solution)/shard_map/ppermute | solution.py:299
  39.8 2.5 %collective-permute-start.6 = (f32[88,128]{1,0:T(8,128)S(1)}, f32[88,128]{1,0:T(8,128)S(1)}, u32[]{:S(2)}, u32[]{:S(2)}) collective-permute-start(f32[88,128]{1,0:T(8,128)S(1)} %get-tuple-element.12), channel_id=1, source_target_pairs={{0,6},{1,7},{2,4},{3,5},{4,2},{5,3},{6,0},{7,1},{8,14},{9,15},{10,... | collective-permute-start | bytes 135176 | tf_op jit(solution)/shard_map/ppermute | solution.py:299
  42.3 0.1 collective-permute-start.5
  42.4 0.3 collective-permute-done.4
  42.7 2.9 %collective-permute-done.6 = f32[88,128]{1,0:T(8,128)S(1)} collective-permute-done((f32[88,128]{1,0:T(8,128)S(1)}, f32[88,128]{1,0:T(8,128)S(1)}, u32[]{:S(2)}, u32[]{:S(2)}) %collective-permute-start.6) | collective-permute-done | bytes 45088 | tf_op jit(solution)/shard_map/ppermute | solution.py:299
  45.6 2.1 %collective-permute-done.5 = f32[88,128]{1,0:T(8,128)S(1)} collective-permute-done((f32[88,128]{1,0:T(8,128)S(1)}, f32[88,128]{1,0:T(8,128)S(1)}, u32[]{:S(2)}, u32[]{:S(2)}) %collective-permute-start.5) | collective-permute-done | bytes 45088 | tf_op jit(solution)/shard_map/ppermute | solution.py:299
  47.7 1.9 %collective-permute-start.9 = (f32[88,128]{1,0:T(8,128)S(1)}, f32[88,128]{1,0:T(8,128)S(1)}, u32[]{:S(2)}, u32[]{:S(2)}) collective-permute-start(f32[88,128]{1,0:T(8,128)S(1)} %get-tuple-element.7), channel_id=1, source_target_pairs={{0,6},{1,7},{2,4},{3,5},{4,2},{5,3},{6,0},{7,1},{8,14},{9,15},{10,... | collective-permute-start | bytes 135176 | tf_op jit(solution)/shard_map/ppermute | solution.py:299
  49.6 0.0 collective-permute-start.8
  49.6 2.5 %collective-permute-start.7 = (f32[88,128]{1,0:T(8,128)S(1)}, f32[88,128]{1,0:T(8,128)S(1)}, u32[]{:S(2)}, u32[]{:S(2)}) collective-permute-start(f32[88,128]{1,0:T(8,128)S(1)} %get-tuple-element.7), channel_id=1, source_target_pairs={{0,2},{1,3},{2,0},{3,1},{4,6},{5,7},{6,4},{7,5},{8,10},{9,11},{10,... | collective-permute-start | bytes 135176 | tf_op jit(solution)/shard_map/ppermute | solution.py:299
  52.2 1.5 %collective-permute-done.9 = f32[88,128]{1,0:T(8,128)S(1)} collective-permute-done((f32[88,128]{1,0:T(8,128)S(1)}, f32[88,128]{1,0:T(8,128)S(1)}, u32[]{:S(2)}, u32[]{:S(2)}) %collective-permute-start.9) | collective-permute-done | bytes 45088 | tf_op jit(solution)/shard_map/ppermute | solution.py:299
  53.6 1.0 %collective-permute-done.8 = f32[88,128]{1,0:T(8,128)S(1)} collective-permute-done((f32[88,128]{1,0:T(8,128)S(1)}, f32[88,128]{1,0:T(8,128)S(1)}, u32[]{:S(2)}, u32[]{:S(2)}) %collective-permute-start.8) | collective-permute-done | bytes 45088 | tf_op jit(solution)/shard_map/ppermute | solution.py:299
  54.7 0.0 collective-permute-done.7
  54.7 1.5 %collective-permute-start.12 = (f32[352,128]{1,0:T(8,128)S(1)}, f32[352,128]{1,0:T(8,128)S(1)}, u32[]{:S(2)}, u32[]{:S(2)}) collective-permute-start(f32[352,128]{1,0:T(8,128)S(1)} %pad_maximum_fusion), channel_id=1, source_target_pairs={{0,17},{1,16},{2,19},{3,18},{4,21},{5,20},{6,23},{7,22},{8,25},{9,... | collective-permute-start | bytes 540680 | tf_op jit(solution)/shard_map/ppermute | solution.py:299
  56.2 1.5 %collective-permute-start.11 = (f32[352,128]{1,0:T(8,128)S(1)}, f32[352,128]{1,0:T(8,128)S(1)}, u32[]{:S(2)}, u32[]{:S(2)}) collective-permute-start(f32[352,128]{1,0:T(8,128)S(1)} %pad_maximum_fusion), channel_id=1, source_target_pairs={{0,1},{1,0},{2,3},{3,2},{4,5},{5,4},{6,7},{7,6},{8,9},{9,8},{10,11... | collective-permute-start | bytes 540680 | tf_op jit(solution)/shard_map/ppermute | solution.py:299
  57.7 0.6 collective-permute-start.10
  58.3 4.9 %collective-permute-done.10 = f32[352,128]{1,0:T(8,128)S(1)} collective-permute-done((f32[352,128]{1,0:T(8,128)S(1)}, f32[352,128]{1,0:T(8,128)S(1)}, u32[]{:S(2)}, u32[]{:S(2)}) %collective-permute-start.10) | collective-permute-done | bytes 180256 | tf_op jit(solution)/shard_map/ppermute | solution.py:299
  63.2 0.0 collective-permute-done.11
  63.2 0.0 collective-permute-done.12
  63.3 0.0 copy-start.1
  63.3 0.1 collective-permute-start.13
  63.4 2.2 %collective-permute-done.13.refs_1_ = f32[1408,128]{1,0:T(8,128)S(1)} collective-permute-done((f32[1408,128]{1,0:T(8,128)S(1)}, f32[1408,128]{1,0:T(8,128)S(1)}, u32[]{:S(2)}, u32[]{:S(2)}) %collective-permute-start.13) | collective-permute-done | bytes 720928 | tf_op jit(solution)/shard_map/ppermute | solution.py:299
  65.5 0.0 copy-done.1
  65.5 0.0 copy-start.2
  65.6 0.9 %copy-done.2 = f32[1408,128]{1,0:T(8,128)} copy-done((f32[1408,128]{1,0:T(8,128)}, f32[1408,128]{1,0:T(8,128)S(1)}, u32[]{:S(2)}) %copy-start.2) | copy-done | bytes 720920
  66.4 19.2 %first_section.1 = f32[96,768]{1,0:T(8,128)} custom-call(s32[3]{0:T(128)} %pad_add_fusion.spot, f32[1408,128]{1,0:T(8,128)} %copy-done.1, f32[1408,128]{1,0:T(8,128)} %copy-done.2), custom_call_target="tpu_custom_call" | custom-call | tf_op jit(solution)/shard_map/first_section/pallas_call | solution.py:278
  (10 shorter events, 0.1 us)
Async XLA Ops:
  20.0 3.6 %copy-start = (f32[2816,128]{1,0:T(8,128)S(1)}, f32[2816,128]{1,0:T(8,128)}, u32[]{:S(2)}) copy-start(f32[2816,128]{1,0:T(8,128)} %get-tuple-element.5) | copy-start | bytes 4325380
  21.3 2.4 %collective-permute-start = (f32[1408,128]{1,0:T(8,128)S(1)}, f32[1408,128]{1,0:T(8,128)S(1)}, u32[]{:S(2)}, u32[]{:S(2)}) collective-permute-start(f32[1408,128]{1,0:T(8,128)S(1)} %slice.31), channel_id=1, source_target_pairs={{0,8},{1,9},{2,10},{3,11},{4,12},{5,13},{6,14},{7,15},{8,0},{9,1},... | collective-permute-start | bytes 2162696 | tf_op jit(solution)/shard_map/ppermute | solution.py:299
  23.8 8.3 %collective-permute-start.1 = (f32[352,128]{1,0:T(8,128)S(1)}, f32[352,128]{1,0:T(8,128)S(1)}, u32[]{:S(2)}, u32[]{:S(2)}) collective-permute-start(f32[352,128]{1,0:T(8,128)S(1)} %get-tuple-element.8), channel_id=1, source_target_pairs={{0,16},{1,17},{2,18},{3,19},{4,20},{5,21},{6,22},{7,23},{8,24},{9,... | collective-permute-start | bytes 540680 | tf_op jit(solution)/shard_map/ppermute | solution.py:299
  26.7 10.0 %collective-permute-start.3 = (f32[352,128]{1,0:T(8,128)S(1)}, f32[352,128]{1,0:T(8,128)S(1)}, u32[]{:S(2)}, u32[]{:S(2)}) collective-permute-start(f32[352,128]{1,0:T(8,128)S(1)} %get-tuple-element.9), channel_id=1, source_target_pairs={{0,17},{1,16},{2,19},{3,18},{4,21},{5,20},{6,23},{7,22},{8,25},{9,... | collective-permute-start | bytes 540680 | tf_op jit(solution)/shard_map/ppermute | solution.py:299
  28.2 9.9 %collective-permute-start.2 = (f32[352,128]{1,0:T(8,128)S(1)}, f32[352,128]{1,0:T(8,128)S(1)}, u32[]{:S(2)}, u32[]{:S(2)}) collective-permute-start(f32[352,128]{1,0:T(8,128)S(1)} %get-tuple-element.10), channel_id=1, source_target_pairs={{0,1},{1,0},{2,3},{3,2},{4,5},{5,4},{6,7},{7,6},{8,9},{9,8},{10,11... | collective-permute-start | bytes 540680 | tf_op jit(solution)/shard_map/ppermute | solution.py:299
  38.2 4.6 %collective-permute-start.4 = (f32[88,128]{1,0:T(8,128)S(1)}, f32[88,128]{1,0:T(8,128)S(1)}, u32[]{:S(2)}, u32[]{:S(2)}) collective-permute-start(f32[88,128]{1,0:T(8,128)S(1)} %get-tuple-element.11), channel_id=1, source_target_pairs={{0,2},{1,3},{2,0},{3,1},{4,6},{5,7},{6,4},{7,5},{8,10},{9,11},{10,... | collective-permute-start | bytes 135176 | tf_op jit(solution)/shard_map/ppermute | solution.py:299
  39.8 5.8 %collective-permute-start.6 = (f32[88,128]{1,0:T(8,128)S(1)}, f32[88,128]{1,0:T(8,128)S(1)}, u32[]{:S(2)}, u32[]{:S(2)}) collective-permute-start(f32[88,128]{1,0:T(8,128)S(1)} %get-tuple-element.12), channel_id=1, source_target_pairs={{0,6},{1,7},{2,4},{3,5},{4,2},{5,3},{6,0},{7,1},{8,14},{9,15},{10,... | collective-permute-start | bytes 135176 | tf_op jit(solution)/shard_map/ppermute | solution.py:299
  42.3 5.4 %collective-permute-start.5 = (f32[88,128]{1,0:T(8,128)S(1)}, f32[88,128]{1,0:T(8,128)S(1)}, u32[]{:S(2)}, u32[]{:S(2)}) collective-permute-start(f32[88,128]{1,0:T(8,128)S(1)} %get-tuple-element.13), channel_id=1, source_target_pairs={{0,4},{1,5},{2,6},{3,7},{4,0},{5,1},{6,2},{7,3},{8,12},{9,13},{10,... | collective-permute-start | bytes 135176 | tf_op jit(solution)/shard_map/ppermute | solution.py:299
  47.7 5.9 %collective-permute-start.9 = (f32[88,128]{1,0:T(8,128)S(1)}, f32[88,128]{1,0:T(8,128)S(1)}, u32[]{:S(2)}, u32[]{:S(2)}) collective-permute-start(f32[88,128]{1,0:T(8,128)S(1)} %get-tuple-element.7), channel_id=1, source_target_pairs={{0,6},{1,7},{2,4},{3,5},{4,2},{5,3},{6,0},{7,1},{8,14},{9,15},{10,... | collective-permute-start | bytes 135176 | tf_op jit(solution)/shard_map/ppermute | solution.py:299
  49.6 5.0 %collective-permute-start.8 = (f32[88,128]{1,0:T(8,128)S(1)}, f32[88,128]{1,0:T(8,128)S(1)}, u32[]{:S(2)}, u32[]{:S(2)}) collective-permute-start(f32[88,128]{1,0:T(8,128)S(1)} %get-tuple-element.7), channel_id=1, source_target_pairs={{0,4},{1,5},{2,6},{3,7},{4,0},{5,1},{6,2},{7,3},{8,12},{9,13},{10,... | collective-permute-start | bytes 135176 | tf_op jit(solution)/shard_map/ppermute | solution.py:299
  49.6 5.0 %collective-permute-start.7 = (f32[88,128]{1,0:T(8,128)S(1)}, f32[88,128]{1,0:T(8,128)S(1)}, u32[]{:S(2)}, u32[]{:S(2)}) collective-permute-start(f32[88,128]{1,0:T(8,128)S(1)} %get-tuple-element.7), channel_id=1, source_target_pairs={{0,2},{1,3},{2,0},{3,1},{4,6},{5,7},{6,4},{7,5},{8,10},{9,11},{10,... | collective-permute-start | bytes 135176 | tf_op jit(solution)/shard_map/ppermute | solution.py:299
  54.7 8.5 %collective-permute-start.12 = (f32[352,128]{1,0:T(8,128)S(1)}, f32[352,128]{1,0:T(8,128)S(1)}, u32[]{:S(2)}, u32[]{:S(2)}) collective-permute-start(f32[352,128]{1,0:T(8,128)S(1)} %pad_maximum_fusion), channel_id=1, source_target_pairs={{0,17},{1,16},{2,19},{3,18},{4,21},{5,20},{6,23},{7,22},{8,25},{9,... | collective-permute-start | bytes 540680 | tf_op jit(solution)/shard_map/ppermute | solution.py:299
  56.2 7.0 %collective-permute-start.11 = (f32[352,128]{1,0:T(8,128)S(1)}, f32[352,128]{1,0:T(8,128)S(1)}, u32[]{:S(2)}, u32[]{:S(2)}) collective-permute-start(f32[352,128]{1,0:T(8,128)S(1)} %pad_maximum_fusion), channel_id=1, source_target_pairs={{0,1},{1,0},{2,3},{3,2},{4,5},{5,4},{6,7},{7,6},{8,9},{9,8},{10,11... | collective-permute-start | bytes 540680 | tf_op jit(solution)/shard_map/ppermute | solution.py:299
  57.7 5.5 %collective-permute-start.10 = (f32[352,128]{1,0:T(8,128)S(1)}, f32[352,128]{1,0:T(8,128)S(1)}, u32[]{:S(2)}, u32[]{:S(2)}) collective-permute-start(f32[352,128]{1,0:T(8,128)S(1)} %pad_maximum_fusion), channel_id=1, source_target_pairs={{0,16},{1,17},{2,18},{3,19},{4,20},{5,21},{6,22},{7,23},{8,24},{9,... | collective-permute-start | bytes 540680 | tf_op jit(solution)/shard_map/ppermute | solution.py:299
  63.3 2.3 %copy-start.1 = (f32[1408,128]{1,0:T(8,128)}, f32[1408,128]{1,0:T(8,128)S(1)}, u32[]{:S(2)}) copy-start(f32[1408,128]{1,0:T(8,128)S(1)} %constant_dynamic-update-slice_fusion.refs_0_) | copy-start | bytes 2162692
  63.3 2.3 %collective-permute-start.13 = (f32[1408,128]{1,0:T(8,128)S(1)}, f32[1408,128]{1,0:T(8,128)S(1)}, u32[]{:S(2)}, u32[]{:S(2)}) collective-permute-start(f32[1408,128]{1,0:T(8,128)S(1)} %constant_dynamic-update-slice_fusion.refs_0_), channel_id=1, source_target_pairs={{0,8},{1,9},{2,10},{3,11},{4,12},{5,13},{6,14},{7,15},{8,0},{9,1},... | collective-permute-start | bytes 2162696 | tf_op jit(solution)/shard_map/ppermute | solution.py:299
  65.5 0.9 %copy-start.2 = (f32[1408,128]{1,0:T(8,128)}, f32[1408,128]{1,0:T(8,128)S(1)}, u32[]{:S(2)}) copy-start(f32[1408,128]{1,0:T(8,128)S(1)} %collective-permute-done.13.refs_1_) | copy-start | bytes 2162692

commit v3 on v2

--- a/solution.py
+++ b/solution.py
@@ -115,11 +115,24 @@
 
 
 def scenario_kernel(
-    count, spot, region, hess, flags, low_d, low_s, up_d, up_s, coup, pattern, first,
-    factor, gram, d_ref, lh, ll, xh, xl, whole,
+    place_fn, count, region, hess_hbm, flags, low_d, low_s, up_d, up_s, coup_hbm, pattern, first,
+    factor_hbm, keep, send, hess, coup, factor, d_ref, ih, il, lh, ll, xh, xl, whole, in_sem, out_sem,
 ):
     n, m = coup.shape
     nt, mt = n // T, m // T
+    loads = []
+    for k in range(nt):
+        cut = (pl.ds(k * T, n - k * T), pl.ds(k * T, T))
+        loads.append(pltpu.make_async_copy(hess_hbm.at[cut], hess.at[cut], in_sem.at[k]))
+        cut = pl.ds(k * T, T)
+        loads.append(pltpu.make_async_copy(coup_hbm.at[cut], coup.at[cut], in_sem.at[nt + k]))
+    for load in loads:
+        load.start()
+    stores = []
+    for k in range(nt):
+        cut = (slice(None), pl.ds(k * T, T))
+        stores.append(pltpu.make_async_copy(factor.at[cut], factor_hbm.at[cut], out_sem.at[k]))
+    lead, wide, place = place_fn()
     r, c = unit_block()
     eye = r == c
     barrier = low_d[...] / low_s[...] + flags[...].astype(F32) * up_d[...] / up_s[...]
@@ -131,6 +144,13 @@
     column = lax.broadcasted_iota(jnp.int32, (nb, m), 1)
     spread = jnp.where((column >= block_row * width) & (column < (block_row + 1) * width), 1.0, 0.0)
     mask = jnp.dot(jnp.broadcast_to(coupled, (8, nb)), spread, preferred_element_type=F32)[0:1, :]
+    for ref in (lh, ll, xh, xl, ih, il):
+        ref[...] = jnp.zeros(ref.shape, BF)
+
+    def solve(t):
+        rows = pl.ds(pl.multiple_of(t * T, T), T)
+        rhs = coup[rows, :] * mask - dot3((lh[rows, :], ll[rows, :]), (xh[...], xl[...]), NN)
+        return rows, dot3((ih[...], il[...]), split(rhs), NN)
 
     def step(t, _):
         for k in range(nt):
@@ -138,56 +158,66 @@
             @pl.when(t == k)
             def _():
                 lo, hi = k * T, (k + 1) * T
+                loads[2 * k].wait()
+                loads[2 * k + 1].wait()
                 panel = hess[lo:, lo:hi]
                 if k:
                     panel = panel - dot3((lh[lo:, :lo], ll[lo:, :lo]), (lh[lo:hi, :lo], ll[lo:hi, :lo]), NT)
+                    factor[:lo, lo:hi] = jnp.zeros((lo, T), F32)
                 d_ref[:, :T] = panel[:T] + jnp.where(eye, barrier[:, lo:hi], 0.0)
                 d_ref[:, T:] = jnp.where(eye, 1.0, 0.0)
                 if k + 1 < nt:
                     factor[hi:, lo:hi] = panel[T:]
-                    factor[lo:hi, hi:] = jnp.zeros((T, n - hi), F32)
-
+
+        rows, solved = solve(jnp.maximum(t - 1, 0))
+        xh[rows, :], xl[rows, :] = split(jnp.where(t > 0, solved, 0.0))
         factor_block(d_ref)
+        ih[...], il[...] = split(d_ref[:, T:])
         for k in range(nt):
 
             @pl.when(t == k)
             def _():
                 lo, hi = k * T, (k + 1) * T
                 factor[lo:hi, lo:hi] = lower_of(d_ref)
-                inv = split(d_ref[:, T:])
                 if k + 1 < nt:
-                    below = dot3(split(factor[hi:, lo:hi]), inv, NT)
+                    below = dot3(split(factor[hi:, lo:hi]), (ih[...], il[...]), NT)
                     factor[hi:, lo:hi] = below
                     lh[hi:, lo:hi], ll[hi:, lo:hi] = split(below)
-                rhs = coup[lo:hi, :] * mask
-                if k:
-                    rhs = rhs - dot3((lh[lo:hi, :lo], ll[lo:hi, :lo]), (xh[:lo], xl[:lo]), NN)
-                xh[lo:hi], xl[lo:hi] = split(dot3(inv, split(rhs), NN))
+                stores[k].start()
 
         return 0
 
     lax.fori_loop(0, nt, step, 0)
+    rows, solved = solve(nt - 1)
+    xh[rows, :], xl[rows, :] = split(solved)
     for j in range(0, m, 2 * T):
         a = (xh[:, j:], xl[:, j:])
         b = (xh[:, j : j + 2 * T], xl[:, j : j + 2 * T])
         whole[j:, j : j + 2 * T] = dot3(a, b, TN)
 
-    @pl.when(spot[0] == 0)
+    @pl.when(lead == 0)
     def _():
         own = first.shape[0]
-        at = pl.ds(pl.multiple_of(spot[1] * own, 8), own)
+        at = pl.ds(pl.multiple_of(wide * own, 8), own)
         whole[at, :] = whole[at, :] + first[...]
 
-    chunk = gram.shape[0] // count
-    for l, at, rows, i, j in pieces(m, gram.shape[0], count):
-        to = pl.multiple_of((spot[2] ^ l) * chunk, 8) + at
-        if i is None:
-            gram[pl.ds(to, rows), :] = jnp.zeros((rows, T), F32)
-        else:
-            gram[pl.ds(to, rows), :] = whole[i : i + rows, j : j + T]
-
-
-def first_kernel(count, spot, *refs):
+    half = count // 2
+    chunk = keep.shape[0] // half
+    for side in range(2):
+
+        @pl.when(place // half == side)
+        def _():
+            for l, at, rows, i, j in pieces(m, count * chunk, count):
+                to = pl.multiple_of(((l ^ place) % half) * chunk, 8) + at
+                target = (keep, send)[(l // half) ^ side]
+                target[pl.ds(to, rows), :] = jnp.zeros((rows, T), F32) if i is None else whole[i : i + rows, j : j + T]
+
+    for store in stores:
+        store.wait()
+
+
+def first_kernel(place_fn, count, *refs):
+    _, wide, place = place_fn()
     parts, (out, d_ref, panel_ref, lh, ll, full, packed) = refs[:-7], refs[-7:]
     m = full.shape[0]
     mt = m // T
@@ -197,7 +227,7 @@
     chunk = packed.shape[0] // count
     each = count // len(parts)
     for p in range(count):
-        to = pl.multiple_of((spot[2] ^ p) * chunk, 8)
+        to = pl.multiple_of((place ^ p) * chunk, 8)
         at = (p % each) * chunk
         packed[pl.ds(to, chunk), :] = parts[p // each][at : at + chunk, :]
 
@@ -232,11 +262,13 @@
 
     lax.fori_loop(0, mt, step, 0)
     own = out.shape[0]
-    out[...] = full[pl.ds(pl.multiple_of(spot[1] * own, 8), own), :]
+    out[...] = full[pl.ds(pl.multiple_of(wide * own, 8), own), :]
 
 
 VMEM = pl.BlockSpec(memory_space=pltpu.VMEM)
 SMEM = pl.BlockSpec(memory_space=pltpu.SMEM)
+HBM = pl.BlockSpec(memory_space=pltpu.HBM)
+GRANT = 24 << 20
 
 
 def packed_rows(m, devices):
@@ -254,31 +286,40 @@
         yield lo // chunk, lo % chunk, hi - lo, None if i is None else i + lo % T, j
 
 
-def scenario(spot, region, hess, flags, low_d, low_s, up_d, up_s, coup, pattern, first, rows, count):
+def scenario(place_fn, region, hess, flags, low_d, low_s, up_d, up_s, coup, pattern, first, rows, count):
     n, m = coup.shape
+    half = jax.ShapeDtypeStruct((rows // 2, T), F32)
     return pl.pallas_call(
-        functools.partial(scenario_kernel, count),
-        out_shape=(jax.ShapeDtypeStruct((n, n), F32), jax.ShapeDtypeStruct((rows, T), F32)),
-        in_specs=[SMEM, SMEM] + [VMEM] * 9,
-        out_specs=(VMEM, VMEM),
+        functools.partial(scenario_kernel, place_fn, count),
+        out_shape=(jax.ShapeDtypeStruct((n, n), F32), half, half),
+        in_specs=[SMEM, HBM] + [VMEM] * 5 + [HBM, VMEM, VMEM],
+        out_specs=(HBM, VMEM, VMEM),
         scratch_shapes=[
+            pltpu.VMEM((n, n), F32),
+            pltpu.VMEM((n, m), F32),
+            pltpu.VMEM((n, n), F32),
             pltpu.VMEM((T, 2 * T), F32),
+            pltpu.VMEM((T, T), BF),
+            pltpu.VMEM((T, T), BF),
             pltpu.VMEM((n, n), BF),
             pltpu.VMEM((n, n), BF),
             pltpu.VMEM((n, m), BF),
             pltpu.VMEM((n, m), BF),
             pltpu.VMEM((m, m), F32),
+            pltpu.SemaphoreType.DMA((2 * n // T,)),
+            pltpu.SemaphoreType.DMA((n // T,)),
         ],
+        compiler_params=pltpu.CompilerParams(vmem_limit_bytes=GRANT),
         name="scenario",
-    )(spot, region, hess, flags, low_d, low_s, up_d, up_s, coup, pattern, first)
-
-
-def first_section(spot, parts, own, m, count):
+    )(region, hess, flags, low_d, low_s, up_d, up_s, coup, pattern, first)
+
+
+def first_section(place_fn, parts, own, m, count):
     rows = sum(part.shape[0] for part in parts)
     return pl.pallas_call(
-        functools.partial(first_kernel, count),
+        functools.partial(first_kernel, place_fn, count),
         out_shape=jax.ShapeDtypeStruct((own, m), F32),
-        in_specs=[SMEM] + [VMEM] * len(parts),
+        in_specs=[VMEM] * len(parts),
         out_specs=VMEM,
         scratch_shapes=[
             pltpu.VMEM((T, 2 * T), F32),
@@ -288,8 +329,9 @@
             pltpu.VMEM((m, m), F32),
             pltpu.VMEM((rows, T), F32),
         ],
+        compiler_params=pltpu.CompilerParams(vmem_limit_bytes=GRANT),
         name="first_section",
-    )(spot, *parts)
+    )(*parts)
 
 
 AXES = ("scen", "wide")
@@ -314,8 +356,9 @@
     return sum(((flat // bit) % 2) << k for k, bit in enumerate(bits))
 
 
-def sum_everywhere(x, rounds, count):
-    for bits in rounds:
+def sum_everywhere(x, sent, rounds, count):
+    x = x + swap(sent, masks_of(rounds[0])[1], count)
+    for bits in rounds[1:]:
         masks = masks_of(bits)
         part = x.shape[0] // len(masks)
         cut = [x[k * part : (k + 1) * part] for k in range(len(masks))]
@@ -333,23 +376,25 @@
     count = sizes[0][1] * sizes[1][1]
     rounds = rounds_of(sizes)
 
+    def where(first_scenario):
+        scen, wide = [lax.axis_index(axis).astype(jnp.int32) for axis in AXES]
+        lead = scen if first_scenario else jnp.int32(1)
+        return lead, wide, place_of(scen * sizes[1][1] + wide, rounds)
+
     def per_device(hess_scen, flags, low_d, low_s, up_d, up_s, coupling, pattern, region, hess_first):
         own, m = hess_first.shape
         rows = packed_rows(m, count)
-        scen, wide = [lax.axis_index(axis).astype(jnp.int32) for axis in AXES]
-        place = place_of(scen * sizes[1][1] + wide, rounds)
-        factors, total = [], None
+        factors, keep, send = [], None, None
         for i in range(hess_scen.shape[0]):
-            lead = scen if i == 0 else jnp.int32(1)
-            factor, gram = scenario(
-                jnp.stack([lead, wide, place]), region[i : i + 1], hess_scen[i],
+            factor, low, high = scenario(
+                functools.partial(where, i == 0), region[i : i + 1], hess_scen[i],
                 flags[i : i + 1], low_d[i : i + 1], low_s[i : i + 1], up_d[i : i + 1], up_s[i : i + 1],
                 coupling[i], pattern[i : i + 1], hess_first, rows, count,
             )
             factors.append(factor)
-            total = gram if total is None else total + gram
-        parts = sum_everywhere(total, rounds, count)
-        mine = first_section(jnp.stack([scen, wide, place]), parts, own, m, count)
+            keep, send = (low, high) if keep is None else (keep + low, send + high)
+        parts = sum_everywhere(keep, send, rounds, count)
+        mine = first_section(functools.partial(where, True), parts, own, m, count)
         return (jnp.stack(factors), mine)
 
     each = P(AXES)

time: 85.8 us -> 86 us (level)
  local copies, waits for them, and re-layouts: 2.26 us -> 7.75 us
  Pallas kernels: 37.2 us -> 32.4 us
    unnamed x11 -> x23, local copies, waits for them, and re-layouts: 0.93 us -> 7.69 us
    pallas_call x2, Pallas kernels: 37.2 us -> 32.4 us  [the longest x1 17.9 us: first_section(): pl.pallas_call(functools.partial(first_kernel, place_fn, count), out_shap...]
    slice x3 -> x2, local copies, waits for them, and re-layouts: 1.32 us -> 0.05 us  [sum_everywhere(): cut = [x[k * part:(k + 1) * part] for k in range(len(masks))]]
where the time goes in v3:
time: 86 us; the launch traced here: 85.6 us
  Pallas kernels  32.4 us (38%)
  waiting for transfers between devices  26.6 us (31%)
  starting transfers between devices  17.3 us (20%)
  local copies, waits for them, and re-layouts  7.75 us (9%)
  between operations  1.4 us (2%)
    ppermute x14, waiting for transfers between devices, swap(): return lax.ppermute(x, AXES, [(i, i ^ mask) for i in range(count)])  26.6 us
    pallas_call x1, Pallas kernels, first_section(): pl.pallas_call(functools.partial(first_kernel, place_fn, count), out_shap...  17.9 us
    ppermute x14, starting transfers between devices, swap(): return lax.ppermute(x, AXES, [(i, i ^ mask) for i in range(count)])  17.3 us
    pallas_call x1, Pallas kernels, scenario(): pl.pallas_call(functools.partial(scenario_kernel, place_fn, count), out_s...  14.5 us
    unnamed x23, local copies, waits for them, and re-layouts  7.69 us
  transfers between devices with their start and end apart: 14, of which 11 were waited for; matrix products, arithmetic and copies ran while one was open for 0% of the time, Pallas kernels for 0%

profile of v3, /device:TPU:0, one launch (start us, length us, event | category | flops | bytes accessed | tf_op | source)
XLA Modules:
  0.0 85.6 jit_solution(396639522939710672)
XLA Ops:
  1.3 0.0 copy-start
  1.3 1.4 %copy-done = f32[1,512,768]{2,1,0:T(8,128)S(1)} copy-done((f32[1,512,768]{2,1,0:T(8,128)S(1)}, f32[1,512,768]{2,1,0:T(8,128)}, u32[]{:S(2)}) %copy-start) | copy-done | bytes 1572888
  2.7 0.0 copy-start.1
  2.7 1.2 %copy-done.1 = f32[1,512,512]{2,1,0:T(8,128)S(1)} copy-done((f32[1,512,512]{2,1,0:T(8,128)S(1)}, f32[1,512,512]{2,1,0:T(8,128)}, u32[]{:S(2)}) %copy-start.1) | copy-done | bytes 1048600
  3.9 0.0 copy-start.2
  3.9 1.0 %copy-done.2 = f32[96,768]{1,0:T(8,128)S(1)} copy-done((f32[96,768]{1,0:T(8,128)S(1)}, f32[96,768]{1,0:T(8,128)}, u32[]{:S(2)}) %copy-start.2) | copy-done | bytes 294936
  4.9 0.0 copy-start.3
  4.9 0.7 copy-done.3
  5.6 0.0 copy-start.4
  5.6 0.7 copy-done.4
  6.2 0.0 copy-start.5
  6.2 0.7 copy-done.5
  6.9 0.0 copy-start.6
  6.9 0.7 copy-done.6
  7.6 0.0 copy-start.7
  7.6 0.7 copy-done.7
  8.3 0.0 copy-start.8
  8.3 0.7 copy-done.8
  8.9 14.5 %scenario.1 = (f32[512,512]{1,0:T(8,128)}, f32[1408,128]{1,0:T(8,128)S(1)}, f32[1408,128]{1,0:T(8,128)S(1)}) custom-call(s32[1]{0:T(128)S(6)} %copy.18.region, f32[512,512]{1,0:T(8,128)S(1)} %bitcast.4, s32[1,512]{1,0:T(1,128)S(1)} %copy-done.3, f32[1,512]{1,0:T(1,128)S(1)} %copy-done.4, f32[1,512]{1,0:T(1,128)S(1)} %copy-done.5, f32[1,512]{1,0:T(1,128)S(1)} %copy-done.6, ...), custom_call_target="tpu_custom_call" | custom-call | tf_op jit(solution)/shard_map/scenario/pallas_call | solution.py:292
  23.5 0.5 collective-permute-start
  24.0 1.8 %collective-permute-done = f32[1408,128]{1,0:T(8,128)S(1)} collective-permute-done((f32[1408,128]{1,0:T(8,128)S(1)}, f32[1408,128]{1,0:T(8,128)S(1)}, u32[]{:S(2)}, u32[]{:S(2)}) %collective-permute-start) | collective-permute-done | bytes 720928 | tf_op jit(solution)/shard_map/ppermute | solution.py:341
  25.8 0.1 add.21
  26.0 2.9 %collective-permute-start.1 = (f32[352,128]{1,0:T(8,128)S(1)}, f32[352,128]{1,0:T(8,128)S(1)}, u32[]{:S(2)}, u32[]{:S(2)}) collective-permute-start(f32[352,128]{1,0:T(8,128)S(1)} %get-tuple-element.10), channel_id=1, source_target_pairs={{0,16},{1,17},{2,18},{3,19},{4,20},{5,21},{6,22},{7,23},{8,24},{9,... | collective-permute-start | bytes 540680 | tf_op jit(solution)/shard_map/ppermute | solution.py:341
  28.9 1.5 %collective-permute-start.3 = (f32[352,128]{1,0:T(8,128)S(1)}, f32[352,128]{1,0:T(8,128)S(1)}, u32[]{:S(2)}, u32[]{:S(2)}) collective-permute-start(f32[352,128]{1,0:T(8,128)S(1)} %get-tuple-element.11), channel_id=1, source_target_pairs={{0,17},{1,16},{2,19},{3,18},{4,21},{5,20},{6,23},{7,22},{8,25},{9,... | collective-permute-start | bytes 540680 | tf_op jit(solution)/shard_map/ppermute | solution.py:341
  30.4 0.0 collective-permute-start.2
  30.4 3.9 %collective-permute-done.1 = f32[352,128]{1,0:T(8,128)S(1)} collective-permute-done((f32[352,128]{1,0:T(8,128)S(1)}, f32[352,128]{1,0:T(8,128)S(1)}, u32[]{:S(2)}, u32[]{:S(2)}) %collective-permute-start.1) | collective-permute-done | bytes 180256 | tf_op jit(solution)/shard_map/ppermute | solution.py:341
  34.3 4.7 %collective-permute-done.3 = f32[352,128]{1,0:T(8,128)S(1)} collective-permute-done((f32[352,128]{1,0:T(8,128)S(1)}, f32[352,128]{1,0:T(8,128)S(1)}, u32[]{:S(2)}, u32[]{:S(2)}) %collective-permute-start.3) | collective-permute-done | bytes 180256 | tf_op jit(solution)/shard_map/ppermute | solution.py:341
  38.9 1.4 %collective-permute-done.2 = f32[352,128]{1,0:T(8,128)S(1)} collective-permute-done((f32[352,128]{1,0:T(8,128)S(1)}, f32[352,128]{1,0:T(8,128)S(1)}, u32[]{:S(2)}, u32[]{:S(2)}) %collective-permute-start.2) | collective-permute-done | bytes 180256 | tf_op jit(solution)/shard_map/ppermute | solution.py:341
  40.3 0.1 fusion.1
  40.4 1.6 %collective-permute-start.4 = (f32[88,128]{1,0:T(8,128)S(1)}, f32[88,128]{1,0:T(8,128)S(1)}, u32[]{:S(2)}, u32[]{:S(2)}) collective-permute-start(f32[88,128]{1,0:T(8,128)S(1)} %get-tuple-element.13), channel_id=1, source_target_pairs={{0,2},{1,3},{2,0},{3,1},{4,6},{5,7},{6,4},{7,5},{8,10},{9,11},{10,... | collective-permute-start | bytes 135176 | tf_op jit(solution)/shard_map/ppermute | solution.py:341
  42.0 2.5 %collective-permute-start.6 = (f32[88,128]{1,0:T(8,128)S(1)}, f32[88,128]{1,0:T(8,128)S(1)}, u32[]{:S(2)}, u32[]{:S(2)}) collective-permute-start(f32[88,128]{1,0:T(8,128)S(1)} %get-tuple-element.14), channel_id=1, source_target_pairs={{0,6},{1,7},{2,4},{3,5},{4,2},{5,3},{6,0},{7,1},{8,14},{9,15},{10,... | collective-permute-start | bytes 135176 | tf_op jit(solution)/shard_map/ppermute | solution.py:341
  44.5 0.1 collective-permute-start.5
  44.6 0.3 collective-permute-done.4
  44.9 2.9 %collective-permute-done.6 = f32[88,128]{1,0:T(8,128)S(1)} collective-permute-done((f32[88,128]{1,0:T(8,128)S(1)}, f32[88,128]{1,0:T(8,128)S(1)}, u32[]{:S(2)}, u32[]{:S(2)}) %collective-permute-start.6) | collective-permute-done | bytes 45088 | tf_op jit(solution)/shard_map/ppermute | solution.py:341
  47.8 2.1 %collective-permute-done.5 = f32[88,128]{1,0:T(8,128)S(1)} collective-permute-done((f32[88,128]{1,0:T(8,128)S(1)}, f32[88,128]{1,0:T(8,128)S(1)}, u32[]{:S(2)}, u32[]{:S(2)}) %collective-permute-start.5) | collective-permute-done | bytes 45088 | tf_op jit(solution)/shard_map/ppermute | solution.py:341
  49.9 1.9 %collective-permute-start.9 = (f32[88,128]{1,0:T(8,128)S(1)}, f32[88,128]{1,0:T(8,128)S(1)}, u32[]{:S(2)}, u32[]{:S(2)}) collective-permute-start(f32[88,128]{1,0:T(8,128)S(1)} %get-tuple-element.9), channel_id=1, source_target_pairs={{0,6},{1,7},{2,4},{3,5},{4,2},{5,3},{6,0},{7,1},{8,14},{9,15},{10,... | collective-permute-start | bytes 135176 | tf_op jit(solution)/shard_map/ppermute | solution.py:341
  51.8 0.0 collective-permute-start.8
  51.9 2.5 %collective-permute-start.7 = (f32[88,128]{1,0:T(8,128)S(1)}, f32[88,128]{1,0:T(8,128)S(1)}, u32[]{:S(2)}, u32[]{:S(2)}) collective-permute-start(f32[88,128]{1,0:T(8,128)S(1)} %get-tuple-element.9), channel_id=1, source_target_pairs={{0,2},{1,3},{2,0},{3,1},{4,6},{5,7},{6,4},{7,5},{8,10},{9,11},{10,... | collective-permute-start | bytes 135176 | tf_op jit(solution)/shard_map/ppermute | solution.py:341
  54.4 1.5 %collective-permute-done.9 = f32[88,128]{1,0:T(8,128)S(1)} collective-permute-done((f32[88,128]{1,0:T(8,128)S(1)}, f32[88,128]{1,0:T(8,128)S(1)}, u32[]{:S(2)}, u32[]{:S(2)}) %collective-permute-start.9) | collective-permute-done | bytes 45088 | tf_op jit(solution)/shard_map/ppermute | solution.py:341
  55.8 1.0 %collective-permute-done.8 = f32[88,128]{1,0:T(8,128)S(1)} collective-permute-done((f32[88,128]{1,0:T(8,128)S(1)}, f32[88,128]{1,0:T(8,128)S(1)}, u32[]{:S(2)}, u32[]{:S(2)}) %collective-permute-start.8) | collective-permute-done | bytes 45088 | tf_op jit(solution)/shard_map/ppermute | solution.py:341
  56.9 0.0 collective-permute-done.7
  56.9 1.5 %collective-permute-start.12 = (f32[352,128]{1,0:T(8,128)S(1)}, f32[352,128]{1,0:T(8,128)S(1)}, u32[]{:S(2)}, u32[]{:S(2)}) collective-permute-start(f32[352,128]{1,0:T(8,128)S(1)} %pad_maximum_fusion), channel_id=1, source_target_pairs={{0,17},{1,16},{2,19},{3,18},{4,21},{5,20},{6,23},{7,22},{8,25},{9,... | collective-permute-start | bytes 540680 | tf_op jit(solution)/shard_map/ppermute | solution.py:341
  58.4 1.5 %collective-permute-start.11 = (f32[352,128]{1,0:T(8,128)S(1)}, f32[352,128]{1,0:T(8,128)S(1)}, u32[]{:S(2)}, u32[]{:S(2)}) collective-permute-start(f32[352,128]{1,0:T(8,128)S(1)} %pad_maximum_fusion), channel_id=1, source_target_pairs={{0,1},{1,0},{2,3},{3,2},{4,5},{5,4},{6,7},{7,6},{8,9},{9,8},{10,11... | collective-permute-start | bytes 540680 | tf_op jit(solution)/shard_map/ppermute | solution.py:341
  59.9 0.6 collective-permute-start.10
  60.5 4.9 %collective-permute-done.10 = f32[352,128]{1,0:T(8,128)S(1)} collective-permute-done((f32[352,128]{1,0:T(8,128)S(1)}, f32[352,128]{1,0:T(8,128)S(1)}, u32[]{:S(2)}, u32[]{:S(2)}) %collective-permute-start.10) | collective-permute-done | bytes 180256 | tf_op jit(solution)/shard_map/ppermute | solution.py:341
  65.4 0.0 collective-permute-done.11
  65.4 0.0 collective-permute-done.12
  65.5 0.1 collective-permute-start.13
  65.6 2.2 %collective-permute-done.13.refs_1_ = f32[1408,128]{1,0:T(8,128)S(1)} collective-permute-done((f32[1408,128]{1,0:T(8,128)S(1)}, f32[1408,128]{1,0:T(8,128)S(1)}, u32[]{:S(2)}, u32[]{:S(2)}) %collective-permute-start.13) | collective-permute-done | bytes 720928 | tf_op jit(solution)/shard_map/ppermute | solution.py:341
  67.7 17.9 %first_section.1 = f32[96,768]{1,0:T(8,128)} custom-call(f32[1408,128]{1,0:T(8,128)S(1)} %constant_dynamic-update-slice_fusion.refs_0_, f32[1408,128]{1,0:T(8,128)S(1)} %collective-permute-done.13.refs_1_), custom_call_target="tpu_custom_call" | custom-call | tf_op jit(solution)/shard_map/first_section/pallas_call | solution.py:319
  (10 shorter events, 0.1 us)
Async XLA Ops:
  1.3 1.4 %copy-start = (f32[1,512,768]{2,1,0:T(8,128)S(1)}, f32[1,512,768]{2,1,0:T(8,128)}, u32[]{:S(2)}) copy-start(f32[1,512,768]{2,1,0:T(8,128)} %param.16) | copy-start | bytes 4718596
  2.7 1.2 %copy-start.1 = (f32[1,512,512]{2,1,0:T(8,128)S(1)}, f32[1,512,512]{2,1,0:T(8,128)}, u32[]{:S(2)}) copy-start(f32[1,512,512]{2,1,0:T(8,128)} %param.10) | copy-start | bytes 3145732
  3.9 1.0 %copy-start.2 = (f32[96,768]{1,0:T(8,128)S(1)}, f32[96,768]{1,0:T(8,128)}, u32[]{:S(2)}) copy-start(f32[96,768]{1,0:T(8,128)} %first.1) | copy-start | bytes 884740
  4.9 0.7 copy-start.3
  5.6 0.7 copy-start.4
  6.2 0.7 copy-start.5
  6.9 0.7 copy-start.6
  7.6 0.7 copy-start.7
  8.3 0.7 copy-start.8
  23.5 2.3 %collective-permute-start = (f32[1408,128]{1,0:T(8,128)S(1)}, f32[1408,128]{1,0:T(8,128)S(1)}, u32[]{:S(2)}, u32[]{:S(2)}) collective-permute-start(f32[1408,128]{1,0:T(8,128)S(1)} %get-tuple-element.7), channel_id=1, source_target_pairs={{0,8},{1,9},{2,10},{3,11},{4,12},{5,13},{6,14},{7,15},{8,0},{9,1},... | collective-permute-start | bytes 2162696 | tf_op jit(solution)/shard_map/ppermute | solution.py:341
  26.0 8.3 %collective-permute-start.1 = (f32[352,128]{1,0:T(8,128)S(1)}, f32[352,128]{1,0:T(8,128)S(1)}, u32[]{:S(2)}, u32[]{:S(2)}) collective-permute-start(f32[352,128]{1,0:T(8,128)S(1)} %get-tuple-element.10), channel_id=1, source_target_pairs={{0,16},{1,17},{2,18},{3,19},{4,20},{5,21},{6,22},{7,23},{8,24},{9,... | collective-permute-start | bytes 540680 | tf_op jit(solution)/shard_map/ppermute | solution.py:341
  28.9 10.1 %collective-permute-start.3 = (f32[352,128]{1,0:T(8,128)S(1)}, f32[352,128]{1,0:T(8,128)S(1)}, u32[]{:S(2)}, u32[]{:S(2)}) collective-permute-start(f32[352,128]{1,0:T(8,128)S(1)} %get-tuple-element.11), channel_id=1, source_target_pairs={{0,17},{1,16},{2,19},{3,18},{4,21},{5,20},{6,23},{7,22},{8,25},{9,... | collective-permute-start | bytes 540680 | tf_op jit(solution)/shard_map/ppermute | solution.py:341
  30.4 9.9 %collective-permute-start.2 = (f32[352,128]{1,0:T(8,128)S(1)}, f32[352,128]{1,0:T(8,128)S(1)}, u32[]{:S(2)}, u32[]{:S(2)}) collective-permute-start(f32[352,128]{1,0:T(8,128)S(1)} %get-tuple-element.12), channel_id=1, source_target_pairs={{0,1},{1,0},{2,3},{3,2},{4,5},{5,4},{6,7},{7,6},{8,9},{9,8},{10,11... | collective-permute-start | bytes 540680 | tf_op jit(solution)/shard_map/ppermute | solution.py:341
  40.4 4.6 %collective-permute-start.4 = (f32[88,128]{1,0:T(8,128)S(1)}, f32[88,128]{1,0:T(8,128)S(1)}, u32[]{:S(2)}, u32[]{:S(2)}) collective-permute-start(f32[88,128]{1,0:T(8,128)S(1)} %get-tuple-element.13), channel_id=1, source_target_pairs={{0,2},{1,3},{2,0},{3,1},{4,6},{5,7},{6,4},{7,5},{8,10},{9,11},{10,... | collective-permute-start | bytes 135176 | tf_op jit(solution)/shard_map/ppermute | solution.py:341
  42.0 5.8 %collective-permute-start.6 = (f32[88,128]{1,0:T(8,128)S(1)}, f32[88,128]{1,0:T(8,128)S(1)}, u32[]{:S(2)}, u32[]{:S(2)}) collective-permute-start(f32[88,128]{1,0:T(8,128)S(1)} %get-tuple-element.14), channel_id=1, source_target_pairs={{0,6},{1,7},{2,4},{3,5},{4,2},{5,3},{6,0},{7,1},{8,14},{9,15},{10,... | collective-permute-start | bytes 135176 | tf_op jit(solution)/shard_map/ppermute | solution.py:341
  44.5 5.4 %collective-permute-start.5 = (f32[88,128]{1,0:T(8,128)S(1)}, f32[88,128]{1,0:T(8,128)S(1)}, u32[]{:S(2)}, u32[]{:S(2)}) collective-permute-start(f32[88,128]{1,0:T(8,128)S(1)} %get-tuple-element.15), channel_id=1, source_target_pairs={{0,4},{1,5},{2,6},{3,7},{4,0},{5,1},{6,2},{7,3},{8,12},{9,13},{10,... | collective-permute-start | bytes 135176 | tf_op jit(solution)/shard_map/ppermute | solution.py:341
  49.9 5.9 %collective-permute-start.9 = (f32[88,128]{1,0:T(8,128)S(1)}, f32[88,128]{1,0:T(8,128)S(1)}, u32[]{:S(2)}, u32[]{:S(2)}) collective-permute-start(f32[88,128]{1,0:T(8,128)S(1)} %get-tuple-element.9), channel_id=1, source_target_pairs={{0,6},{1,7},{2,4},{3,5},{4,2},{5,3},{6,0},{7,1},{8,14},{9,15},{10,... | collective-permute-start | bytes 135176 | tf_op jit(solution)/shard_map/ppermute | solution.py:341
  51.8 5.0 %collective-permute-start.8 = (f32[88,128]{1,0:T(8,128)S(1)}, f32[88,128]{1,0:T(8,128)S(1)}, u32[]{:S(2)}, u32[]{:S(2)}) collective-permute-start(f32[88,128]{1,0:T(8,128)S(1)} %get-tuple-element.9), channel_id=1, source_target_pairs={{0,4},{1,5},{2,6},{3,7},{4,0},{5,1},{6,2},{7,3},{8,12},{9,13},{10,... | collective-permute-start | bytes 135176 | tf_op jit(solution)/shard_map/ppermute | solution.py:341
  51.9 5.0 %collective-permute-start.7 = (f32[88,128]{1,0:T(8,128)S(1)}, f32[88,128]{1,0:T(8,128)S(1)}, u32[]{:S(2)}, u32[]{:S(2)}) collective-permute-start(f32[88,128]{1,0:T(8,128)S(1)} %get-tuple-element.9), channel_id=1, source_target_pairs={{0,2},{1,3},{2,0},{3,1},{4,6},{5,7},{6,4},{7,5},{8,10},{9,11},{10,... | collective-permute-start | bytes 135176 | tf_op jit(solution)/shard_map/ppermute | solution.py:341
  56.9 8.5 %collective-permute-start.12 = (f32[352,128]{1,0:T(8,128)S(1)}, f32[352,128]{1,0:T(8,128)S(1)}, u32[]{:S(2)}, u32[]{:S(2)}) collective-permute-start(f32[352,128]{1,0:T(8,128)S(1)} %pad_maximum_fusion), channel_id=1, source_target_pairs={{0,17},{1,16},{2,19},{3,18},{4,21},{5,20},{6,23},{7,22},{8,25},{9,... | collective-permute-start | bytes 540680 | tf_op jit(solution)/shard_map/ppermute | solution.py:341
  58.4 7.0 %collective-permute-start.11 = (f32[352,128]{1,0:T(8,128)S(1)}, f32[352,128]{1,0:T(8,128)S(1)}, u32[]{:S(2)}, u32[]{:S(2)}) collective-permute-start(f32[352,128]{1,0:T(8,128)S(1)} %pad_maximum_fusion), channel_id=1, source_target_pairs={{0,1},{1,0},{2,3},{3,2},{4,5},{5,4},{6,7},{7,6},{8,9},{9,8},{10,11... | collective-permute-start | bytes 540680 | tf_op jit(solution)/shard_map/ppermute | solution.py:341
  59.9 5.5 %collective-permute-start.10 = (f32[352,128]{1,0:T(8,128)S(1)}, f32[352,128]{1,0:T(8,128)S(1)}, u32[]{:S(2)}, u32[]{:S(2)}) collective-permute-start(f32[352,128]{1,0:T(8,128)S(1)} %pad_maximum_fusion), channel_id=1, source_target_pairs={{0,16},{1,17},{2,18},{3,19},{4,20},{5,21},{6,22},{7,23},{8,24},{9,... | collective-permute-start | bytes 540680 | tf_op jit(solution)/shard_map/ppermute | solution.py:341
  65.5 2.3 %collective-permute-start.13 = (f32[1408,128]{1,0:T(8,128)S(1)}, f32[1408,128]{1,0:T(8,128)S(1)}, u32[]{:S(2)}, u32[]{:S(2)}) collective-permute-start(f32[1408,128]{1,0:T(8,128)S(1)} %constant_dynamic-update-slice_fusion.refs_0_), channel_id=1, source_target_pairs={{0,8},{1,9},{2,10},{3,11},{4,12},{5,13},{6,14},{7,15},{8,0},{9,1},... | collective-permute-start | bytes 2162696 | tf_op jit(solution)/shard_map/ppermute | solution.py:341

commit v4 on v3

--- a/solution.py
+++ b/solution.py
@@ -311,7 +311,7 @@
         ],
         compiler_params=pltpu.CompilerParams(vmem_limit_bytes=GRANT),
         name="scenario",
-    )(region, hess, flags, low_d, low_s, up_d, up_s, coup, pattern, first)
+    )(region, *[pltpu.with_memory_space_constraint(v, pltpu.HBM) for v in (hess, flags, low_d, low_s, up_d, up_s, coup, pattern, first)])
 
 
 def first_section(place_fn, parts, own, m, count):
@@ -356,13 +356,17 @@
     return sum(((flat // bit) % 2) << k for k, bit in enumerate(bits))
 
 
+def farthest_first(n):
+    return sorted(range(1, n), key=lambda k: (-k.bit_count(), k))
+
+
 def sum_everywhere(x, sent, rounds, count):
     x = x + swap(sent, masks_of(rounds[0])[1], count)
     for bits in rounds[1:]:
         masks = masks_of(bits)
         part = x.shape[0] // len(masks)
         cut = [x[k * part : (k + 1) * part] for k in range(len(masks))]
-        got = [swap(c, mask, count) for c, mask in zip(cut[1:], masks[1:])]
+        got = [swap(cut[k], masks[k], count) for k in farthest_first(len(masks))]
         x = functools.reduce(jnp.add, got, cut[0])
     parts = [x]
     for bits in reversed(rounds):

time: 86 us -> 78.3 us (0.910)
  local copies, waits for them, and re-layouts: 7.75 us -> 0.1 us
  waiting for transfers between devices: 26.6 us -> 25.4 us
  Pallas kernels: 32.4 us -> 33.4 us
    unnamed x23 -> x5, local copies, waits for them, and re-layouts: 7.69 us -> 0.04 us
    ppermute x14, waiting for transfers between devices: 26.6 us -> 25.4 us  [swap(): return lax.ppermute(x, AXES, [(i, i ^ mask) for i in range(count)])]
    pallas_call x1, Pallas kernels: 14.5 us -> 15.6 us  [scenario(): pl.pallas_call(functools.partial(scenario_kernel, place_fn, count), out_s...]
  transfers between devices with their start and end apart: 14 -> 14, of which waited for: 11 -> 10; matrix products, arithmetic and copies ran while one was open for 0% -> 0% of each run, Pallas kernels for 0% -> 0%
where the time goes in v4:
time: 78.3 us; the launch traced here: 78.1 us
  Pallas kernels  33.4 us (43%)
  waiting for transfers between devices  25.4 us (32%)
  starting transfers between devices  17.6 us (22%)
  between operations  1.38 us (2%)
    ppermute x14, waiting for transfers between devices, swap(): return lax.ppermute(x, AXES, [(i, i ^ mask) for i in range(count)])  25.4 us
    pallas_call x1, Pallas kernels, first_section(): pl.pallas_call(functools.partial(first_kernel, place_fn, count), out_shap...  17.9 us
    ppermute x14, starting transfers between devices, swap(): return lax.ppermute(x, AXES, [(i, i ^ mask) for i in range(count)])  17.6 us
    pallas_call x1, Pallas kernels, scenario(): pl.pallas_call(functools.partial(scenario_kernel, place_fn, count), out_s...  15.6 us
  transfers between devices with their start and end apart: 14, of which 10 were waited for; matrix products, arithmetic and copies ran while one was open for 0% of the time, Pallas kernels for 0%

profile of v4, /device:TPU:0, one launch (start us, length us, event | category | flops | bytes accessed | tf_op | source)
XLA Modules:
  0.0 78.1 jit_solution(2017158119928434150)
XLA Ops:
  1.3 15.6 %scenario.1 = (f32[512,512]{1,0:T(8,128)}, f32[1408,128]{1,0:T(8,128)S(1)}, f32[1408,128]{1,0:T(8,128)S(1)}) custom-call(s32[1]{0:T(128)S(6)} %copy.18.region, f32[512,512]{1,0:T(8,128)} %bitcast.4, s32[1,512]{1,0:T(1,128)} %flags.1, f32[1,512]{1,0:T(1,128)} %low_d.1, f32[1,512]{1,0:T(1,128)} %low_s.1, f32[1,512]{1,0:T(1,128)} %up_d.1, f32[1,512]{1,0:T(1,128)} %up_s.1, ...), custom_call_target="tpu_custom_call" | custom-call | tf_op jit(solution)/shard_map/scenario/pallas_call | solution.py:292
  16.8 0.5 collective-permute-start
  17.4 1.8 %collective-permute-done = f32[1408,128]{1,0:T(8,128)S(1)} collective-permute-done((f32[1408,128]{1,0:T(8,128)S(1)}, f32[1408,128]{1,0:T(8,128)S(1)}, u32[]{:S(2)}, u32[]{:S(2)}) %collective-permute-start) | collective-permute-done | bytes 720928 | tf_op jit(solution)/shard_map/ppermute | solution.py:341
  19.2 0.1 add.21
  19.3 3.9 %collective-permute-start.1 = (f32[352,128]{1,0:T(8,128)S(1)}, f32[352,128]{1,0:T(8,128)S(1)}, u32[]{:S(2)}, u32[]{:S(2)}) collective-permute-start(f32[352,128]{1,0:T(8,128)S(1)} %get-tuple-element.10), channel_id=1, source_target_pairs={{0,17},{1,16},{2,19},{3,18},{4,21},{5,20},{6,23},{7,22},{8,25},{9,... | collective-permute-start | bytes 540680 | tf_op jit(solution)/shard_map/ppermute | solution.py:341
  23.2 0.5 collective-permute-start.3
  23.7 0.1 collective-permute-start.2
  23.8 4.8 %collective-permute-done.1 = f32[352,128]{1,0:T(8,128)S(1)} collective-permute-done((f32[352,128]{1,0:T(8,128)S(1)}, f32[352,128]{1,0:T(8,128)S(1)}, u32[]{:S(2)}, u32[]{:S(2)}) %collective-permute-start.1) | collective-permute-done | bytes 180256 | tf_op jit(solution)/shard_map/ppermute | solution.py:341
  28.6 3.3 %collective-permute-done.3 = f32[352,128]{1,0:T(8,128)S(1)} collective-permute-done((f32[352,128]{1,0:T(8,128)S(1)}, f32[352,128]{1,0:T(8,128)S(1)}, u32[]{:S(2)}, u32[]{:S(2)}) %collective-permute-start.3) | collective-permute-done | bytes 180256 | tf_op jit(solution)/shard_map/ppermute | solution.py:341
  31.9 0.3 collective-permute-done.2
  32.2 0.1 fusion.1
  32.3 3.7 %collective-permute-start.4 = (f32[88,128]{1,0:T(8,128)S(1)}, f32[88,128]{1,0:T(8,128)S(1)}, u32[]{:S(2)}, u32[]{:S(2)}) collective-permute-start(f32[88,128]{1,0:T(8,128)S(1)} %get-tuple-element.13), channel_id=1, source_target_pairs={{0,6},{1,7},{2,4},{3,5},{4,2},{5,3},{6,0},{7,1},{8,14},{9,15},{10,... | collective-permute-start | bytes 135176 | tf_op jit(solution)/shard_map/ppermute | solution.py:341
  36.0 0.0 collective-permute-start.6
  36.0 0.8 %collective-permute-start.5 = (f32[88,128]{1,0:T(8,128)S(1)}, f32[88,128]{1,0:T(8,128)S(1)}, u32[]{:S(2)}, u32[]{:S(2)}) collective-permute-start(f32[88,128]{1,0:T(8,128)S(1)} %get-tuple-element.15), channel_id=1, source_target_pairs={{0,2},{1,3},{2,0},{3,1},{4,6},{5,7},{6,4},{7,5},{8,10},{9,11},{10,... | collective-permute-start | bytes 135176 | tf_op jit(solution)/shard_map/ppermute | solution.py:341
  36.8 1.6 %collective-permute-done.4 = f32[88,128]{1,0:T(8,128)S(1)} collective-permute-done((f32[88,128]{1,0:T(8,128)S(1)}, f32[88,128]{1,0:T(8,128)S(1)}, u32[]{:S(2)}, u32[]{:S(2)}) %collective-permute-start.4) | collective-permute-done | bytes 45088 | tf_op jit(solution)/shard_map/ppermute | solution.py:341
  38.3 2.6 %collective-permute-done.6 = f32[88,128]{1,0:T(8,128)S(1)} collective-permute-done((f32[88,128]{1,0:T(8,128)S(1)}, f32[88,128]{1,0:T(8,128)S(1)}, u32[]{:S(2)}, u32[]{:S(2)}) %collective-permute-start.6) | collective-permute-done | bytes 45088 | tf_op jit(solution)/shard_map/ppermute | solution.py:341
  40.9 0.0 collective-permute-done.5
  40.9 1.9 %collective-permute-start.9 = (f32[88,128]{1,0:T(8,128)S(1)}, f32[88,128]{1,0:T(8,128)S(1)}, u32[]{:S(2)}, u32[]{:S(2)}) collective-permute-start(f32[88,128]{1,0:T(8,128)S(1)} %get-tuple-element.9), channel_id=1, source_target_pairs={{0,6},{1,7},{2,4},{3,5},{4,2},{5,3},{6,0},{7,1},{8,14},{9,15},{10,... | collective-permute-start | bytes 135176 | tf_op jit(solution)/shard_map/ppermute | solution.py:341
  42.9 0.2 collective-permute-start.8
  43.1 2.3 %collective-permute-start.7 = (f32[88,128]{1,0:T(8,128)S(1)}, f32[88,128]{1,0:T(8,128)S(1)}, u32[]{:S(2)}, u32[]{:S(2)}) collective-permute-start(f32[88,128]{1,0:T(8,128)S(1)} %get-tuple-element.9), channel_id=1, source_target_pairs={{0,2},{1,3},{2,0},{3,1},{4,6},{5,7},{6,4},{7,5},{8,10},{9,11},{10,... | collective-permute-start | bytes 135176 | tf_op jit(solution)/shard_map/ppermute | solution.py:341
  45.4 1.5 %collective-permute-done.9 = f32[88,128]{1,0:T(8,128)S(1)} collective-permute-done((f32[88,128]{1,0:T(8,128)S(1)}, f32[88,128]{1,0:T(8,128)S(1)}, u32[]{:S(2)}, u32[]{:S(2)}) %collective-permute-start.9) | collective-permute-done | bytes 45088 | tf_op jit(solution)/shard_map/ppermute | solution.py:341
  46.9 1.4 %collective-permute-done.8 = f32[88,128]{1,0:T(8,128)S(1)} collective-permute-done((f32[88,128]{1,0:T(8,128)S(1)}, f32[88,128]{1,0:T(8,128)S(1)}, u32[]{:S(2)}, u32[]{:S(2)}) %collective-permute-start.8) | collective-permute-done | bytes 45088 | tf_op jit(solution)/shard_map/ppermute | solution.py:341
  48.3 0.0 collective-permute-done.7
  48.3 1.3 %collective-permute-start.12 = (f32[352,128]{1,0:T(8,128)S(1)}, f32[352,128]{1,0:T(8,128)S(1)}, u32[]{:S(2)}, u32[]{:S(2)}) collective-permute-start(f32[352,128]{1,0:T(8,128)S(1)} %pad_maximum_fusion), channel_id=1, source_target_pairs={{0,17},{1,16},{2,19},{3,18},{4,21},{5,20},{6,23},{7,22},{8,25},{9,... | collective-permute-start | bytes 540680 | tf_op jit(solution)/shard_map/ppermute | solution.py:341
  49.6 1.7 %collective-permute-start.11 = (f32[352,128]{1,0:T(8,128)S(1)}, f32[352,128]{1,0:T(8,128)S(1)}, u32[]{:S(2)}, u32[]{:S(2)}) collective-permute-start(f32[352,128]{1,0:T(8,128)S(1)} %pad_maximum_fusion), channel_id=1, source_target_pairs={{0,1},{1,0},{2,3},{3,2},{4,5},{5,4},{6,7},{7,6},{8,9},{9,8},{10,11... | collective-permute-start | bytes 540680 | tf_op jit(solution)/shard_map/ppermute | solution.py:341
  51.3 0.6 collective-permute-start.10
  51.9 6.0 %collective-permute-done.10 = f32[352,128]{1,0:T(8,128)S(1)} collective-permute-done((f32[352,128]{1,0:T(8,128)S(1)}, f32[352,128]{1,0:T(8,128)S(1)}, u32[]{:S(2)}, u32[]{:S(2)}) %collective-permute-start.10) | collective-permute-done | bytes 180256 | tf_op jit(solution)/shard_map/ppermute | solution.py:341
  57.9 0.0 collective-permute-done.11
  57.9 0.0 collective-permute-done.12
  58.0 0.1 collective-permute-start.13
  58.0 2.2 %collective-permute-done.13.refs_1_ = f32[1408,128]{1,0:T(8,128)S(1)} collective-permute-done((f32[1408,128]{1,0:T(8,128)S(1)}, f32[1408,128]{1,0:T(8,128)S(1)}, u32[]{:S(2)}, u32[]{:S(2)}) %collective-permute-start.13) | collective-permute-done | bytes 720928 | tf_op jit(solution)/shard_map/ppermute | solution.py:341
  60.2 17.9 %first_section.1 = f32[96,768]{1,0:T(8,128)} custom-call(f32[1408,128]{1,0:T(8,128)S(1)} %constant_dynamic-update-slice_fusion.refs_0_, f32[1408,128]{1,0:T(8,128)S(1)} %collective-permute-done.13.refs_1_), custom_call_target="tpu_custom_call" | custom-call | tf_op jit(solution)/shard_map/first_section/pallas_call | solution.py:319
  (10 shorter events, 0.1 us)
Async XLA Ops:
  16.8 2.3 %collective-permute-start = (f32[1408,128]{1,0:T(8,128)S(1)}, f32[1408,128]{1,0:T(8,128)S(1)}, u32[]{:S(2)}, u32[]{:S(2)}) collective-permute-start(f32[1408,128]{1,0:T(8,128)S(1)} %get-tuple-element.7), channel_id=1, source_target_pairs={{0,8},{1,9},{2,10},{3,11},{4,12},{5,13},{6,14},{7,15},{8,0},{9,1},... | collective-permute-start | bytes 2162696 | tf_op jit(solution)/shard_map/ppermute | solution.py:341
  19.3 9.3 %collective-permute-start.1 = (f32[352,128]{1,0:T(8,128)S(1)}, f32[352,128]{1,0:T(8,128)S(1)}, u32[]{:S(2)}, u32[]{:S(2)}) collective-permute-start(f32[352,128]{1,0:T(8,128)S(1)} %get-tuple-element.10), channel_id=1, source_target_pairs={{0,17},{1,16},{2,19},{3,18},{4,21},{5,20},{6,23},{7,22},{8,25},{9,... | collective-permute-start | bytes 540680 | tf_op jit(solution)/shard_map/ppermute | solution.py:341
  23.2 8.7 %collective-permute-start.3 = (f32[352,128]{1,0:T(8,128)S(1)}, f32[352,128]{1,0:T(8,128)S(1)}, u32[]{:S(2)}, u32[]{:S(2)}) collective-permute-start(f32[352,128]{1,0:T(8,128)S(1)} %get-tuple-element.11), channel_id=1, source_target_pairs={{0,1},{1,0},{2,3},{3,2},{4,5},{5,4},{6,7},{7,6},{8,9},{9,8},{10,11... | collective-permute-start | bytes 540680 | tf_op jit(solution)/shard_map/ppermute | solution.py:341
  23.7 8.5 %collective-permute-start.2 = (f32[352,128]{1,0:T(8,128)S(1)}, f32[352,128]{1,0:T(8,128)S(1)}, u32[]{:S(2)}, u32[]{:S(2)}) collective-permute-start(f32[352,128]{1,0:T(8,128)S(1)} %get-tuple-element.12), channel_id=1, source_target_pairs={{0,16},{1,17},{2,18},{3,19},{4,20},{5,21},{6,22},{7,23},{8,24},{9,... | collective-permute-start | bytes 540680 | tf_op jit(solution)/shard_map/ppermute | solution.py:341
  32.3 6.0 %collective-permute-start.4 = (f32[88,128]{1,0:T(8,128)S(1)}, f32[88,128]{1,0:T(8,128)S(1)}, u32[]{:S(2)}, u32[]{:S(2)}) collective-permute-start(f32[88,128]{1,0:T(8,128)S(1)} %get-tuple-element.13), channel_id=1, source_target_pairs={{0,6},{1,7},{2,4},{3,5},{4,2},{5,3},{6,0},{7,1},{8,14},{9,15},{10,... | collective-permute-start | bytes 135176 | tf_op jit(solution)/shard_map/ppermute | solution.py:341
  36.0 4.9 %collective-permute-start.6 = (f32[88,128]{1,0:T(8,128)S(1)}, f32[88,128]{1,0:T(8,128)S(1)}, u32[]{:S(2)}, u32[]{:S(2)}) collective-permute-start(f32[88,128]{1,0:T(8,128)S(1)} %get-tuple-element.14), channel_id=1, source_target_pairs={{0,4},{1,5},{2,6},{3,7},{4,0},{5,1},{6,2},{7,3},{8,12},{9,13},{10,... | collective-permute-start | bytes 135176 | tf_op jit(solution)/shard_map/ppermute | solution.py:341
  36.0 4.9 %collective-permute-start.5 = (f32[88,128]{1,0:T(8,128)S(1)}, f32[88,128]{1,0:T(8,128)S(1)}, u32[]{:S(2)}, u32[]{:S(2)}) collective-permute-start(f32[88,128]{1,0:T(8,128)S(1)} %get-tuple-element.15), channel_id=1, source_target_pairs={{0,2},{1,3},{2,0},{3,1},{4,6},{5,7},{6,4},{7,5},{8,10},{9,11},{10,... | collective-permute-start | bytes 135176 | tf_op jit(solution)/shard_map/ppermute | solution.py:341
  40.9 6.0 %collective-permute-start.9 = (f32[88,128]{1,0:T(8,128)S(1)}, f32[88,128]{1,0:T(8,128)S(1)}, u32[]{:S(2)}, u32[]{:S(2)}) collective-permute-start(f32[88,128]{1,0:T(8,128)S(1)} %get-tuple-element.9), channel_id=1, source_target_pairs={{0,6},{1,7},{2,4},{3,5},{4,2},{5,3},{6,0},{7,1},{8,14},{9,15},{10,... | collective-permute-start | bytes 135176 | tf_op jit(solution)/shard_map/ppermute | solution.py:341
  42.9 5.4 %collective-permute-start.8 = (f32[88,128]{1,0:T(8,128)S(1)}, f32[88,128]{1,0:T(8,128)S(1)}, u32[]{:S(2)}, u32[]{:S(2)}) collective-permute-start(f32[88,128]{1,0:T(8,128)S(1)} %get-tuple-element.9), channel_id=1, source_target_pairs={{0,4},{1,5},{2,6},{3,7},{4,0},{5,1},{6,2},{7,3},{8,12},{9,13},{10,... | collective-permute-start | bytes 135176 | tf_op jit(solution)/shard_map/ppermute | solution.py:341
  43.1 5.2 %collective-permute-start.7 = (f32[88,128]{1,0:T(8,128)S(1)}, f32[88,128]{1,0:T(8,128)S(1)}, u32[]{:S(2)}, u32[]{:S(2)}) collective-permute-start(f32[88,128]{1,0:T(8,128)S(1)} %get-tuple-element.9), channel_id=1, source_target_pairs={{0,2},{1,3},{2,0},{3,1},{4,6},{5,7},{6,4},{7,5},{8,10},{9,11},{10,... | collective-permute-start | bytes 135176 | tf_op jit(solution)/shard_map/ppermute | solution.py:341
  48.3 9.6 %collective-permute-start.12 = (f32[352,128]{1,0:T(8,128)S(1)}, f32[352,128]{1,0:T(8,128)S(1)}, u32[]{:S(2)}, u32[]{:S(2)}) collective-permute-start(f32[352,128]{1,0:T(8,128)S(1)} %pad_maximum_fusion), channel_id=1, source_target_pairs={{0,17},{1,16},{2,19},{3,18},{4,21},{5,20},{6,23},{7,22},{8,25},{9,... | collective-permute-start | bytes 540680 | tf_op jit(solution)/shard_map/ppermute | solution.py:341
  49.6 8.3 %collective-permute-start.11 = (f32[352,128]{1,0:T(8,128)S(1)}, f32[352,128]{1,0:T(8,128)S(1)}, u32[]{:S(2)}, u32[]{:S(2)}) collective-permute-start(f32[352,128]{1,0:T(8,128)S(1)} %pad_maximum_fusion), channel_id=1, source_target_pairs={{0,1},{1,0},{2,3},{3,2},{4,5},{5,4},{6,7},{7,6},{8,9},{9,8},{10,11... | collective-permute-start | bytes 540680 | tf_op jit(solution)/shard_map/ppermute | solution.py:341
  51.3 6.5 %collective-permute-start.10 = (f32[352,128]{1,0:T(8,128)S(1)}, f32[352,128]{1,0:T(8,128)S(1)}, u32[]{:S(2)}, u32[]{:S(2)}) collective-permute-start(f32[352,128]{1,0:T(8,128)S(1)} %pad_maximum_fusion), channel_id=1, source_target_pairs={{0,16},{1,17},{2,18},{3,19},{4,20},{5,21},{6,22},{7,23},{8,24},{9,... | collective-permute-start | bytes 540680 | tf_op jit(solution)/shard_map/ppermute | solution.py:341
  58.0 2.3 %collective-permute-start.13 = (f32[1408,128]{1,0:T(8,128)S(1)}, f32[1408,128]{1,0:T(8,128)S(1)}, u32[]{:S(2)}, u32[]{:S(2)}) collective-permute-start(f32[1408,128]{1,0:T(8,128)S(1)} %constant_dynamic-update-slice_fusion.refs_0_), channel_id=1, source_target_pairs={{0,8},{1,9},{2,10},{3,11},{4,12},{5,13},{6,14},{7,15},{8,0},{9,1},... | collective-permute-start | bytes 2162696 | tf_op jit(solution)/shard_map/ppermute | solution.py:341

commit v5 on v4

--- a/solution.py
+++ b/solution.py
@@ -116,7 +116,7 @@
 
 def scenario_kernel(
     place_fn, count, region, hess_hbm, flags, low_d, low_s, up_d, up_s, coup_hbm, pattern, first,
-    factor_hbm, keep, send, hess, coup, factor, d_ref, ih, il, lh, ll, xh, xl, whole, in_sem, out_sem,
+    factor_hbm, keep, send, hess, coup, factor, d_ref, ih, il, lh, ll, xh, xl, whole, diagonal, in_sem, out_sem,
 ):
     n, m = coup.shape
     nt, mt = n // T, m // T
@@ -201,16 +201,19 @@
         at = pl.ds(pl.multiple_of(wide * own, 8), own)
         whole[at, :] = whole[at, :] + first[...]
 
+    pack_diagonal(whole, diagonal)
     half = count // 2
     chunk = keep.shape[0] // half
     for side in range(2):
 
         @pl.when(place // half == side)
         def _():
-            for l, at, rows, i, j in pieces(m, count * chunk, count):
+            for l, at, rows, square, i, j in pieces(m, count * chunk, count):
                 to = pl.multiple_of(((l ^ place) % half) * chunk, 8) + at
                 target = (keep, send)[(l // half) ^ side]
-                target[pl.ds(to, rows), :] = jnp.zeros((rows, T), F32) if i is None else whole[i : i + rows, j : j + T]
+                source = whole if square else diagonal
+                value = jnp.zeros((rows, T), F32) if square is None else source[i : i + rows, j : j + T]
+                target[pl.ds(to, rows), :] = value
 
     for store in stores:
         store.wait()
@@ -218,18 +221,27 @@
 
 def first_kernel(place_fn, count, *refs):
     _, wide, place = place_fn()
-    parts, (out, d_ref, panel_ref, lh, ll, full, packed) = refs[:-7], refs[-7:]
+    parts, (out, d_ref, ahead, lh, ll, full, work, diagonal) = refs[:-8], refs[-8:]
     m = full.shape[0]
     mt = m // T
     r, c = unit_block()
     eye = r == c
-    start = [sum(m - i * T for i in range(j)) for j in range(mt)]
-    chunk = packed.shape[0] // count
-    each = count // len(parts)
-    for p in range(count):
-        to = pl.multiple_of((place ^ p) * chunk, 8)
-        at = (p % each) * chunk
-        packed[pl.ds(to, chunk), :] = parts[p // each][at : at + chunk, :]
+    half = count // 2
+    chunk = parts[0].shape[0] // half
+    for side in range(2):
+
+        @pl.when(place // half == side)
+        def _():
+            for l, at, rows, square, i, j in pieces(m, count * chunk, count):
+                if square is not None:
+                    begin = pl.multiple_of(((l ^ place) % half) * chunk, 8) + at
+                    target = work if square else diagonal
+                    target[i : i + rows, j : j + T] = parts[(l // half) ^ side][pl.ds(begin, rows), :]
+
+    unpack_diagonal(work, diagonal)
+    for ref in (lh, ll):
+        ref[...] = jnp.zeros(ref.shape, BF)
+    ahead[...] = work[:, :T]
 
     def step(t, _):
         for k in range(mt):
@@ -237,15 +249,18 @@
             @pl.when(t == k)
             def _():
                 lo, hi = k * T, (k + 1) * T
-                panel = packed[start[k] : start[k] + m - lo, :]
+                panel = ahead[lo:, :]
                 if k:
-                    panel = panel - dot3((lh[lo:, :lo], ll[lo:, :lo]), (lh[lo:hi, :lo], ll[lo:hi, :lo]), NT)
+                    last = slice(lo - T, lo)
+                    panel = panel - dot3((lh[lo:, last], ll[lo:, last]), (lh[lo:hi, last], ll[lo:hi, last]), NT)
                 d_ref[:, :T] = panel[:T]
                 d_ref[:, T:] = jnp.where(eye, 1.0, 0.0)
                 if k + 1 < mt:
-                    panel_ref[hi:, :] = panel[T:]
+                    full[hi:, lo:hi] = panel[T:]
                     full[lo:hi, hi:] = jnp.zeros((T, m - hi), F32)
 
+        cut = pl.ds(pl.multiple_of(jnp.minimum(t + 1, mt - 1) * T, T), T)
+        ahead[...] = work[:, cut] - dot3((lh[...], ll[...]), (lh[cut, :], ll[cut, :]), NT)
         factor_block(d_ref)
         for k in range(mt):
 
@@ -254,7 +269,7 @@
                 lo, hi = k * T, (k + 1) * T
                 full[lo:hi, lo:hi] = lower_of(d_ref)
                 if k + 1 < mt:
-                    below = dot3(split(panel_ref[hi:, :]), split(d_ref[:, T:]), NT)
+                    below = dot3(split(full[hi:, lo:hi]), split(d_ref[:, T:]), NT)
                     full[hi:, lo:hi] = below
                     lh[hi:, lo:hi], ll[hi:, lo:hi] = split(below)
 
@@ -271,19 +286,64 @@
 GRANT = 24 << 20
 
 
+def spans_of(m):
+    mt = m // T
+    spans = [(True, i, j, T) for j in range(0, m, T) for i in range(j + T, m, T)]
+    if mt % 2:
+        spans.append((True, m - T, m - T, T))
+    spans.append((False, 0, 0, mt // 2 * 3 * (T // 2)))
+    return spans
+
+
 def packed_rows(m, devices):
-    rows = sum(m - j * T for j in range(m // T))
+    rows = sum(span[3] for span in spans_of(m))
     unit = 8 * devices
     return -(-rows // unit) * unit
 
 
 def pieces(m, total, count):
     chunk = total // count
-    spans = [(i, j) for j in range(0, m, T) for i in range(j, m, T)]
-    cuts = sorted(set(range(0, total, chunk)) | set(range(0, len(spans) * T, T)) | {len(spans) * T, total})
-    for lo, hi in zip(cuts, cuts[1:]):
-        i, j = spans[lo // T] if lo < len(spans) * T else (None, None)
-        yield lo // chunk, lo % chunk, hi - lo, None if i is None else i + lo % T, j
+    begin = 0
+    for square, i, j, rows in spans_of(m):
+        lo = begin
+        while lo < begin + rows:
+            hi = min(begin + rows, (lo // chunk + 1) * chunk)
+            yield lo // chunk, lo % chunk, hi - lo, square, i + lo - begin, j
+            lo = hi
+        begin += rows
+    lo = begin
+    while lo < total:
+        hi = (lo // chunk + 1) * chunk
+        yield lo // chunk, lo % chunk, hi - lo, None, None, None
+        lo = hi
+
+
+def left_lanes():
+    return lax.broadcasted_iota(jnp.int32, (T // 2, T), 1) < T // 2
+
+
+def pack_diagonal(square, diagonal):
+    h, left = T // 2, left_lanes()
+    for p in range(square.shape[0] // (2 * T)):
+        a, b = [square[k : k + T, k : k + T] for k in (2 * p * T, (2 * p + 1) * T)]
+        at = 3 * h * p
+        diagonal[at : at + h, :] = jnp.where(left, a[:h], a[h:])
+        diagonal[at + h : at + 2 * h, :] = jnp.where(left, b[:h], b[h:])
+        diagonal[at + 2 * h : at + 3 * h, :] = jnp.where(left, a[h:], b[:h])
+
+
+def unpack_diagonal(square, diagonal):
+    h, left = T // 2, left_lanes()
+    for p in range(square.shape[0] // (2 * T)):
+        at = 3 * h * p
+        a, b, side = [diagonal[at + k * h : at + (k + 1) * h, :] for k in range(3)]
+        turned = jnp.concatenate([side, side], axis=0).T
+        k = 2 * p * T
+        square[k : k + h, k : k + T] = jnp.where(left, a, turned[:h])
+        square[k + h : k + T, k : k + T] = jnp.where(left, side, a)
+        k += T
+        square[k : k + h, k : k + T] = jnp.where(left, b, side)
+        square[k + h : k + T, k : k + T] = jnp.where(left, turned[h:], b)
 
 
 def scenario(place_fn, region, hess, flags, low_d, low_s, up_d, up_s, coup, pattern, first, rows, count):
@@ -306,6 +366,7 @@
             pltpu.VMEM((n, m), BF),
             pltpu.VMEM((n, m), BF),
             pltpu.VMEM((m, m), F32),
+            pltpu.VMEM((m // (2 * T) * 3 * (T // 2), T), F32),
             pltpu.SemaphoreType.DMA((2 * n // T,)),
             pltpu.SemaphoreType.DMA((n // T,)),
         ],
@@ -315,7 +376,6 @@
 
 
 def first_section(place_fn, parts, own, m, count):
-    rows = sum(part.shape[0] for part in parts)
     return pl.pallas_call(
         functools.partial(first_kernel, place_fn, count),
         out_shape=jax.ShapeDtypeStruct((own, m), F32),
@@ -327,7 +387,8 @@
             pltpu.VMEM((m, m), BF),
             pltpu.VMEM((m, m), BF),
             pltpu.VMEM((m, m), F32),
-            pltpu.VMEM((rows, T), F32),
+            pltpu.VMEM((m, m), F32),
+            pltpu.VMEM((m // (2 * T) * 3 * (T // 2), T), F32),
         ],
         compiler_params=pltpu.CompilerParams(vmem_limit_bytes=GRANT),
         name="first_section",

time: 78.3 us -> 78.5 us (level)
  Pallas kernels: 33.4 us -> 35.9 us
  waiting for transfers between devices: 25.4 us -> 23.2 us
    pallas_call x1, Pallas kernels: 17.9 us -> 20.3 us  [first_section(): pl.pallas_call(functools.partial(first_kernel, place_fn, count), out_shap...]
    ppermute x14, waiting for transfers between devices: 25.4 us -> 23.2 us  [swap(): return lax.ppermute(x, AXES, [(i, i ^ mask) for i in range(count)])]
  transfers between devices with their start and end apart: 14 -> 14, of which waited for: 10 -> 11; matrix products, arithmetic and copies ran while one was open for 0% -> 0% of each run, Pallas kernels for 0% -> 0%
where the time goes in v5:
time: 78.5 us; the launch traced here: 78.3 us
  Pallas kernels  35.9 us (46%)
  waiting for transfers between devices  23.2 us (30%)
  starting transfers between devices  17.6 us (22%)
  between operations  1.38 us (2%)
    ppermute x14, waiting for transfers between devices, swap(): return lax.ppermute(x, AXES, [(i, i ^ mask) for i in range(count)])  23.2 us
    pallas_call x1, Pallas kernels, first_section(): pl.pallas_call(functools.partial(first_kernel, place_fn, count), out_shap...  20.3 us
    ppermute x14, starting transfers between devices, swap(): return lax.ppermute(x, AXES, [(i, i ^ mask) for i in range(count)])  17.6 us
    pallas_call x1, Pallas kernels, scenario(): pl.pallas_call(functools.partial(scenario_kernel, place_fn, count), out_s...  15.6 us
  transfers between devices with their start and end apart: 14, of which 11 were waited for; matrix products, arithmetic and copies ran while one was open for 0% of the time, Pallas kernels for 0%

profile of v5, /device:TPU:0, one launch (start us, length us, event | category | flops | bytes accessed | tf_op | source)
XLA Modules:
  0.0 78.3 jit_solution(497797195349247297)
XLA Ops:
  1.3 15.6 %scenario.1 = (f32[512,512]{1,0:T(8,128)}, f32[1280,128]{1,0:T(8,128)S(1)}, f32[1280,128]{1,0:T(8,128)S(1)}) custom-call(s32[1]{0:T(128)S(6)} %copy.18.region, f32[512,512]{1,0:T(8,128)} %bitcast.4, s32[1,512]{1,0:T(1,128)} %flags.1, f32[1,512]{1,0:T(1,128)} %low_d.1, f32[1,512]{1,0:T(1,128)} %low_s.1, f32[1,512]{1,0:T(1,128)} %up_d.1, f32[1,512]{1,0:T(1,128)} %up_s.1, ...), custom_call_target="tpu_custom_call" | custom-call | tf_op jit(solution)/shard_map/scenario/pallas_call | solution.py:352
  16.8 0.5 collective-permute-start
  17.4 1.7 %collective-permute-done = f32[1280,128]{1,0:T(8,128)S(1)} collective-permute-done((f32[1280,128]{1,0:T(8,128)S(1)}, f32[1280,128]{1,0:T(8,128)S(1)}, u32[]{:S(2)}, u32[]{:S(2)}) %collective-permute-start) | collective-permute-done | bytes 655392 | tf_op jit(solution)/shard_map/ppermute | solution.py:402
  19.1 0.1 add.21
  19.2 3.9 %collective-permute-start.1 = (f32[320,128]{1,0:T(8,128)S(1)}, f32[320,128]{1,0:T(8,128)S(1)}, u32[]{:S(2)}, u32[]{:S(2)}) collective-permute-start(f32[320,128]{1,0:T(8,128)S(1)} %get-tuple-element.10), channel_id=1, source_target_pairs={{0,17},{1,16},{2,19},{3,18},{4,21},{5,20},{6,23},{7,22},{8,25},{9,... | collective-permute-start | bytes 491528 | tf_op jit(solution)/shard_map/ppermute | solution.py:402
  23.1 0.5 collective-permute-start.3
  23.6 0.1 collective-permute-start.2
  23.7 4.4 %collective-permute-done.1 = f32[320,128]{1,0:T(8,128)S(1)} collective-permute-done((f32[320,128]{1,0:T(8,128)S(1)}, f32[320,128]{1,0:T(8,128)S(1)}, u32[]{:S(2)}, u32[]{:S(2)}) %collective-permute-start.1) | collective-permute-done | bytes 163872 | tf_op jit(solution)/shard_map/ppermute | solution.py:402
  28.1 3.0 %collective-permute-done.3 = f32[320,128]{1,0:T(8,128)S(1)} collective-permute-done((f32[320,128]{1,0:T(8,128)S(1)}, f32[320,128]{1,0:T(8,128)S(1)}, u32[]{:S(2)}, u32[]{:S(2)}) %collective-permute-start.3) | collective-permute-done | bytes 163872 | tf_op jit(solution)/shard_map/ppermute | solution.py:402
  31.1 0.3 collective-permute-done.2
  31.4 0.1 fusion.1
  31.5 3.7 %collective-permute-start.4 = (f32[80,128]{1,0:T(8,128)S(1)}, f32[80,128]{1,0:T(8,128)S(1)}, u32[]{:S(2)}, u32[]{:S(2)}) collective-permute-start(f32[80,128]{1,0:T(8,128)S(1)} %get-tuple-element.13), channel_id=1, source_target_pairs={{0,6},{1,7},{2,4},{3,5},{4,2},{5,3},{6,0},{7,1},{8,14},{9,15},{10,... | collective-permute-start | bytes 122888 | tf_op jit(solution)/shard_map/ppermute | solution.py:402
  35.1 0.0 collective-permute-start.6
  35.2 0.8 %collective-permute-start.5 = (f32[80,128]{1,0:T(8,128)S(1)}, f32[80,128]{1,0:T(8,128)S(1)}, u32[]{:S(2)}, u32[]{:S(2)}) collective-permute-start(f32[80,128]{1,0:T(8,128)S(1)} %get-tuple-element.15), channel_id=1, source_target_pairs={{0,2},{1,3},{2,0},{3,1},{4,6},{5,7},{6,4},{7,5},{8,10},{9,11},{10,... | collective-permute-start | bytes 122888 | tf_op jit(solution)/shard_map/ppermute | solution.py:402
  35.9 1.5 %collective-permute-done.4 = f32[80,128]{1,0:T(8,128)S(1)} collective-permute-done((f32[80,128]{1,0:T(8,128)S(1)}, f32[80,128]{1,0:T(8,128)S(1)}, u32[]{:S(2)}, u32[]{:S(2)}) %collective-permute-start.4) | collective-permute-done | bytes 40992 | tf_op jit(solution)/shard_map/ppermute | solution.py:402
  37.4 2.6 %collective-permute-done.6 = f32[80,128]{1,0:T(8,128)S(1)} collective-permute-done((f32[80,128]{1,0:T(8,128)S(1)}, f32[80,128]{1,0:T(8,128)S(1)}, u32[]{:S(2)}, u32[]{:S(2)}) %collective-permute-start.6) | collective-permute-done | bytes 40992 | tf_op jit(solution)/shard_map/ppermute | solution.py:402
  40.0 0.0 collective-permute-done.5
  40.1 1.7 %collective-permute-start.9 = (f32[80,128]{1,0:T(8,128)S(1)}, f32[80,128]{1,0:T(8,128)S(1)}, u32[]{:S(2)}, u32[]{:S(2)}) collective-permute-start(f32[80,128]{1,0:T(8,128)S(1)} %get-tuple-element.9), channel_id=1, source_target_pairs={{0,6},{1,7},{2,4},{3,5},{4,2},{5,3},{6,0},{7,1},{8,14},{9,15},{10,... | collective-permute-start | bytes 122888 | tf_op jit(solution)/shard_map/ppermute | solution.py:402
  41.8 0.5 collective-permute-start.8
  42.2 2.3 %collective-permute-start.7 = (f32[80,128]{1,0:T(8,128)S(1)}, f32[80,128]{1,0:T(8,128)S(1)}, u32[]{:S(2)}, u32[]{:S(2)}) collective-permute-start(f32[80,128]{1,0:T(8,128)S(1)} %get-tuple-element.9), channel_id=1, source_target_pairs={{0,2},{1,3},{2,0},{3,1},{4,6},{5,7},{6,4},{7,5},{8,10},{9,11},{10,... | collective-permute-start | bytes 122888 | tf_op jit(solution)/shard_map/ppermute | solution.py:402
  44.5 1.4 %collective-permute-done.9 = f32[80,128]{1,0:T(8,128)S(1)} collective-permute-done((f32[80,128]{1,0:T(8,128)S(1)}, f32[80,128]{1,0:T(8,128)S(1)}, u32[]{:S(2)}, u32[]{:S(2)}) %collective-permute-start.9) | collective-permute-done | bytes 40992 | tf_op jit(solution)/shard_map/ppermute | solution.py:402
  45.9 0.7 collective-permute-done.8
  46.7 0.3 collective-permute-done.7
  47.0 1.7 %collective-permute-start.12 = (f32[320,128]{1,0:T(8,128)S(1)}, f32[320,128]{1,0:T(8,128)S(1)}, u32[]{:S(2)}, u32[]{:S(2)}) collective-permute-start(f32[320,128]{1,0:T(8,128)S(1)} %pad_maximum_fusion), channel_id=1, source_target_pairs={{0,17},{1,16},{2,19},{3,18},{4,21},{5,20},{6,23},{7,22},{8,25},{9,... | collective-permute-start | bytes 491528 | tf_op jit(solution)/shard_map/ppermute | solution.py:402
  48.7 1.3 %collective-permute-start.11 = (f32[320,128]{1,0:T(8,128)S(1)}, f32[320,128]{1,0:T(8,128)S(1)}, u32[]{:S(2)}, u32[]{:S(2)}) collective-permute-start(f32[320,128]{1,0:T(8,128)S(1)} %pad_maximum_fusion), channel_id=1, source_target_pairs={{0,1},{1,0},{2,3},{3,2},{4,5},{5,4},{6,7},{7,6},{8,9},{9,8},{10,11... | collective-permute-start | bytes 491528 | tf_op jit(solution)/shard_map/ppermute | solution.py:402
  50.0 0.5 collective-permute-start.10
  50.5 5.2 %collective-permute-done.10 = f32[320,128]{1,0:T(8,128)S(1)} collective-permute-done((f32[320,128]{1,0:T(8,128)S(1)}, f32[320,128]{1,0:T(8,128)S(1)}, u32[]{:S(2)}, u32[]{:S(2)}) %collective-permute-start.10) | collective-permute-done | bytes 163872 | tf_op jit(solution)/shard_map/ppermute | solution.py:402
  55.8 0.0 collective-permute-done.11
  55.8 0.0 collective-permute-done.12
  55.8 0.1 collective-permute-start.13
  55.9 2.1 %collective-permute-done.13.refs_1_ = f32[1280,128]{1,0:T(8,128)S(1)} collective-permute-done((f32[1280,128]{1,0:T(8,128)S(1)}, f32[1280,128]{1,0:T(8,128)S(1)}, u32[]{:S(2)}, u32[]{:S(2)}) %collective-permute-start.13) | collective-permute-done | bytes 655392 | tf_op jit(solution)/shard_map/ppermute | solution.py:402
  58.0 20.3 %first_section.1 = f32[96,768]{1,0:T(8,128)} custom-call(f32[1280,128]{1,0:T(8,128)S(1)} %constant_dynamic-update-slice_fusion.refs_0_, f32[1280,128]{1,0:T(8,128)S(1)} %collective-permute-done.13.refs_1_), custom_call_target="tpu_custom_call" | custom-call | tf_op jit(solution)/shard_map/first_section/pallas_call | solution.py:379
  (10 shorter events, 0.1 us)
Async XLA Ops:
  16.8 2.3 %collective-permute-start = (f32[1280,128]{1,0:T(8,128)S(1)}, f32[1280,128]{1,0:T(8,128)S(1)}, u32[]{:S(2)}, u32[]{:S(2)}) collective-permute-start(f32[1280,128]{1,0:T(8,128)S(1)} %get-tuple-element.7), channel_id=1, source_target_pairs={{0,8},{1,9},{2,10},{3,11},{4,12},{5,13},{6,14},{7,15},{8,0},{9,1},... | collective-permute-start | bytes 1966088 | tf_op jit(solution)/shard_map/ppermute | solution.py:402
  19.2 8.9 %collective-permute-start.1 = (f32[320,128]{1,0:T(8,128)S(1)}, f32[320,128]{1,0:T(8,128)S(1)}, u32[]{:S(2)}, u32[]{:S(2)}) collective-permute-start(f32[320,128]{1,0:T(8,128)S(1)} %get-tuple-element.10), channel_id=1, source_target_pairs={{0,17},{1,16},{2,19},{3,18},{4,21},{5,20},{6,23},{7,22},{8,25},{9,... | collective-permute-start | bytes 491528 | tf_op jit(solution)/shard_map/ppermute | solution.py:402
  23.1 8.0 %collective-permute-start.3 = (f32[320,128]{1,0:T(8,128)S(1)}, f32[320,128]{1,0:T(8,128)S(1)}, u32[]{:S(2)}, u32[]{:S(2)}) collective-permute-start(f32[320,128]{1,0:T(8,128)S(1)} %get-tuple-element.11), channel_id=1, source_target_pairs={{0,1},{1,0},{2,3},{3,2},{4,5},{5,4},{6,7},{7,6},{8,9},{9,8},{10,11... | collective-permute-start | bytes 491528 | tf_op jit(solution)/shard_map/ppermute | solution.py:402
  23.6 7.8 %collective-permute-start.2 = (f32[320,128]{1,0:T(8,128)S(1)}, f32[320,128]{1,0:T(8,128)S(1)}, u32[]{:S(2)}, u32[]{:S(2)}) collective-permute-start(f32[320,128]{1,0:T(8,128)S(1)} %get-tuple-element.12), channel_id=1, source_target_pairs={{0,16},{1,17},{2,18},{3,19},{4,20},{5,21},{6,22},{7,23},{8,24},{9,... | collective-permute-start | bytes 491528 | tf_op jit(solution)/shard_map/ppermute | solution.py:402
  31.5 5.9 %collective-permute-start.4 = (f32[80,128]{1,0:T(8,128)S(1)}, f32[80,128]{1,0:T(8,128)S(1)}, u32[]{:S(2)}, u32[]{:S(2)}) collective-permute-start(f32[80,128]{1,0:T(8,128)S(1)} %get-tuple-element.13), channel_id=1, source_target_pairs={{0,6},{1,7},{2,4},{3,5},{4,2},{5,3},{6,0},{7,1},{8,14},{9,15},{10,... | collective-permute-start | bytes 122888 | tf_op jit(solution)/shard_map/ppermute | solution.py:402
  35.1 4.9 %collective-permute-start.6 = (f32[80,128]{1,0:T(8,128)S(1)}, f32[80,128]{1,0:T(8,128)S(1)}, u32[]{:S(2)}, u32[]{:S(2)}) collective-permute-start(f32[80,128]{1,0:T(8,128)S(1)} %get-tuple-element.14), channel_id=1, source_target_pairs={{0,4},{1,5},{2,6},{3,7},{4,0},{5,1},{6,2},{7,3},{8,12},{9,13},{10,... | collective-permute-start | bytes 122888 | tf_op jit(solution)/shard_map/ppermute | solution.py:402
  35.2 4.9 %collective-permute-start.5 = (f32[80,128]{1,0:T(8,128)S(1)}, f32[80,128]{1,0:T(8,128)S(1)}, u32[]{:S(2)}, u32[]{:S(2)}) collective-permute-start(f32[80,128]{1,0:T(8,128)S(1)} %get-tuple-element.15), channel_id=1, source_target_pairs={{0,2},{1,3},{2,0},{3,1},{4,6},{5,7},{6,4},{7,5},{8,10},{9,11},{10,... | collective-permute-start | bytes 122888 | tf_op jit(solution)/shard_map/ppermute | solution.py:402
  40.1 5.9 %collective-permute-start.9 = (f32[80,128]{1,0:T(8,128)S(1)}, f32[80,128]{1,0:T(8,128)S(1)}, u32[]{:S(2)}, u32[]{:S(2)}) collective-permute-start(f32[80,128]{1,0:T(8,128)S(1)} %get-tuple-element.9), channel_id=1, source_target_pairs={{0,6},{1,7},{2,4},{3,5},{4,2},{5,3},{6,0},{7,1},{8,14},{9,15},{10,... | collective-permute-start | bytes 122888 | tf_op jit(solution)/shard_map/ppermute | solution.py:402
  41.8 4.9 %collective-permute-start.8 = (f32[80,128]{1,0:T(8,128)S(1)}, f32[80,128]{1,0:T(8,128)S(1)}, u32[]{:S(2)}, u32[]{:S(2)}) collective-permute-start(f32[80,128]{1,0:T(8,128)S(1)} %get-tuple-element.9), channel_id=1, source_target_pairs={{0,4},{1,5},{2,6},{3,7},{4,0},{5,1},{6,2},{7,3},{8,12},{9,13},{10,... | collective-permute-start | bytes 122888 | tf_op jit(solution)/shard_map/ppermute | solution.py:402
  42.2 4.7 %collective-permute-start.7 = (f32[80,128]{1,0:T(8,128)S(1)}, f32[80,128]{1,0:T(8,128)S(1)}, u32[]{:S(2)}, u32[]{:S(2)}) collective-permute-start(f32[80,128]{1,0:T(8,128)S(1)} %get-tuple-element.9), channel_id=1, source_target_pairs={{0,2},{1,3},{2,0},{3,1},{4,6},{5,7},{6,4},{7,5},{8,10},{9,11},{10,... | collective-permute-start | bytes 122888 | tf_op jit(solution)/shard_map/ppermute | solution.py:402
  47.0 8.8 %collective-permute-start.12 = (f32[320,128]{1,0:T(8,128)S(1)}, f32[320,128]{1,0:T(8,128)S(1)}, u32[]{:S(2)}, u32[]{:S(2)}) collective-permute-start(f32[320,128]{1,0:T(8,128)S(1)} %pad_maximum_fusion), channel_id=1, source_target_pairs={{0,17},{1,16},{2,19},{3,18},{4,21},{5,20},{6,23},{7,22},{8,25},{9,... | collective-permute-start | bytes 491528 | tf_op jit(solution)/shard_map/ppermute | solution.py:402
  48.7 7.1 %collective-permute-start.11 = (f32[320,128]{1,0:T(8,128)S(1)}, f32[320,128]{1,0:T(8,128)S(1)}, u32[]{:S(2)}, u32[]{:S(2)}) collective-permute-start(f32[320,128]{1,0:T(8,128)S(1)} %pad_maximum_fusion), channel_id=1, source_target_pairs={{0,1},{1,0},{2,3},{3,2},{4,5},{5,4},{6,7},{7,6},{8,9},{9,8},{10,11... | collective-permute-start | bytes 491528 | tf_op jit(solution)/shard_map/ppermute | solution.py:402
  50.0 5.8 %collective-permute-start.10 = (f32[320,128]{1,0:T(8,128)S(1)}, f32[320,128]{1,0:T(8,128)S(1)}, u32[]{:S(2)}, u32[]{:S(2)}) collective-permute-start(f32[320,128]{1,0:T(8,128)S(1)} %pad_maximum_fusion), channel_id=1, source_target_pairs={{0,16},{1,17},{2,18},{3,19},{4,20},{5,21},{6,22},{7,23},{8,24},{9,... | collective-permute-start | bytes 491528 | tf_op jit(solution)/shard_map/ppermute | solution.py:402
  55.8 2.2 %collective-permute-start.13 = (f32[1280,128]{1,0:T(8,128)S(1)}, f32[1280,128]{1,0:T(8,128)S(1)}, u32[]{:S(2)}, u32[]{:S(2)}) collective-permute-start(f32[1280,128]{1,0:T(8,128)S(1)} %constant_dynamic-update-slice_fusion.refs_0_), channel_id=1, source_target_pairs={{0,8},{1,9},{2,10},{3,11},{4,12},{5,13},{6,14},{7,15},{8,0},{9,1},... | collective-permute-start | bytes 1966088 | tf_op jit(solution)/shard_map/ppermute | solution.py:402

commit v6 on v5

--- a/solution.py
+++ b/solution.py
@@ -221,7 +221,7 @@
 
 def first_kernel(place_fn, count, *refs):
     _, wide, place = place_fn()
-    parts, (out, d_ref, ahead, lh, ll, full, work, diagonal) = refs[:-8], refs[-8:]
+    parts, (out, d_ref, lh, ll, full, work, diagonal) = refs[:-7], refs[-7:]
     m = full.shape[0]
     mt = m // T
     r, c = unit_block()
@@ -239,9 +239,6 @@
                     target[i : i + rows, j : j + T] = parts[(l // half) ^ side][pl.ds(begin, rows), :]
 
     unpack_diagonal(work, diagonal)
-    for ref in (lh, ll):
-        ref[...] = jnp.zeros(ref.shape, BF)
-    ahead[...] = work[:, :T]
 
     def step(t, _):
         for k in range(mt):
@@ -249,18 +246,15 @@
             @pl.when(t == k)
             def _():
                 lo, hi = k * T, (k + 1) * T
-                panel = ahead[lo:, :]
+                panel = work[lo:, lo:hi]
                 if k:
-                    last = slice(lo - T, lo)
-                    panel = panel - dot3((lh[lo:, last], ll[lo:, last]), (lh[lo:hi, last], ll[lo:hi, last]), NT)
+                    panel = panel - dot3((lh[lo:, :lo], ll[lo:, :lo]), (lh[lo:hi, :lo], ll[lo:hi, :lo]), NT)
                 d_ref[:, :T] = panel[:T]
                 d_ref[:, T:] = jnp.where(eye, 1.0, 0.0)
                 if k + 1 < mt:
                     full[hi:, lo:hi] = panel[T:]
                     full[lo:hi, hi:] = jnp.zeros((T, m - hi), F32)
 
-        cut = pl.ds(pl.multiple_of(jnp.minimum(t + 1, mt - 1) * T, T), T)
-        ahead[...] = work[:, cut] - dot3((lh[...], ll[...]), (lh[cut, :], ll[cut, :]), NT)
         factor_block(d_ref)
         for k in range(mt):
 
@@ -383,7 +377,6 @@
         out_specs=VMEM,
         scratch_shapes=[
             pltpu.VMEM((T, 2 * T), F32),
-            pltpu.VMEM((m, T), F32),
             pltpu.VMEM((m, m), BF),
             pltpu.VMEM((m, m), BF),
             pltpu.VMEM((m, m), F32),

time: 78.5 us -> 76.2 us (0.971)
  Pallas kernels: 35.9 us -> 33.6 us
    pallas_call x1, Pallas kernels: 20.3 us -> 18 us  [first_section(): pl.pallas_call(functools.partial(first_kernel, place_fn, count), out_shap...]
where the time goes in v6:
time: 76.2 us; the launch traced here: 76 us
  Pallas kernels  33.6 us (44%)
  waiting for transfers between devices  23.2 us (30%)
  starting transfers between devices  17.6 us (23%)
  between operations  1.38 us (2%)
    ppermute x14, waiting for transfers between devices, swap(): return lax.ppermute(x, AXES, [(i, i ^ mask) for i in range(count)])  23.2 us
    pallas_call x1, Pallas kernels, first_section(): pl.pallas_call(functools.partial(first_kernel, place_fn, count), out_shap...  18 us
    ppermute x14, starting transfers between devices, swap(): return lax.ppermute(x, AXES, [(i, i ^ mask) for i in range(count)])  17.6 us
    pallas_call x1, Pallas kernels, scenario(): pl.pallas_call(functools.partial(scenario_kernel, place_fn, count), out_s...  15.6 us
  transfers between devices with their start and end apart: 14, of which 11 were waited for; matrix products, arithmetic and copies ran while one was open for 0% of the time, Pallas kernels for 0%

profile of v6, /device:TPU:0, one launch (start us, length us, event | category | flops | bytes accessed | tf_op | source)
XLA Modules:
  0.0 76.0 jit_solution(11728361941957933708)
XLA Ops:
  1.3 15.6 %scenario.1 = (f32[512,512]{1,0:T(8,128)}, f32[1280,128]{1,0:T(8,128)S(1)}, f32[1280,128]{1,0:T(8,128)S(1)}) custom-call(s32[1]{0:T(128)S(6)} %copy.18.region, f32[512,512]{1,0:T(8,128)} %bitcast.4, s32[1,512]{1,0:T(1,128)} %flags.1, f32[1,512]{1,0:T(1,128)} %low_d.1, f32[1,512]{1,0:T(1,128)} %low_s.1, f32[1,512]{1,0:T(1,128)} %up_d.1, f32[1,512]{1,0:T(1,128)} %up_s.1, ...), custom_call_target="tpu_custom_call" | custom-call | tf_op jit(solution)/shard_map/scenario/pallas_call | solution.py:346
  16.8 0.5 collective-permute-start
  17.4 1.7 %collective-permute-done = f32[1280,128]{1,0:T(8,128)S(1)} collective-permute-done((f32[1280,128]{1,0:T(8,128)S(1)}, f32[1280,128]{1,0:T(8,128)S(1)}, u32[]{:S(2)}, u32[]{:S(2)}) %collective-permute-start) | collective-permute-done | bytes 655392 | tf_op jit(solution)/shard_map/ppermute | solution.py:395
  19.1 0.1 add.21
  19.2 3.9 %collective-permute-start.1 = (f32[320,128]{1,0:T(8,128)S(1)}, f32[320,128]{1,0:T(8,128)S(1)}, u32[]{:S(2)}, u32[]{:S(2)}) collective-permute-start(f32[320,128]{1,0:T(8,128)S(1)} %get-tuple-element.10), channel_id=1, source_target_pairs={{0,17},{1,16},{2,19},{3,18},{4,21},{5,20},{6,23},{7,22},{8,25},{9,... | collective-permute-start | bytes 491528 | tf_op jit(solution)/shard_map/ppermute | solution.py:395
  23.1 0.5 collective-permute-start.3
  23.6 0.1 collective-permute-start.2
  23.7 4.4 %collective-permute-done.1 = f32[320,128]{1,0:T(8,128)S(1)} collective-permute-done((f32[320,128]{1,0:T(8,128)S(1)}, f32[320,128]{1,0:T(8,128)S(1)}, u32[]{:S(2)}, u32[]{:S(2)}) %collective-permute-start.1) | collective-permute-done | bytes 163872 | tf_op jit(solution)/shard_map/ppermute | solution.py:395
  28.1 3.0 %collective-permute-done.3 = f32[320,128]{1,0:T(8,128)S(1)} collective-permute-done((f32[320,128]{1,0:T(8,128)S(1)}, f32[320,128]{1,0:T(8,128)S(1)}, u32[]{:S(2)}, u32[]{:S(2)}) %collective-permute-start.3) | collective-permute-done | bytes 163872 | tf_op jit(solution)/shard_map/ppermute | solution.py:395
  31.1 0.3 collective-permute-done.2
  31.4 0.1 fusion.1
  31.5 3.7 %collective-permute-start.4 = (f32[80,128]{1,0:T(8,128)S(1)}, f32[80,128]{1,0:T(8,128)S(1)}, u32[]{:S(2)}, u32[]{:S(2)}) collective-permute-start(f32[80,128]{1,0:T(8,128)S(1)} %get-tuple-element.13), channel_id=1, source_target_pairs={{0,6},{1,7},{2,4},{3,5},{4,2},{5,3},{6,0},{7,1},{8,14},{9,15},{10,... | collective-permute-start | bytes 122888 | tf_op jit(solution)/shard_map/ppermute | solution.py:395
  35.1 0.0 collective-permute-start.6
  35.2 0.8 %collective-permute-start.5 = (f32[80,128]{1,0:T(8,128)S(1)}, f32[80,128]{1,0:T(8,128)S(1)}, u32[]{:S(2)}, u32[]{:S(2)}) collective-permute-start(f32[80,128]{1,0:T(8,128)S(1)} %get-tuple-element.15), channel_id=1, source_target_pairs={{0,2},{1,3},{2,0},{3,1},{4,6},{5,7},{6,4},{7,5},{8,10},{9,11},{10,... | collective-permute-start | bytes 122888 | tf_op jit(solution)/shard_map/ppermute | solution.py:395
  35.9 1.5 %collective-permute-done.4 = f32[80,128]{1,0:T(8,128)S(1)} collective-permute-done((f32[80,128]{1,0:T(8,128)S(1)}, f32[80,128]{1,0:T(8,128)S(1)}, u32[]{:S(2)}, u32[]{:S(2)}) %collective-permute-start.4) | collective-permute-done | bytes 40992 | tf_op jit(solution)/shard_map/ppermute | solution.py:395
  37.4 2.6 %collective-permute-done.6 = f32[80,128]{1,0:T(8,128)S(1)} collective-permute-done((f32[80,128]{1,0:T(8,128)S(1)}, f32[80,128]{1,0:T(8,128)S(1)}, u32[]{:S(2)}, u32[]{:S(2)}) %collective-permute-start.6) | collective-permute-done | bytes 40992 | tf_op jit(solution)/shard_map/ppermute | solution.py:395
  40.0 0.0 collective-permute-done.5
  40.1 1.7 %collective-permute-start.9 = (f32[80,128]{1,0:T(8,128)S(1)}, f32[80,128]{1,0:T(8,128)S(1)}, u32[]{:S(2)}, u32[]{:S(2)}) collective-permute-start(f32[80,128]{1,0:T(8,128)S(1)} %get-tuple-element.9), channel_id=1, source_target_pairs={{0,6},{1,7},{2,4},{3,5},{4,2},{5,3},{6,0},{7,1},{8,14},{9,15},{10,... | collective-permute-start | bytes 122888 | tf_op jit(solution)/shard_map/ppermute | solution.py:395
  41.8 0.5 collective-permute-start.8
  42.2 2.3 %collective-permute-start.7 = (f32[80,128]{1,0:T(8,128)S(1)}, f32[80,128]{1,0:T(8,128)S(1)}, u32[]{:S(2)}, u32[]{:S(2)}) collective-permute-start(f32[80,128]{1,0:T(8,128)S(1)} %get-tuple-element.9), channel_id=1, source_target_pairs={{0,2},{1,3},{2,0},{3,1},{4,6},{5,7},{6,4},{7,5},{8,10},{9,11},{10,... | collective-permute-start | bytes 122888 | tf_op jit(solution)/shard_map/ppermute | solution.py:395
  44.5 1.4 %collective-permute-done.9 = f32[80,128]{1,0:T(8,128)S(1)} collective-permute-done((f32[80,128]{1,0:T(8,128)S(1)}, f32[80,128]{1,0:T(8,128)S(1)}, u32[]{:S(2)}, u32[]{:S(2)}) %collective-permute-start.9) | collective-permute-done | bytes 40992 | tf_op jit(solution)/shard_map/ppermute | solution.py:395
  45.9 0.7 collective-permute-done.8
  46.7 0.3 collective-permute-done.7
  47.0 1.7 %collective-permute-start.12 = (f32[320,128]{1,0:T(8,128)S(1)}, f32[320,128]{1,0:T(8,128)S(1)}, u32[]{:S(2)}, u32[]{:S(2)}) collective-permute-start(f32[320,128]{1,0:T(8,128)S(1)} %pad_maximum_fusion), channel_id=1, source_target_pairs={{0,17},{1,16},{2,19},{3,18},{4,21},{5,20},{6,23},{7,22},{8,25},{9,... | collective-permute-start | bytes 491528 | tf_op jit(solution)/shard_map/ppermute | solution.py:395
  48.7 1.3 %collective-permute-start.11 = (f32[320,128]{1,0:T(8,128)S(1)}, f32[320,128]{1,0:T(8,128)S(1)}, u32[]{:S(2)}, u32[]{:S(2)}) collective-permute-start(f32[320,128]{1,0:T(8,128)S(1)} %pad_maximum_fusion), channel_id=1, source_target_pairs={{0,1},{1,0},{2,3},{3,2},{4,5},{5,4},{6,7},{7,6},{8,9},{9,8},{10,11... | collective-permute-start | bytes 491528 | tf_op jit(solution)/shard_map/ppermute | solution.py:395
  50.0 0.5 collective-permute-start.10
  50.5 5.2 %collective-permute-done.10 = f32[320,128]{1,0:T(8,128)S(1)} collective-permute-done((f32[320,128]{1,0:T(8,128)S(1)}, f32[320,128]{1,0:T(8,128)S(1)}, u32[]{:S(2)}, u32[]{:S(2)}) %collective-permute-start.10) | collective-permute-done | bytes 163872 | tf_op jit(solution)/shard_map/ppermute | solution.py:395
  55.8 0.0 collective-permute-done.11
  55.8 0.0 collective-permute-done.12
  55.8 0.1 collective-permute-start.13
  55.9 2.1 %collective-permute-done.13.refs_1_ = f32[1280,128]{1,0:T(8,128)S(1)} collective-permute-done((f32[1280,128]{1,0:T(8,128)S(1)}, f32[1280,128]{1,0:T(8,128)S(1)}, u32[]{:S(2)}, u32[]{:S(2)}) %collective-permute-start.13) | collective-permute-done | bytes 655392 | tf_op jit(solution)/shard_map/ppermute | solution.py:395
  58.0 18.0 %first_section.1 = f32[96,768]{1,0:T(8,128)} custom-call(f32[1280,128]{1,0:T(8,128)S(1)} %constant_dynamic-update-slice_fusion.refs_0_, f32[1280,128]{1,0:T(8,128)S(1)} %collective-permute-done.13.refs_1_), custom_call_target="tpu_custom_call" | custom-call | tf_op jit(solution)/shard_map/first_section/pallas_call | solution.py:373
  (10 shorter events, 0.1 us)
Async XLA Ops:
  16.8 2.3 %collective-permute-start = (f32[1280,128]{1,0:T(8,128)S(1)}, f32[1280,128]{1,0:T(8,128)S(1)}, u32[]{:S(2)}, u32[]{:S(2)}) collective-permute-start(f32[1280,128]{1,0:T(8,128)S(1)} %get-tuple-element.7), channel_id=1, source_target_pairs={{0,8},{1,9},{2,10},{3,11},{4,12},{5,13},{6,14},{7,15},{8,0},{9,1},... | collective-permute-start | bytes 1966088 | tf_op jit(solution)/shard_map/ppermute | solution.py:395
  19.2 8.9 %collective-permute-start.1 = (f32[320,128]{1,0:T(8,128)S(1)}, f32[320,128]{1,0:T(8,128)S(1)}, u32[]{:S(2)}, u32[]{:S(2)}) collective-permute-start(f32[320,128]{1,0:T(8,128)S(1)} %get-tuple-element.10), channel_id=1, source_target_pairs={{0,17},{1,16},{2,19},{3,18},{4,21},{5,20},{6,23},{7,22},{8,25},{9,... | collective-permute-start | bytes 491528 | tf_op jit(solution)/shard_map/ppermute | solution.py:395
  23.1 8.0 %collective-permute-start.3 = (f32[320,128]{1,0:T(8,128)S(1)}, f32[320,128]{1,0:T(8,128)S(1)}, u32[]{:S(2)}, u32[]{:S(2)}) collective-permute-start(f32[320,128]{1,0:T(8,128)S(1)} %get-tuple-element.11), channel_id=1, source_target_pairs={{0,1},{1,0},{2,3},{3,2},{4,5},{5,4},{6,7},{7,6},{8,9},{9,8},{10,11... | collective-permute-start | bytes 491528 | tf_op jit(solution)/shard_map/ppermute | solution.py:395
  23.6 7.8 %collective-permute-start.2 = (f32[320,128]{1,0:T(8,128)S(1)}, f32[320,128]{1,0:T(8,128)S(1)}, u32[]{:S(2)}, u32[]{:S(2)}) collective-permute-start(f32[320,128]{1,0:T(8,128)S(1)} %get-tuple-element.12), channel_id=1, source_target_pairs={{0,16},{1,17},{2,18},{3,19},{4,20},{5,21},{6,22},{7,23},{8,24},{9,... | collective-permute-start | bytes 491528 | tf_op jit(solution)/shard_map/ppermute | solution.py:395
  31.5 5.9 %collective-permute-start.4 = (f32[80,128]{1,0:T(8,128)S(1)}, f32[80,128]{1,0:T(8,128)S(1)}, u32[]{:S(2)}, u32[]{:S(2)}) collective-permute-start(f32[80,128]{1,0:T(8,128)S(1)} %get-tuple-element.13), channel_id=1, source_target_pairs={{0,6},{1,7},{2,4},{3,5},{4,2},{5,3},{6,0},{7,1},{8,14},{9,15},{10,... | collective-permute-start | bytes 122888 | tf_op jit(solution)/shard_map/ppermute | solution.py:395
  35.1 4.9 %collective-permute-start.6 = (f32[80,128]{1,0:T(8,128)S(1)}, f32[80,128]{1,0:T(8,128)S(1)}, u32[]{:S(2)}, u32[]{:S(2)}) collective-permute-start(f32[80,128]{1,0:T(8,128)S(1)} %get-tuple-element.14), channel_id=1, source_target_pairs={{0,4},{1,5},{2,6},{3,7},{4,0},{5,1},{6,2},{7,3},{8,12},{9,13},{10,... | collective-permute-start | bytes 122888 | tf_op jit(solution)/shard_map/ppermute | solution.py:395
  35.2 4.9 %collective-permute-start.5 = (f32[80,128]{1,0:T(8,128)S(1)}, f32[80,128]{1,0:T(8,128)S(1)}, u32[]{:S(2)}, u32[]{:S(2)}) collective-permute-start(f32[80,128]{1,0:T(8,128)S(1)} %get-tuple-element.15), channel_id=1, source_target_pairs={{0,2},{1,3},{2,0},{3,1},{4,6},{5,7},{6,4},{7,5},{8,10},{9,11},{10,... | collective-permute-start | bytes 122888 | tf_op jit(solution)/shard_map/ppermute | solution.py:395
  40.1 5.9 %collective-permute-start.9 = (f32[80,128]{1,0:T(8,128)S(1)}, f32[80,128]{1,0:T(8,128)S(1)}, u32[]{:S(2)}, u32[]{:S(2)}) collective-permute-start(f32[80,128]{1,0:T(8,128)S(1)} %get-tuple-element.9), channel_id=1, source_target_pairs={{0,6},{1,7},{2,4},{3,5},{4,2},{5,3},{6,0},{7,1},{8,14},{9,15},{10,... | collective-permute-start | bytes 122888 | tf_op jit(solution)/shard_map/ppermute | solution.py:395
  41.8 4.9 %collective-permute-start.8 = (f32[80,128]{1,0:T(8,128)S(1)}, f32[80,128]{1,0:T(8,128)S(1)}, u32[]{:S(2)}, u32[]{:S(2)}) collective-permute-start(f32[80,128]{1,0:T(8,128)S(1)} %get-tuple-element.9), channel_id=1, source_target_pairs={{0,4},{1,5},{2,6},{3,7},{4,0},{5,1},{6,2},{7,3},{8,12},{9,13},{10,... | collective-permute-start | bytes 122888 | tf_op jit(solution)/shard_map/ppermute | solution.py:395
  42.2 4.7 %collective-permute-start.7 = (f32[80,128]{1,0:T(8,128)S(1)}, f32[80,128]{1,0:T(8,128)S(1)}, u32[]{:S(2)}, u32[]{:S(2)}) collective-permute-start(f32[80,128]{1,0:T(8,128)S(1)} %get-tuple-element.9), channel_id=1, source_target_pairs={{0,2},{1,3},{2,0},{3,1},{4,6},{5,7},{6,4},{7,5},{8,10},{9,11},{10,... | collective-permute-start | bytes 122888 | tf_op jit(solution)/shard_map/ppermute | solution.py:395
  47.0 8.8 %collective-permute-start.12 = (f32[320,128]{1,0:T(8,128)S(1)}, f32[320,128]{1,0:T(8,128)S(1)}, u32[]{:S(2)}, u32[]{:S(2)}) collective-permute-start(f32[320,128]{1,0:T(8,128)S(1)} %pad_maximum_fusion), channel_id=1, source_target_pairs={{0,17},{1,16},{2,19},{3,18},{4,21},{5,20},{6,23},{7,22},{8,25},{9,... | collective-permute-start | bytes 491528 | tf_op jit(solution)/shard_map/ppermute | solution.py:395
  48.7 7.1 %collective-permute-start.11 = (f32[320,128]{1,0:T(8,128)S(1)}, f32[320,128]{1,0:T(8,128)S(1)}, u32[]{:S(2)}, u32[]{:S(2)}) collective-permute-start(f32[320,128]{1,0:T(8,128)S(1)} %pad_maximum_fusion), channel_id=1, source_target_pairs={{0,1},{1,0},{2,3},{3,2},{4,5},{5,4},{6,7},{7,6},{8,9},{9,8},{10,11... | collective-permute-start | bytes 491528 | tf_op jit(solution)/shard_map/ppermute | solution.py:395
  50.0 5.8 %collective-permute-start.10 = (f32[320,128]{1,0:T(8,128)S(1)}, f32[320,128]{1,0:T(8,128)S(1)}, u32[]{:S(2)}, u32[]{:S(2)}) collective-permute-start(f32[320,128]{1,0:T(8,128)S(1)} %pad_maximum_fusion), channel_id=1, source_target_pairs={{0,16},{1,17},{2,18},{3,19},{4,20},{5,21},{6,22},{7,23},{8,24},{9,... | collective-permute-start | bytes 491528 | tf_op jit(solution)/shard_map/ppermute | solution.py:395
  55.8 2.2 %collective-permute-start.13 = (f32[1280,128]{1,0:T(8,128)S(1)}, f32[1280,128]{1,0:T(8,128)S(1)}, u32[]{:S(2)}, u32[]{:S(2)}) collective-permute-start(f32[1280,128]{1,0:T(8,128)S(1)} %constant_dynamic-update-slice_fusion.refs_0_), channel_id=1, source_target_pairs={{0,8},{1,9},{2,10},{3,11},{4,12},{5,13},{6,14},{7,15},{8,0},{9,1},... | collective-permute-start | bytes 1966088 | tf_op jit(solution)/shard_map/ppermute | solution.py:395

commit v7 on v6

--- a/solution.py
+++ b/solution.py
@@ -84,7 +84,7 @@
         out.append(jnp.concatenate([w * scale for w in v[g]], axis=1))
         for h in range(g + 2, n):
             for k in (g + 1, g + 2):
-                if k <= h and (h, k) not in block:
+                if k <= h and (h, k) not in block and (k == g + 1 or h == k):
                     fetch(h, k)
     return out
 
@@ -226,17 +226,17 @@
     mt = m // T
     r, c = unit_block()
     eye = r == c
-    half = count // 2
-    chunk = parts[0].shape[0] // half
-    for side in range(2):
-
-        @pl.when(place // half == side)
+    each = count // len(parts)
+    chunk = parts[0].shape[0] // each
+    for top in range(len(parts)):
+
+        @pl.when(place // each == top)
         def _():
             for l, at, rows, square, i, j in pieces(m, count * chunk, count):
                 if square is not None:
-                    begin = pl.multiple_of(((l ^ place) % half) * chunk, 8) + at
+                    begin = pl.multiple_of(((l ^ place) % each) * chunk, 8) + at
                     target = work if square else diagonal
-                    target[i : i + rows, j : j + T] = parts[(l // half) ^ side][pl.ds(begin, rows), :]
+                    target[i : i + rows, j : j + T] = parts[(l // each) ^ top][pl.ds(begin, rows), :]
 
     unpack_diagonal(work, diagonal)
 
@@ -423,10 +423,10 @@
         got = [swap(cut[k], masks[k], count) for k in farthest_first(len(masks))]
         x = functools.reduce(jnp.add, got, cut[0])
     parts = [x]
-    for bits in reversed(rounds):
+    for bits in reversed(rounds[1:]):
         x = parts[0] if len(parts) == 1 else jnp.concatenate(parts)
         parts = [x] + [swap(x, mask, count) for mask in masks_of(bits)[1:]]
-    return parts
+    return parts + [swap(part, masks_of(rounds[0])[1], count) for part in parts]
 
 
 def solution(mesh):

time: 76.2 us -> 75.1 us (0.986)
  waiting for transfers between devices: 23.2 us -> 22.3 us
    ppermute x14 -> x17, waiting for transfers between devices: 23.2 us -> 22.3 us  [swap(): return lax.ppermute(x, AXES, [(i, i ^ mask) for i in range(count)])]
    ppermute x14 -> x17, starting transfers between devices: 17.6 us -> 17.9 us  [swap(): return lax.ppermute(x, AXES, [(i, i ^ mask) for i in range(count)])]
  transfers between devices with their start and end apart: 14 -> 17, of which waited for: 11 -> 14; matrix products, arithmetic and copies ran while one was open for 0% -> 0% of each run, Pallas kernels for 0% -> 0%
where the time goes in v7:
time: 75.1 us; the launch traced here: 74.9 us
  Pallas kernels  33.2 us (44%)
  waiting for transfers between devices  22.3 us (30%)
  starting transfers between devices  17.9 us (24%)
  between operations  1.33 us (2%)
    ppermute x17, waiting for transfers between devices, swap(): return lax.ppermute(x, AXES, [(i, i ^ mask) for i in range(count)])  22.3 us
    ppermute x17, starting transfers between devices, swap(): return lax.ppermute(x, AXES, [(i, i ^ mask) for i in range(count)])  17.9 us
    pallas_call x1, Pallas kernels, first_section(): pl.pallas_call(functools.partial(first_kernel, place_fn, count), out_shap...  17.8 us
    pallas_call x1, Pallas kernels, scenario(): pl.pallas_call(functools.partial(scenario_kernel, place_fn, count), out_s...  15.4 us
  transfers between devices with their start and end apart: 17, of which 14 were waited for; matrix products, arithmetic and copies ran while one was open for 0% of the time, Pallas kernels for 0%

profile of v7, /device:TPU:0, one launch (start us, length us, event | category | flops | bytes accessed | tf_op | source)
XLA Modules:
  0.0 74.9 jit_solution(12317391170918762251)
XLA Ops:
  1.3 15.4 %scenario.1 = (f32[512,512]{1,0:T(8,128)}, f32[1280,128]{1,0:T(8,128)S(1)}, f32[1280,128]{1,0:T(8,128)S(1)}) custom-call(s32[1]{0:T(128)S(6)} %copy.12.region, f32[512,512]{1,0:T(8,128)} %bitcast.4, s32[1,512]{1,0:T(1,128)} %flags.1, f32[1,512]{1,0:T(1,128)} %low_d.1, f32[1,512]{1,0:T(1,128)} %low_s.1, f32[1,512]{1,0:T(1,128)} %up_d.1, f32[1,512]{1,0:T(1,128)} %up_s.1, ...), custom_call_target="tpu_custom_call" | custom-call | tf_op jit(solution)/shard_map/scenario/pallas_call | solution.py:346
  16.7 0.5 collective-permute-start
  17.2 1.7 %collective-permute-done = f32[1280,128]{1,0:T(8,128)S(1)} collective-permute-done((f32[1280,128]{1,0:T(8,128)S(1)}, f32[1280,128]{1,0:T(8,128)S(1)}, u32[]{:S(2)}, u32[]{:S(2)}) %collective-permute-start) | collective-permute-done | bytes 655392 | tf_op jit(solution)/shard_map/ppermute | solution.py:395
  19.0 0.1 add.21
  19.1 3.9 %collective-permute-start.1 = (f32[320,128]{1,0:T(8,128)S(1)}, f32[320,128]{1,0:T(8,128)S(1)}, u32[]{:S(2)}, u32[]{:S(2)}) collective-permute-start(f32[320,128]{1,0:T(8,128)S(1)} %get-tuple-element.8), channel_id=1, source_target_pairs={{0,17},{1,16},{2,19},{3,18},{4,21},{5,20},{6,23},{7,22},{8,25},{9,... | collective-permute-start | bytes 491528 | tf_op jit(solution)/shard_map/ppermute | solution.py:395
  22.9 0.5 collective-permute-start.3
  23.4 0.1 collective-permute-start.2
  23.6 4.4 %collective-permute-done.1 = f32[320,128]{1,0:T(8,128)S(1)} collective-permute-done((f32[320,128]{1,0:T(8,128)S(1)}, f32[320,128]{1,0:T(8,128)S(1)}, u32[]{:S(2)}, u32[]{:S(2)}) %collective-permute-start.1) | collective-permute-done | bytes 163872 | tf_op jit(solution)/shard_map/ppermute | solution.py:395
  28.0 3.0 %collective-permute-done.3 = f32[320,128]{1,0:T(8,128)S(1)} collective-permute-done((f32[320,128]{1,0:T(8,128)S(1)}, f32[320,128]{1,0:T(8,128)S(1)}, u32[]{:S(2)}, u32[]{:S(2)}) %collective-permute-start.3) | collective-permute-done | bytes 163872 | tf_op jit(solution)/shard_map/ppermute | solution.py:395
  31.0 0.3 collective-permute-done.2
  31.3 0.1 fusion.1
  31.3 3.7 %collective-permute-start.4 = (f32[80,128]{1,0:T(8,128)S(1)}, f32[80,128]{1,0:T(8,128)S(1)}, u32[]{:S(2)}, u32[]{:S(2)}) collective-permute-start(f32[80,128]{1,0:T(8,128)S(1)} %get-tuple-element.11), channel_id=1, source_target_pairs={{0,6},{1,7},{2,4},{3,5},{4,2},{5,3},{6,0},{7,1},{8,14},{9,15},{10,... | collective-permute-start | bytes 122888 | tf_op jit(solution)/shard_map/ppermute | solution.py:395
  35.0 0.0 collective-permute-start.6
  35.0 0.8 %collective-permute-start.5 = (f32[80,128]{1,0:T(8,128)S(1)}, f32[80,128]{1,0:T(8,128)S(1)}, u32[]{:S(2)}, u32[]{:S(2)}) collective-permute-start(f32[80,128]{1,0:T(8,128)S(1)} %get-tuple-element.13), channel_id=1, source_target_pairs={{0,2},{1,3},{2,0},{3,1},{4,6},{5,7},{6,4},{7,5},{8,10},{9,11},{10,... | collective-permute-start | bytes 122888 | tf_op jit(solution)/shard_map/ppermute | solution.py:395
  35.8 1.5 %collective-permute-done.4 = f32[80,128]{1,0:T(8,128)S(1)} collective-permute-done((f32[80,128]{1,0:T(8,128)S(1)}, f32[80,128]{1,0:T(8,128)S(1)}, u32[]{:S(2)}, u32[]{:S(2)}) %collective-permute-start.4) | collective-permute-done | bytes 40992 | tf_op jit(solution)/shard_map/ppermute | solution.py:395
  37.3 2.6 %collective-permute-done.6 = f32[80,128]{1,0:T(8,128)S(1)} collective-permute-done((f32[80,128]{1,0:T(8,128)S(1)}, f32[80,128]{1,0:T(8,128)S(1)}, u32[]{:S(2)}, u32[]{:S(2)}) %collective-permute-start.6) | collective-permute-done | bytes 40992 | tf_op jit(solution)/shard_map/ppermute | solution.py:395
  39.9 0.0 collective-permute-done.5
  39.9 1.7 %collective-permute-start.9 = (f32[80,128]{1,0:T(8,128)S(1)}, f32[80,128]{1,0:T(8,128)S(1)}, u32[]{:S(2)}, u32[]{:S(2)}) collective-permute-start(f32[80,128]{1,0:T(8,128)S(1)} %fusion.3), channel_id=1, source_target_pairs={{0,6},{1,7},{2,4},{3,5},{4,2},{5,3},{6,0},{7,1},{8,14},{9,15},{10,... | collective-permute-start | bytes 122888 | tf_op jit(solution)/shard_map/ppermute | solution.py:395
  41.6 0.5 collective-permute-start.8
  42.1 2.3 %collective-permute-start.7 = (f32[80,128]{1,0:T(8,128)S(1)}, f32[80,128]{1,0:T(8,128)S(1)}, u32[]{:S(2)}, u32[]{:S(2)}) collective-permute-start(f32[80,128]{1,0:T(8,128)S(1)} %fusion.3), channel_id=1, source_target_pairs={{0,2},{1,3},{2,0},{3,1},{4,6},{5,7},{6,4},{7,5},{8,10},{9,11},{10,... | collective-permute-start | bytes 122888 | tf_op jit(solution)/shard_map/ppermute | solution.py:395
  44.4 1.4 %collective-permute-done.9 = f32[80,128]{1,0:T(8,128)S(1)} collective-permute-done((f32[80,128]{1,0:T(8,128)S(1)}, f32[80,128]{1,0:T(8,128)S(1)}, u32[]{:S(2)}, u32[]{:S(2)}) %collective-permute-start.9) | collective-permute-done | bytes 40992 | tf_op jit(solution)/shard_map/ppermute | solution.py:395
  45.8 0.7 collective-permute-done.8
  46.5 0.3 collective-permute-done.7
  46.8 1.7 %collective-permute-start.12 = (f32[320,128]{1,0:T(8,128)S(1)}, f32[320,128]{1,0:T(8,128)S(1)}, u32[]{:S(2)}, u32[]{:S(2)}) collective-permute-start(f32[320,128]{1,0:T(8,128)S(1)} %pad_maximum_fusion.refs_0_), channel_id=1, source_target_pairs={{0,17},{1,16},{2,19},{3,18},{4,21},{5,20},{6,23},{7,22},{8,25},{9,... | collective-permute-start | bytes 491528 | tf_op jit(solution)/shard_map/ppermute | solution.py:395
  48.5 1.3 %collective-permute-start.11 = (f32[320,128]{1,0:T(8,128)S(1)}, f32[320,128]{1,0:T(8,128)S(1)}, u32[]{:S(2)}, u32[]{:S(2)}) collective-permute-start(f32[320,128]{1,0:T(8,128)S(1)} %pad_maximum_fusion.refs_0_), channel_id=1, source_target_pairs={{0,1},{1,0},{2,3},{3,2},{4,5},{5,4},{6,7},{7,6},{8,9},{9,8},{10,11... | collective-permute-start | bytes 491528 | tf_op jit(solution)/shard_map/ppermute | solution.py:395
  49.8 0.6 collective-permute-start.10
  50.4 0.0 collective-permute-start.13
  50.4 3.5 %collective-permute-done.12.refs_3_ = f32[320,128]{1,0:T(8,128)S(1)} collective-permute-done((f32[320,128]{1,0:T(8,128)S(1)}, f32[320,128]{1,0:T(8,128)S(1)}, u32[]{:S(2)}, u32[]{:S(2)}) %collective-permute-start.12) | collective-permute-done | bytes 163872 | tf_op jit(solution)/shard_map/ppermute | solution.py:395
  53.9 0.0 collective-permute-start.16
  53.9 1.6 %collective-permute-done.11.refs_2_ = f32[320,128]{1,0:T(8,128)S(1)} collective-permute-done((f32[320,128]{1,0:T(8,128)S(1)}, f32[320,128]{1,0:T(8,128)S(1)}, u32[]{:S(2)}, u32[]{:S(2)}) %collective-permute-start.11) | collective-permute-done | bytes 163872 | tf_op jit(solution)/shard_map/ppermute | solution.py:395
  55.5 0.0 collective-permute-start.15
  55.5 0.1 collective-permute-done.10.refs_1_
  55.6 0.4 collective-permute-start.14
  56.0 0.0 collective-permute-done.13.refs_4_
  56.0 0.0 collective-permute-done.16.refs_7_
  56.0 0.9 %collective-permute-done.15.refs_6_ = f32[320,128]{1,0:T(8,128)S(1)} collective-permute-done((f32[320,128]{1,0:T(8,128)S(1)}, f32[320,128]{1,0:T(8,128)S(1)}, u32[]{:S(2)}, u32[]{:S(2)}) %collective-permute-start.15) | collective-permute-done | bytes 163872 | tf_op jit(solution)/shard_map/ppermute | solution.py:395
  56.9 0.2 collective-permute-done.14.refs_5_
  57.1 17.8 %first_section.1 = f32[96,768]{1,0:T(8,128)} custom-call(f32[320,128]{1,0:T(8,128)S(1)} %pad_maximum_fusion.refs_0_, f32[320,128]{1,0:T(8,128)S(1)} %collective-permute-done.10.refs_1_, f32[320,128]{1,0:T(8,128)S(1)} %collective-permute-done.11.refs_2_, f32[320,128]{1,0:T(8,128)S(1)} %collective-permute-done.12.refs_3_, ...), custom_call_target="tpu_custom_call" | custom-call | tf_op jit(solution)/shard_map/first_section/pallas_call | solution.py:373
  (4 shorter events, 0.1 us)
Async XLA Ops:
  16.7 2.3 %collective-permute-start = (f32[1280,128]{1,0:T(8,128)S(1)}, f32[1280,128]{1,0:T(8,128)S(1)}, u32[]{:S(2)}, u32[]{:S(2)}) collective-permute-start(f32[1280,128]{1,0:T(8,128)S(1)} %get-tuple-element.7), channel_id=1, source_target_pairs={{0,8},{1,9},{2,10},{3,11},{4,12},{5,13},{6,14},{7,15},{8,0},{9,1},... | collective-permute-start | bytes 1966088 | tf_op jit(solution)/shard_map/ppermute | solution.py:395
  19.1 8.9 %collective-permute-start.1 = (f32[320,128]{1,0:T(8,128)S(1)}, f32[320,128]{1,0:T(8,128)S(1)}, u32[]{:S(2)}, u32[]{:S(2)}) collective-permute-start(f32[320,128]{1,0:T(8,128)S(1)} %get-tuple-element.8), channel_id=1, source_target_pairs={{0,17},{1,16},{2,19},{3,18},{4,21},{5,20},{6,23},{7,22},{8,25},{9,... | collective-permute-start | bytes 491528 | tf_op jit(solution)/shard_map/ppermute | solution.py:395
  22.9 8.0 %collective-permute-start.3 = (f32[320,128]{1,0:T(8,128)S(1)}, f32[320,128]{1,0:T(8,128)S(1)}, u32[]{:S(2)}, u32[]{:S(2)}) collective-permute-start(f32[320,128]{1,0:T(8,128)S(1)} %get-tuple-element.9), channel_id=1, source_target_pairs={{0,1},{1,0},{2,3},{3,2},{4,5},{5,4},{6,7},{7,6},{8,9},{9,8},{10,11... | collective-permute-start | bytes 491528 | tf_op jit(solution)/shard_map/ppermute | solution.py:395
  23.4 7.8 %collective-permute-start.2 = (f32[320,128]{1,0:T(8,128)S(1)}, f32[320,128]{1,0:T(8,128)S(1)}, u32[]{:S(2)}, u32[]{:S(2)}) collective-permute-start(f32[320,128]{1,0:T(8,128)S(1)} %get-tuple-element.10), channel_id=1, source_target_pairs={{0,16},{1,17},{2,18},{3,19},{4,20},{5,21},{6,22},{7,23},{8,24},{9,... | collective-permute-start | bytes 491528 | tf_op jit(solution)/shard_map/ppermute | solution.py:395
  31.3 5.9 %collective-permute-start.4 = (f32[80,128]{1,0:T(8,128)S(1)}, f32[80,128]{1,0:T(8,128)S(1)}, u32[]{:S(2)}, u32[]{:S(2)}) collective-permute-start(f32[80,128]{1,0:T(8,128)S(1)} %get-tuple-element.11), channel_id=1, source_target_pairs={{0,6},{1,7},{2,4},{3,5},{4,2},{5,3},{6,0},{7,1},{8,14},{9,15},{10,... | collective-permute-start | bytes 122888 | tf_op jit(solution)/shard_map/ppermute | solution.py:395
  35.0 4.9 %collective-permute-start.6 = (f32[80,128]{1,0:T(8,128)S(1)}, f32[80,128]{1,0:T(8,128)S(1)}, u32[]{:S(2)}, u32[]{:S(2)}) collective-permute-start(f32[80,128]{1,0:T(8,128)S(1)} %get-tuple-element.12), channel_id=1, source_target_pairs={{0,4},{1,5},{2,6},{3,7},{4,0},{5,1},{6,2},{7,3},{8,12},{9,13},{10,... | collective-permute-start | bytes 122888 | tf_op jit(solution)/shard_map/ppermute | solution.py:395
  35.0 4.9 %collective-permute-start.5 = (f32[80,128]{1,0:T(8,128)S(1)}, f32[80,128]{1,0:T(8,128)S(1)}, u32[]{:S(2)}, u32[]{:S(2)}) collective-permute-start(f32[80,128]{1,0:T(8,128)S(1)} %get-tuple-element.13), channel_id=1, source_target_pairs={{0,2},{1,3},{2,0},{3,1},{4,6},{5,7},{6,4},{7,5},{8,10},{9,11},{10,... | collective-permute-start | bytes 122888 | tf_op jit(solution)/shard_map/ppermute | solution.py:395
  39.9 5.9 %collective-permute-start.9 = (f32[80,128]{1,0:T(8,128)S(1)}, f32[80,128]{1,0:T(8,128)S(1)}, u32[]{:S(2)}, u32[]{:S(2)}) collective-permute-start(f32[80,128]{1,0:T(8,128)S(1)} %fusion.3), channel_id=1, source_target_pairs={{0,6},{1,7},{2,4},{3,5},{4,2},{5,3},{6,0},{7,1},{8,14},{9,15},{10,... | collective-permute-start | bytes 122888 | tf_op jit(solution)/shard_map/ppermute | solution.py:395
  41.6 4.9 %collective-permute-start.8 = (f32[80,128]{1,0:T(8,128)S(1)}, f32[80,128]{1,0:T(8,128)S(1)}, u32[]{:S(2)}, u32[]{:S(2)}) collective-permute-start(f32[80,128]{1,0:T(8,128)S(1)} %fusion.3), channel_id=1, source_target_pairs={{0,4},{1,5},{2,6},{3,7},{4,0},{5,1},{6,2},{7,3},{8,12},{9,13},{10,... | collective-permute-start | bytes 122888 | tf_op jit(solution)/shard_map/ppermute | solution.py:395
  42.1 4.7 %collective-permute-start.7 = (f32[80,128]{1,0:T(8,128)S(1)}, f32[80,128]{1,0:T(8,128)S(1)}, u32[]{:S(2)}, u32[]{:S(2)}) collective-permute-start(f32[80,128]{1,0:T(8,128)S(1)} %fusion.3), channel_id=1, source_target_pairs={{0,2},{1,3},{2,0},{3,1},{4,6},{5,7},{6,4},{7,5},{8,10},{9,11},{10,... | collective-permute-start | bytes 122888 | tf_op jit(solution)/shard_map/ppermute | solution.py:395
  46.8 7.1 %collective-permute-start.12 = (f32[320,128]{1,0:T(8,128)S(1)}, f32[320,128]{1,0:T(8,128)S(1)}, u32[]{:S(2)}, u32[]{:S(2)}) collective-permute-start(f32[320,128]{1,0:T(8,128)S(1)} %pad_maximum_fusion.refs_0_), channel_id=1, source_target_pairs={{0,17},{1,16},{2,19},{3,18},{4,21},{5,20},{6,23},{7,22},{8,25},{9,... | collective-permute-start | bytes 491528 | tf_op jit(solution)/shard_map/ppermute | solution.py:395
  48.5 7.0 %collective-permute-start.11 = (f32[320,128]{1,0:T(8,128)S(1)}, f32[320,128]{1,0:T(8,128)S(1)}, u32[]{:S(2)}, u32[]{:S(2)}) collective-permute-start(f32[320,128]{1,0:T(8,128)S(1)} %pad_maximum_fusion.refs_0_), channel_id=1, source_target_pairs={{0,1},{1,0},{2,3},{3,2},{4,5},{5,4},{6,7},{7,6},{8,9},{9,8},{10,11... | collective-permute-start | bytes 491528 | tf_op jit(solution)/shard_map/ppermute | solution.py:395
  49.8 5.8 %collective-permute-start.10 = (f32[320,128]{1,0:T(8,128)S(1)}, f32[320,128]{1,0:T(8,128)S(1)}, u32[]{:S(2)}, u32[]{:S(2)}) collective-permute-start(f32[320,128]{1,0:T(8,128)S(1)} %pad_maximum_fusion.refs_0_), channel_id=1, source_target_pairs={{0,16},{1,17},{2,18},{3,19},{4,20},{5,21},{6,22},{7,23},{8,24},{9,... | collective-permute-start | bytes 491528 | tf_op jit(solution)/shard_map/ppermute | solution.py:395
  50.4 5.7 %collective-permute-start.13 = (f32[320,128]{1,0:T(8,128)S(1)}, f32[320,128]{1,0:T(8,128)S(1)}, u32[]{:S(2)}, u32[]{:S(2)}) collective-permute-start(f32[320,128]{1,0:T(8,128)S(1)} %pad_maximum_fusion.refs_0_), channel_id=1, source_target_pairs={{0,8},{1,9},{2,10},{3,11},{4,12},{5,13},{6,14},{7,15},{8,0},{9,1},... | collective-permute-start | bytes 491528 | tf_op jit(solution)/shard_map/ppermute | solution.py:395
  53.9 2.1 %collective-permute-start.16 = (f32[320,128]{1,0:T(8,128)S(1)}, f32[320,128]{1,0:T(8,128)S(1)}, u32[]{:S(2)}, u32[]{:S(2)}) collective-permute-start(f32[320,128]{1,0:T(8,128)S(1)} %collective-permute-done.12.refs_3_), channel_id=1, source_target_pairs={{0,8},{1,9},{2,10},{3,11},{4,12},{5,13},{6,14},{7,15},{8,0},{9,1},... | collective-permute-start | bytes 491528 | tf_op jit(solution)/shard_map/ppermute | solution.py:395
  55.5 1.4 %collective-permute-start.15 = (f32[320,128]{1,0:T(8,128)S(1)}, f32[320,128]{1,0:T(8,128)S(1)}, u32[]{:S(2)}, u32[]{:S(2)}) collective-permute-start(f32[320,128]{1,0:T(8,128)S(1)} %collective-permute-done.11.refs_2_), channel_id=1, source_target_pairs={{0,8},{1,9},{2,10},{3,11},{4,12},{5,13},{6,14},{7,15},{8,0},{9,1},... | collective-permute-start | bytes 491528 | tf_op jit(solution)/shard_map/ppermute | solution.py:395
  55.6 1.5 %collective-permute-start.14 = (f32[320,128]{1,0:T(8,128)S(1)}, f32[320,128]{1,0:T(8,128)S(1)}, u32[]{:S(2)}, u32[]{:S(2)}) collective-permute-start(f32[320,128]{1,0:T(8,128)S(1)} %collective-permute-done.10.refs_1_), channel_id=1, source_target_pairs={{0,8},{1,9},{2,10},{3,11},{4,12},{5,13},{6,14},{7,15},{8,0},{9,1},... | collective-permute-start | bytes 491528 | tf_op jit(solution)/shard_map/ppermute | solution.py:395

commit v8 on v7

--- a/solution.py
+++ b/solution.py
@@ -115,9 +115,10 @@
 
 
 def scenario_kernel(
-    place_fn, count, region, hess_hbm, flags, low_d, low_s, up_d, up_s, coup_hbm, pattern, first,
-    factor_hbm, keep, send, hess, coup, factor, d_ref, ih, il, lh, ll, xh, xl, whole, diagonal, in_sem, out_sem,
+    place_fn, count, outs, region, hess_hbm, flags, low_d, low_s, up_d, up_s, coup_hbm, pattern, first, factor_hbm, *refs
 ):
+    parts = refs[:outs]
+    hess, coup, factor, d_ref, ih, il, lh, ll, xh, xl, whole, diagonal, in_sem, out_sem = refs[outs:]
     n, m = coup.shape
     nt, mt = n // T, m // T
     loads = []
@@ -202,18 +203,17 @@
         whole[at, :] = whole[at, :] + first[...]
 
     pack_diagonal(whole, diagonal)
-    half = count // 2
-    chunk = keep.shape[0] // half
-    for side in range(2):
-
-        @pl.when(place // half == side)
+    each = count // outs
+    chunk = parts[0].shape[0] // each
+    for top in range(outs):
+
+        @pl.when(place // each == top)
         def _():
             for l, at, rows, square, i, j in pieces(m, count * chunk, count):
-                to = pl.multiple_of(((l ^ place) % half) * chunk, 8) + at
-                target = (keep, send)[(l // half) ^ side]
+                to = pl.multiple_of(((l ^ place) % each) * chunk, 8) + at
                 source = whole if square else diagonal
                 value = jnp.zeros((rows, T), F32) if square is None else source[i : i + rows, j : j + T]
-                target[pl.ds(to, rows), :] = value
+                parts[(l // each) ^ top][pl.ds(to, rows), :] = value
 
     for store in stores:
         store.wait()
@@ -340,14 +340,14 @@
         square[k + h : k + T, k : k + T] = jnp.where(left, turned[h:], b)
 
 
-def scenario(place_fn, region, hess, flags, low_d, low_s, up_d, up_s, coup, pattern, first, rows, count):
+def scenario(place_fn, region, hess, flags, low_d, low_s, up_d, up_s, coup, pattern, first, rows, count, outs):
     n, m = coup.shape
-    half = jax.ShapeDtypeStruct((rows // 2, T), F32)
+    part = jax.ShapeDtypeStruct((rows // outs, T), F32)
     return pl.pallas_call(
-        functools.partial(scenario_kernel, place_fn, count),
-        out_shape=(jax.ShapeDtypeStruct((n, n), F32), half, half),
+        functools.partial(scenario_kernel, place_fn, count, outs),
+        out_shape=(jax.ShapeDtypeStruct((n, n), F32),) + (part,) * outs,
         in_specs=[SMEM, HBM] + [VMEM] * 5 + [HBM, VMEM, VMEM],
-        out_specs=(HBM, VMEM, VMEM),
+        out_specs=(HBM,) + (VMEM,) * outs,
         scratch_shapes=[
             pltpu.VMEM((n, n), F32),
             pltpu.VMEM((n, m), F32),
@@ -414,12 +414,14 @@
     return sorted(range(1, n), key=lambda k: (-k.bit_count(), k))
 
 
-def sum_everywhere(x, sent, rounds, count):
-    x = x + swap(sent, masks_of(rounds[0])[1], count)
-    for bits in rounds[1:]:
+def sum_everywhere(kept, sent, rounds, count):
+    order = farthest_first(len(kept)) + [0]
+    cut = {k: kept[k] + swap(sent[k], masks_of(rounds[0])[1], count) for k in order}
+    for step, bits in enumerate(rounds[1:]):
         masks = masks_of(bits)
-        part = x.shape[0] // len(masks)
-        cut = [x[k * part : (k + 1) * part] for k in range(len(masks))]
+        if step:
+            part = x.shape[0] // len(masks)
+            cut = [x[k * part : (k + 1) * part] for k in range(len(masks))]
         got = [swap(cut[k], masks[k], count) for k in farthest_first(len(masks))]
         x = functools.reduce(jnp.add, got, cut[0])
     parts = [x]
@@ -442,16 +444,17 @@
     def per_device(hess_scen, flags, low_d, low_s, up_d, up_s, coupling, pattern, region, hess_first):
         own, m = hess_first.shape
         rows = packed_rows(m, count)
-        factors, keep, send = [], None, None
+        outs = 2 * len(masks_of(rounds[1]))
+        factors, parts = [], None
         for i in range(hess_scen.shape[0]):
-            factor, low, high = scenario(
+            factor, *new = scenario(
                 functools.partial(where, i == 0), region[i : i + 1], hess_scen[i],
                 flags[i : i + 1], low_d[i : i + 1], low_s[i : i + 1], up_d[i : i + 1], up_s[i : i + 1],
-                coupling[i], pattern[i : i + 1], hess_first, rows, count,
+                coupling[i], pattern[i : i + 1], hess_first, rows, count, outs,
             )
             factors.append(factor)
-            keep, send = (low, high) if keep is None else (keep + low, send + high)
-        parts = sum_everywhere(keep, send, rounds, count)
+            parts = new if parts is None else [a + b for a, b in zip(parts, new)]
+        parts = sum_everywhere(parts[: outs // 2], parts[outs // 2 :], rounds, count)
         mine = first_section(functools.partial(where, True), parts, own, m, count)
         return (jnp.stack(factors), mine)
 

time: 75.1 us -> 74.7 us (level)
  waiting for transfers between devices: 22.3 us -> 20.8 us
  starting transfers between devices: 17.9 us -> 18.8 us
    ppermute x17 -> x20, waiting for transfers between devices: 22.3 us -> 20.8 us  [swap(): return lax.ppermute(x, AXES, [(i, i ^ mask) for i in range(count)])]
    ppermute x17 -> x20, starting transfers between devices: 17.9 us -> 18.8 us  [swap(): return lax.ppermute(x, AXES, [(i, i ^ mask) for i in range(count)])]
  transfers between devices with their start and end apart: 17 -> 20, of which waited for: 14 -> 12; matrix products, arithmetic and copies ran while one was open for 0% -> 0% of each run, Pallas kernels for 0% -> 0%
where the time goes in v8:
time: 74.7 us; the launch traced here: 74.6 us
  Pallas kernels  33.4 us (45%)
  waiting for transfers between devices  20.8 us (28%)
  starting transfers between devices  18.8 us (25%)
  between operations  1.32 us (2%)
    ppermute x20, waiting for transfers between devices, swap(): return lax.ppermute(x, AXES, [(i, i ^ mask) for i in range(count)])  20.8 us
    ppermute x20, starting transfers between devices, swap(): return lax.ppermute(x, AXES, [(i, i ^ mask) for i in range(count)])  18.8 us
    pallas_call x1, Pallas kernels, first_section(): pl.pallas_call(functools.partial(first_kernel, place_fn, count), out_shap...  18 us
    pallas_call x1, Pallas kernels, scenario(): pl.pallas_call(functools.partial(scenario_kernel, place_fn, count, outs),...  15.5 us
  transfers between devices with their start and end apart: 20, of which 12 were waited for; matrix products, arithmetic and copies ran while one was open for 0% of the time, Pallas kernels for 0%

profile of v8, /device:TPU:0, one launch (start us, length us, event | category | flops | bytes accessed | tf_op | source)
XLA Modules:
  0.0 74.6 jit_solution(18077078134797283659)
XLA Ops:
  1.3 15.5 %scenario.1 = (f32[512,512]{1,0:T(8,128)}, f32[320,128]{1,0:T(8,128)S(1)}, f32[320,128]{1,0:T(8,128)S(1)}, f32[320,128]{1,0:T(8,128)S(1)}, f32[320,128]{1,0:T(8,...) custom-call(s32[1]{0:T(128)S(6)} %copy.12.region, ...), custom_call_target="tpu_custom_call" | custom-call | tf_op jit(solution)/shard_map/scenario/pallas_call | solution.py:346
  16.7 0.5 collective-permute-start.1
  17.3 0.1 collective-permute-start.3
  17.4 0.4 collective-permute-start.5
  17.8 0.1 collective-permute-start
  17.9 0.4 collective-permute-done.1
  18.3 3.9 %collective-permute-start.2 = (f32[320,128]{1,0:T(8,128)S(1)}, f32[320,128]{1,0:T(8,128)S(1)}, u32[]{:S(2)}, u32[]{:S(2)}) collective-permute-start(f32[320,128]{1,0:T(8,128)S(1)} %add.31), channel_id=1, source_target_pairs={{0,17},{1,16},{2,19},{3,18},{4,21},{5,20},{6,23},{7,22},{8,25},{9,... | collective-permute-start | bytes 491528 | tf_op jit(solution)/shard_map/ppermute | solution.py:395
  22.2 0.0 collective-permute-done.3
  22.2 0.6 collective-permute-start.4
  22.9 0.0 collective-permute-done.5
  22.9 0.2 collective-permute-start.6
  23.1 0.0 collective-permute-done
  23.1 4.2 %collective-permute-done.2 = f32[320,128]{1,0:T(8,128)S(1)} collective-permute-done((f32[320,128]{1,0:T(8,128)S(1)}, f32[320,128]{1,0:T(8,128)S(1)}, u32[]{:S(2)}, u32[]{:S(2)}) %collective-permute-start.2) | collective-permute-done | bytes 163872 | tf_op jit(solution)/shard_map/ppermute | solution.py:395
  27.2 3.3 %collective-permute-done.4 = f32[320,128]{1,0:T(8,128)S(1)} collective-permute-done((f32[320,128]{1,0:T(8,128)S(1)}, f32[320,128]{1,0:T(8,128)S(1)}, u32[]{:S(2)}, u32[]{:S(2)}) %collective-permute-start.4) | collective-permute-done | bytes 163872 | tf_op jit(solution)/shard_map/ppermute | solution.py:395
  30.5 0.0 collective-permute-done.6
  30.5 0.1 add_add_fusion
  30.6 3.7 %collective-permute-start.7 = (f32[80,128]{1,0:T(8,128)S(1)}, f32[80,128]{1,0:T(8,128)S(1)}, u32[]{:S(2)}, u32[]{:S(2)}) collective-permute-start(f32[80,128]{1,0:T(8,128)S(1)} %get-tuple-element.20), channel_id=1, source_target_pairs={{0,6},{1,7},{2,4},{3,5},{4,2},{5,3},{6,0},{7,1},{8,14},{9,15},{10,... | collective-permute-start | bytes 122888 | tf_op jit(solution)/shard_map/ppermute | solution.py:395
  34.3 0.0 collective-permute-start.9
  34.3 0.8 %collective-permute-start.8 = (f32[80,128]{1,0:T(8,128)S(1)}, f32[80,128]{1,0:T(8,128)S(1)}, u32[]{:S(2)}, u32[]{:S(2)}) collective-permute-start(f32[80,128]{1,0:T(8,128)S(1)} %get-tuple-element.22), channel_id=1, source_target_pairs={{0,2},{1,3},{2,0},{3,1},{4,6},{5,7},{6,4},{7,5},{8,10},{9,11},{10,... | collective-permute-start | bytes 122888 | tf_op jit(solution)/shard_map/ppermute | solution.py:395
  35.1 1.6 %collective-permute-done.7 = f32[80,128]{1,0:T(8,128)S(1)} collective-permute-done((f32[80,128]{1,0:T(8,128)S(1)}, f32[80,128]{1,0:T(8,128)S(1)}, u32[]{:S(2)}, u32[]{:S(2)}) %collective-permute-start.7) | collective-permute-done | bytes 40992 | tf_op jit(solution)/shard_map/ppermute | solution.py:395
  36.7 2.5 %collective-permute-done.9 = f32[80,128]{1,0:T(8,128)S(1)} collective-permute-done((f32[80,128]{1,0:T(8,128)S(1)}, f32[80,128]{1,0:T(8,128)S(1)}, u32[]{:S(2)}, u32[]{:S(2)}) %collective-permute-start.9) | collective-permute-done | bytes 40992 | tf_op jit(solution)/shard_map/ppermute | solution.py:395
  39.2 0.0 collective-permute-done.8
  39.2 1.6 %collective-permute-start.12 = (f32[80,128]{1,0:T(8,128)S(1)}, f32[80,128]{1,0:T(8,128)S(1)}, u32[]{:S(2)}, u32[]{:S(2)}) collective-permute-start(f32[80,128]{1,0:T(8,128)S(1)} %fusion.1), channel_id=1, source_target_pairs={{0,6},{1,7},{2,4},{3,5},{4,2},{5,3},{6,0},{7,1},{8,14},{9,15},{10,... | collective-permute-start | bytes 122888 | tf_op jit(solution)/shard_map/ppermute | solution.py:395
  40.8 0.6 collective-permute-start.11
  41.4 2.3 %collective-permute-start.10 = (f32[80,128]{1,0:T(8,128)S(1)}, f32[80,128]{1,0:T(8,128)S(1)}, u32[]{:S(2)}, u32[]{:S(2)}) collective-permute-start(f32[80,128]{1,0:T(8,128)S(1)} %fusion.1), channel_id=1, source_target_pairs={{0,2},{1,3},{2,0},{3,1},{4,6},{5,7},{6,4},{7,5},{8,10},{9,11},{10,... | collective-permute-start | bytes 122888 | tf_op jit(solution)/shard_map/ppermute | solution.py:395
  43.7 1.4 %collective-permute-done.12 = f32[80,128]{1,0:T(8,128)S(1)} collective-permute-done((f32[80,128]{1,0:T(8,128)S(1)}, f32[80,128]{1,0:T(8,128)S(1)}, u32[]{:S(2)}, u32[]{:S(2)}) %collective-permute-start.12) | collective-permute-done | bytes 40992 | tf_op jit(solution)/shard_map/ppermute | solution.py:395
  45.1 0.7 %collective-permute-done.11 = f32[80,128]{1,0:T(8,128)S(1)} collective-permute-done((f32[80,128]{1,0:T(8,128)S(1)}, f32[80,128]{1,0:T(8,128)S(1)}, u32[]{:S(2)}, u32[]{:S(2)}) %collective-permute-start.11) | collective-permute-done | bytes 40992 | tf_op jit(solution)/shard_map/ppermute | solution.py:395
  45.8 0.3 collective-permute-done.10
  46.1 2.6 %collective-permute-start.15 = (f32[320,128]{1,0:T(8,128)S(1)}, f32[320,128]{1,0:T(8,128)S(1)}, u32[]{:S(2)}, u32[]{:S(2)}) collective-permute-start(f32[320,128]{1,0:T(8,128)S(1)} %pad_maximum_fusion.refs_0_), channel_id=1, source_target_pairs={{0,17},{1,16},{2,19},{3,18},{4,21},{5,20},{6,23},{7,22},{8,25},{9,... | collective-permute-start | bytes 491528 | tf_op jit(solution)/shard_map/ppermute | solution.py:395
  48.7 0.4 collective-permute-start.14
  49.1 0.6 collective-permute-start.13
  49.6 0.0 collective-permute-start.16
  49.6 4.1 %collective-permute-done.15.refs_3_ = f32[320,128]{1,0:T(8,128)S(1)} collective-permute-done((f32[320,128]{1,0:T(8,128)S(1)}, f32[320,128]{1,0:T(8,128)S(1)}, u32[]{:S(2)}, u32[]{:S(2)}) %collective-permute-start.15) | collective-permute-done | bytes 163872 | tf_op jit(solution)/shard_map/ppermute | solution.py:395
  53.8 0.0 collective-permute-start.19
  53.8 1.2 %collective-permute-done.14.refs_2_ = f32[320,128]{1,0:T(8,128)S(1)} collective-permute-done((f32[320,128]{1,0:T(8,128)S(1)}, f32[320,128]{1,0:T(8,128)S(1)}, u32[]{:S(2)}, u32[]{:S(2)}) %collective-permute-start.14) | collective-permute-done | bytes 163872 | tf_op jit(solution)/shard_map/ppermute | solution.py:395
  55.0 0.0 collective-permute-start.18
  55.0 0.0 collective-permute-done.13.refs_1_
  55.0 0.5 collective-permute-start.17
  55.5 0.0 collective-permute-done.16.refs_4_
  55.5 0.0 collective-permute-done.19.refs_7_
  55.5 0.9 %collective-permute-done.18.refs_6_ = f32[320,128]{1,0:T(8,128)S(1)} collective-permute-done((f32[320,128]{1,0:T(8,128)S(1)}, f32[320,128]{1,0:T(8,128)S(1)}, u32[]{:S(2)}, u32[]{:S(2)}) %collective-permute-start.18) | collective-permute-done | bytes 163872 | tf_op jit(solution)/shard_map/ppermute | solution.py:395
  56.3 0.2 collective-permute-done.17.refs_5_
  56.6 18.0 %first_section.1 = f32[96,768]{1,0:T(8,128)} custom-call(f32[320,128]{1,0:T(8,128)S(1)} %pad_maximum_fusion.refs_0_, f32[320,128]{1,0:T(8,128)S(1)} %collective-permute-done.13.refs_1_, f32[320,128]{1,0:T(8,128)S(1)} %collective-permute-done.14.refs_2_, f32[320,128]{1,0:T(8,128)S(1)} %collective-permute-done.15.refs_3_, ...), custom_call_target="tpu_custom_call" | custom-call | tf_op jit(solution)/shard_map/first_section/pallas_call | solution.py:373
  (6 shorter events, 0.1 us)
Async XLA Ops:
  16.7 1.6 %collective-permute-start.1 = (f32[320,128]{1,0:T(8,128)S(1)}, f32[320,128]{1,0:T(8,128)S(1)}, u32[]{:S(2)}, u32[]{:S(2)}) collective-permute-start(f32[320,128]{1,0:T(8,128)S(1)} %get-tuple-element.15), channel_id=1, source_target_pairs={{0,8},{1,9},{2,10},{3,11},{4,12},{5,13},{6,14},{7,15},{8,0},{9,1},... | collective-permute-start | bytes 491528 | tf_op jit(solution)/shard_map/ppermute | solution.py:395
  17.3 4.9 %collective-permute-start.3 = (f32[320,128]{1,0:T(8,128)S(1)}, f32[320,128]{1,0:T(8,128)S(1)}, u32[]{:S(2)}, u32[]{:S(2)}) collective-permute-start(f32[320,128]{1,0:T(8,128)S(1)} %get-tuple-element.17), channel_id=1, source_target_pairs={{0,8},{1,9},{2,10},{3,11},{4,12},{5,13},{6,14},{7,15},{8,0},{9,1},... | collective-permute-start | bytes 491528 | tf_op jit(solution)/shard_map/ppermute | solution.py:395
  17.4 5.5 %collective-permute-start.5 = (f32[320,128]{1,0:T(8,128)S(1)}, f32[320,128]{1,0:T(8,128)S(1)}, u32[]{:S(2)}, u32[]{:S(2)}) collective-permute-start(f32[320,128]{1,0:T(8,128)S(1)} %get-tuple-element.19), channel_id=1, source_target_pairs={{0,8},{1,9},{2,10},{3,11},{4,12},{5,13},{6,14},{7,15},{8,0},{9,1},... | collective-permute-start | bytes 491528 | tf_op jit(solution)/shard_map/ppermute | solution.py:395
  17.8 5.3 %collective-permute-start = (f32[320,128]{1,0:T(8,128)S(1)}, f32[320,128]{1,0:T(8,128)S(1)}, u32[]{:S(2)}, u32[]{:S(2)}) collective-permute-start(f32[320,128]{1,0:T(8,128)S(1)} %get-tuple-element.13), channel_id=1, source_target_pairs={{0,8},{1,9},{2,10},{3,11},{4,12},{5,13},{6,14},{7,15},{8,0},{9,1},... | collective-permute-start | bytes 491528 | tf_op jit(solution)/shard_map/ppermute | solution.py:395
  18.3 8.9 %collective-permute-start.2 = (f32[320,128]{1,0:T(8,128)S(1)}, f32[320,128]{1,0:T(8,128)S(1)}, u32[]{:S(2)}, u32[]{:S(2)}) collective-permute-start(f32[320,128]{1,0:T(8,128)S(1)} %add.31), channel_id=1, source_target_pairs={{0,17},{1,16},{2,19},{3,18},{4,21},{5,20},{6,23},{7,22},{8,25},{9,... | collective-permute-start | bytes 491528 | tf_op jit(solution)/shard_map/ppermute | solution.py:395
  22.2 8.3 %collective-permute-start.4 = (f32[320,128]{1,0:T(8,128)S(1)}, f32[320,128]{1,0:T(8,128)S(1)}, u32[]{:S(2)}, u32[]{:S(2)}) collective-permute-start(f32[320,128]{1,0:T(8,128)S(1)} %add.33), channel_id=1, source_target_pairs={{0,16},{1,17},{2,18},{3,19},{4,20},{5,21},{6,22},{7,23},{8,24},{9,... | collective-permute-start | bytes 491528 | tf_op jit(solution)/shard_map/ppermute | solution.py:395
  22.9 7.7 %collective-permute-start.6 = (f32[320,128]{1,0:T(8,128)S(1)}, f32[320,128]{1,0:T(8,128)S(1)}, u32[]{:S(2)}, u32[]{:S(2)}) collective-permute-start(f32[320,128]{1,0:T(8,128)S(1)} %add.35), channel_id=1, source_target_pairs={{0,1},{1,0},{2,3},{3,2},{4,5},{5,4},{6,7},{7,6},{8,9},{9,8},{10,11... | collective-permute-start | bytes 491528 | tf_op jit(solution)/shard_map/ppermute | solution.py:395
  30.6 6.1 %collective-permute-start.7 = (f32[80,128]{1,0:T(8,128)S(1)}, f32[80,128]{1,0:T(8,128)S(1)}, u32[]{:S(2)}, u32[]{:S(2)}) collective-permute-start(f32[80,128]{1,0:T(8,128)S(1)} %get-tuple-element.20), channel_id=1, source_target_pairs={{0,6},{1,7},{2,4},{3,5},{4,2},{5,3},{6,0},{7,1},{8,14},{9,15},{10,... | collective-permute-start | bytes 122888 | tf_op jit(solution)/shard_map/ppermute | solution.py:395
  34.3 4.9 %collective-permute-start.9 = (f32[80,128]{1,0:T(8,128)S(1)}, f32[80,128]{1,0:T(8,128)S(1)}, u32[]{:S(2)}, u32[]{:S(2)}) collective-permute-start(f32[80,128]{1,0:T(8,128)S(1)} %get-tuple-element.21), channel_id=1, source_target_pairs={{0,4},{1,5},{2,6},{3,7},{4,0},{5,1},{6,2},{7,3},{8,12},{9,13},{10,... | collective-permute-start | bytes 122888 | tf_op jit(solution)/shard_map/ppermute | solution.py:395
  34.3 4.9 %collective-permute-start.8 = (f32[80,128]{1,0:T(8,128)S(1)}, f32[80,128]{1,0:T(8,128)S(1)}, u32[]{:S(2)}, u32[]{:S(2)}) collective-permute-start(f32[80,128]{1,0:T(8,128)S(1)} %get-tuple-element.22), channel_id=1, source_target_pairs={{0,2},{1,3},{2,0},{3,1},{4,6},{5,7},{6,4},{7,5},{8,10},{9,11},{10,... | collective-permute-start | bytes 122888 | tf_op jit(solution)/shard_map/ppermute | solution.py:395
  39.2 5.9 %collective-permute-start.12 = (f32[80,128]{1,0:T(8,128)S(1)}, f32[80,128]{1,0:T(8,128)S(1)}, u32[]{:S(2)}, u32[]{:S(2)}) collective-permute-start(f32[80,128]{1,0:T(8,128)S(1)} %fusion.1), channel_id=1, source_target_pairs={{0,6},{1,7},{2,4},{3,5},{4,2},{5,3},{6,0},{7,1},{8,14},{9,15},{10,... | collective-permute-start | bytes 122888 | tf_op jit(solution)/shard_map/ppermute | solution.py:395
  40.8 5.0 %collective-permute-start.11 = (f32[80,128]{1,0:T(8,128)S(1)}, f32[80,128]{1,0:T(8,128)S(1)}, u32[]{:S(2)}, u32[]{:S(2)}) collective-permute-start(f32[80,128]{1,0:T(8,128)S(1)} %fusion.1), channel_id=1, source_target_pairs={{0,4},{1,5},{2,6},{3,7},{4,0},{5,1},{6,2},{7,3},{8,12},{9,13},{10,... | collective-permute-start | bytes 122888 | tf_op jit(solution)/shard_map/ppermute | solution.py:395
  41.4 4.7 %collective-permute-start.10 = (f32[80,128]{1,0:T(8,128)S(1)}, f32[80,128]{1,0:T(8,128)S(1)}, u32[]{:S(2)}, u32[]{:S(2)}) collective-permute-start(f32[80,128]{1,0:T(8,128)S(1)} %fusion.1), channel_id=1, source_target_pairs={{0,2},{1,3},{2,0},{3,1},{4,6},{5,7},{6,4},{7,5},{8,10},{9,11},{10,... | collective-permute-start | bytes 122888 | tf_op jit(solution)/shard_map/ppermute | solution.py:395
  46.1 7.7 %collective-permute-start.15 = (f32[320,128]{1,0:T(8,128)S(1)}, f32[320,128]{1,0:T(8,128)S(1)}, u32[]{:S(2)}, u32[]{:S(2)}) collective-permute-start(f32[320,128]{1,0:T(8,128)S(1)} %pad_maximum_fusion.refs_0_), channel_id=1, source_target_pairs={{0,17},{1,16},{2,19},{3,18},{4,21},{5,20},{6,23},{7,22},{8,25},{9,... | collective-permute-start | bytes 491528 | tf_op jit(solution)/shard_map/ppermute | solution.py:395
  48.7 6.3 %collective-permute-start.14 = (f32[320,128]{1,0:T(8,128)S(1)}, f32[320,128]{1,0:T(8,128)S(1)}, u32[]{:S(2)}, u32[]{:S(2)}) collective-permute-start(f32[320,128]{1,0:T(8,128)S(1)} %pad_maximum_fusion.refs_0_), channel_id=1, source_target_pairs={{0,1},{1,0},{2,3},{3,2},{4,5},{5,4},{6,7},{7,6},{8,9},{9,8},{10,11... | collective-permute-start | bytes 491528 | tf_op jit(solution)/shard_map/ppermute | solution.py:395
  49.1 5.9 %collective-permute-start.13 = (f32[320,128]{1,0:T(8,128)S(1)}, f32[320,128]{1,0:T(8,128)S(1)}, u32[]{:S(2)}, u32[]{:S(2)}) collective-permute-start(f32[320,128]{1,0:T(8,128)S(1)} %pad_maximum_fusion.refs_0_), channel_id=1, source_target_pairs={{0,16},{1,17},{2,18},{3,19},{4,20},{5,21},{6,22},{7,23},{8,24},{9,... | collective-permute-start | bytes 491528 | tf_op jit(solution)/shard_map/ppermute | solution.py:395
  49.6 5.8 %collective-permute-start.16 = (f32[320,128]{1,0:T(8,128)S(1)}, f32[320,128]{1,0:T(8,128)S(1)}, u32[]{:S(2)}, u32[]{:S(2)}) collective-permute-start(f32[320,128]{1,0:T(8,128)S(1)} %pad_maximum_fusion.refs_0_), channel_id=1, source_target_pairs={{0,8},{1,9},{2,10},{3,11},{4,12},{5,13},{6,14},{7,15},{8,0},{9,1},... | collective-permute-start | bytes 491528 | tf_op jit(solution)/shard_map/ppermute | solution.py:395
  53.8 1.7 %collective-permute-start.19 = (f32[320,128]{1,0:T(8,128)S(1)}, f32[320,128]{1,0:T(8,128)S(1)}, u32[]{:S(2)}, u32[]{:S(2)}) collective-permute-start(f32[320,128]{1,0:T(8,128)S(1)} %collective-permute-done.15.refs_3_), channel_id=1, source_target_pairs={{0,8},{1,9},{2,10},{3,11},{4,12},{5,13},{6,14},{7,15},{8,0},{9,1},... | collective-permute-start | bytes 491528 | tf_op jit(solution)/shard_map/ppermute | solution.py:395
  55.0 1.4 %collective-permute-start.18 = (f32[320,128]{1,0:T(8,128)S(1)}, f32[320,128]{1,0:T(8,128)S(1)}, u32[]{:S(2)}, u32[]{:S(2)}) collective-permute-start(f32[320,128]{1,0:T(8,128)S(1)} %collective-permute-done.14.refs_2_), channel_id=1, source_target_pairs={{0,8},{1,9},{2,10},{3,11},{4,12},{5,13},{6,14},{7,15},{8,0},{9,1},... | collective-permute-start | bytes 491528 | tf_op jit(solution)/shard_map/ppermute | solution.py:395
  55.0 1.6 %collective-permute-start.17 = (f32[320,128]{1,0:T(8,128)S(1)}, f32[320,128]{1,0:T(8,128)S(1)}, u32[]{:S(2)}, u32[]{:S(2)}) collective-permute-start(f32[320,128]{1,0:T(8,128)S(1)} %collective-permute-done.13.refs_1_), channel_id=1, source_target_pairs={{0,8},{1,9},{2,10},{3,11},{4,12},{5,13},{6,14},{7,15},{8,0},{9,1},... | collective-permute-start | bytes 491528 | tf_op jit(solution)/shard_map/ppermute | solution.py:395

commit v9 on v8

--- a/solution.py
+++ b/solution.py
@@ -22,6 +22,13 @@
     bh, bl = b
     d = functools.partial(lax.dot_general, dimension_numbers=(dims, ((), ())), preferred_element_type=F32)
     return d(ah, bh) + (d(ah, bl) + d(al, bh))
+
+
+def dot3_stacked(a, b, dims):
+    (ah, al), (bh, bl), ((ka,), (kb,)) = a, b, dims
+    left = jnp.concatenate([ah, ah, al], axis=ka)
+    right = jnp.concatenate([bh, bl, bh], axis=kb)
+    return lax.dot_general(left, right, (dims, ((), ())), preferred_element_type=F32)
 
 
 NN = ((1,), (0,))
@@ -248,7 +255,7 @@
                 lo, hi = k * T, (k + 1) * T
                 panel = work[lo:, lo:hi]
                 if k:
-                    panel = panel - dot3((lh[lo:, :lo], ll[lo:, :lo]), (lh[lo:hi, :lo], ll[lo:hi, :lo]), NT)
+                    panel = panel - dot3_stacked((lh[lo:, :lo], ll[lo:, :lo]), (lh[lo:hi, :lo], ll[lo:hi, :lo]), NT)
                 d_ref[:, :T] = panel[:T]
                 d_ref[:, T:] = jnp.where(eye, 1.0, 0.0)
                 if k + 1 < mt:
@@ -263,7 +270,7 @@
                 lo, hi = k * T, (k + 1) * T
                 full[lo:hi, lo:hi] = lower_of(d_ref)
                 if k + 1 < mt:
-                    below = dot3(split(full[hi:, lo:hi]), split(d_ref[:, T:]), NT)
+                    below = dot3_stacked(split(full[hi:, lo:hi]), split(d_ref[:, T:]), NT)
                     full[hi:, lo:hi] = below
                     lh[hi:, lo:hi], ll[hi:, lo:hi] = split(below)
 
@@ -415,14 +422,14 @@
 
 
 def sum_everywhere(kept, sent, rounds, count):
-    order = farthest_first(len(kept)) + [0]
+    order = list(range(len(kept)))[::-1]
     cut = {k: kept[k] + swap(sent[k], masks_of(rounds[0])[1], count) for k in order}
     for step, bits in enumerate(rounds[1:]):
         masks = masks_of(bits)
         if step:
             part = x.shape[0] // len(masks)
             cut = [x[k * part : (k + 1) * part] for k in range(len(masks))]
-        got = [swap(cut[k], masks[k], count) for k in farthest_first(len(masks))]
+        got = [swap(cut[k], masks[k], count) for k in (farthest_first(len(masks)) if step else order[:-1])]
         x = functools.reduce(jnp.add, got, cut[0])
     parts = [x]
     for bits in reversed(rounds[1:]):

time: 74.7 us -> 74.5 us (level)
  transfers between devices with their start and end apart: 20 -> 20, of which waited for: 12 -> 14; matrix products, arithmetic and copies ran while one was open for 0% -> 0% of each run, Pallas kernels for 0% -> 0%
where the time goes in v9:
time: 74.5 us; the launch traced here: 74.3 us
  Pallas kernels  33.4 us (45%)
  waiting for transfers between devices  20.8 us (28%)
  starting transfers between devices  18.7 us (25%)
  between operations  1.32 us (2%)
    ppermute x20, waiting for transfers between devices, swap(): return lax.ppermute(x, AXES, [(i, i ^ mask) for i in range(count)])  20.8 us
    ppermute x20, starting transfers between devices, swap(): return lax.ppermute(x, AXES, [(i, i ^ mask) for i in range(count)])  18.7 us
    pallas_call x1, Pallas kernels, first_section(): pl.pallas_call(functools.partial(first_kernel, place_fn, count), out_shap...  17.9 us
    pallas_call x1, Pallas kernels, scenario(): pl.pallas_call(functools.partial(scenario_kernel, place_fn, count, outs),...  15.5 us
  transfers between devices with their start and end apart: 20, of which 14 were waited for; matrix products, arithmetic and copies ran while one was open for 0% of the time, Pallas kernels for 0%

profile of v9, /device:TPU:0, one launch (start us, length us, event | category | flops | bytes accessed | tf_op | source)
XLA Modules:
  0.0 74.3 jit_solution(36248877297950863)
XLA Ops:
  1.3 15.5 %scenario.1 = (f32[512,512]{1,0:T(8,128)}, f32[320,128]{1,0:T(8,128)S(1)}, f32[320,128]{1,0:T(8,128)S(1)}, f32[320,128]{1,0:T(8,128)S(1)}, f32[320,128]{1,0:T(8,...) custom-call(s32[1]{0:T(128)S(6)} %copy.12.region, ...), custom_call_target="tpu_custom_call" | custom-call | tf_op jit(solution)/shard_map/scenario/pallas_call | solution.py:353
  16.7 0.5 collective-permute-start.1
  17.3 0.1 collective-permute-start.3
  17.4 0.4 collective-permute-start.5
  17.8 0.1 collective-permute-start
  17.9 0.4 collective-permute-done.1
  18.3 3.9 %collective-permute-start.2 = (f32[320,128]{1,0:T(8,128)S(1)}, f32[320,128]{1,0:T(8,128)S(1)}, u32[]{:S(2)}, u32[]{:S(2)}) collective-permute-start(f32[320,128]{1,0:T(8,128)S(1)} %add.31), channel_id=1, source_target_pairs={{0,17},{1,16},{2,19},{3,18},{4,21},{5,20},{6,23},{7,22},{8,25},{9,... | collective-permute-start | bytes 491528 | tf_op jit(solution)/shard_map/ppermute | solution.py:402
  22.2 0.0 collective-permute-done.3
  22.2 0.6 collective-permute-start.4
  22.8 0.0 collective-permute-done.5
  22.8 0.3 collective-permute-start.6
  23.1 0.0 collective-permute-done
  23.1 4.2 %collective-permute-done.2 = f32[320,128]{1,0:T(8,128)S(1)} collective-permute-done((f32[320,128]{1,0:T(8,128)S(1)}, f32[320,128]{1,0:T(8,128)S(1)}, u32[]{:S(2)}, u32[]{:S(2)}) %collective-permute-start.2) | collective-permute-done | bytes 163872 | tf_op jit(solution)/shard_map/ppermute | solution.py:402
  27.2 3.0 %collective-permute-done.4 = f32[320,128]{1,0:T(8,128)S(1)} collective-permute-done((f32[320,128]{1,0:T(8,128)S(1)}, f32[320,128]{1,0:T(8,128)S(1)}, u32[]{:S(2)}, u32[]{:S(2)}) %collective-permute-start.4) | collective-permute-done | bytes 163872 | tf_op jit(solution)/shard_map/ppermute | solution.py:402
  30.2 0.3 collective-permute-done.6
  30.5 0.1 add_add_fusion
  30.6 3.7 %collective-permute-start.7 = (f32[80,128]{1,0:T(8,128)S(1)}, f32[80,128]{1,0:T(8,128)S(1)}, u32[]{:S(2)}, u32[]{:S(2)}) collective-permute-start(f32[80,128]{1,0:T(8,128)S(1)} %get-tuple-element.20), channel_id=1, source_target_pairs={{0,6},{1,7},{2,4},{3,5},{4,2},{5,3},{6,0},{7,1},{8,14},{9,15},{10,... | collective-permute-start | bytes 122888 | tf_op jit(solution)/shard_map/ppermute | solution.py:402
  34.3 0.0 collective-permute-start.9
  34.3 0.8 %collective-permute-start.8 = (f32[80,128]{1,0:T(8,128)S(1)}, f32[80,128]{1,0:T(8,128)S(1)}, u32[]{:S(2)}, u32[]{:S(2)}) collective-permute-start(f32[80,128]{1,0:T(8,128)S(1)} %get-tuple-element.22), channel_id=1, source_target_pairs={{0,2},{1,3},{2,0},{3,1},{4,6},{5,7},{6,4},{7,5},{8,10},{9,11},{10,... | collective-permute-start | bytes 122888 | tf_op jit(solution)/shard_map/ppermute | solution.py:402
  35.1 1.5 %collective-permute-done.7 = f32[80,128]{1,0:T(8,128)S(1)} collective-permute-done((f32[80,128]{1,0:T(8,128)S(1)}, f32[80,128]{1,0:T(8,128)S(1)}, u32[]{:S(2)}, u32[]{:S(2)}) %collective-permute-start.7) | collective-permute-done | bytes 40992 | tf_op jit(solution)/shard_map/ppermute | solution.py:402
  36.5 2.6 %collective-permute-done.9 = f32[80,128]{1,0:T(8,128)S(1)} collective-permute-done((f32[80,128]{1,0:T(8,128)S(1)}, f32[80,128]{1,0:T(8,128)S(1)}, u32[]{:S(2)}, u32[]{:S(2)}) %collective-permute-start.9) | collective-permute-done | bytes 40992 | tf_op jit(solution)/shard_map/ppermute | solution.py:402
  39.2 0.0 collective-permute-done.8
  39.2 1.7 %collective-permute-start.12 = (f32[80,128]{1,0:T(8,128)S(1)}, f32[80,128]{1,0:T(8,128)S(1)}, u32[]{:S(2)}, u32[]{:S(2)}) collective-permute-start(f32[80,128]{1,0:T(8,128)S(1)} %fusion.1), channel_id=1, source_target_pairs={{0,6},{1,7},{2,4},{3,5},{4,2},{5,3},{6,0},{7,1},{8,14},{9,15},{10,... | collective-permute-start | bytes 122888 | tf_op jit(solution)/shard_map/ppermute | solution.py:402
  40.9 0.5 collective-permute-start.11
  41.4 2.3 %collective-permute-start.10 = (f32[80,128]{1,0:T(8,128)S(1)}, f32[80,128]{1,0:T(8,128)S(1)}, u32[]{:S(2)}, u32[]{:S(2)}) collective-permute-start(f32[80,128]{1,0:T(8,128)S(1)} %fusion.1), channel_id=1, source_target_pairs={{0,2},{1,3},{2,0},{3,1},{4,6},{5,7},{6,4},{7,5},{8,10},{9,11},{10,... | collective-permute-start | bytes 122888 | tf_op jit(solution)/shard_map/ppermute | solution.py:402
  43.7 1.4 %collective-permute-done.12 = f32[80,128]{1,0:T(8,128)S(1)} collective-permute-done((f32[80,128]{1,0:T(8,128)S(1)}, f32[80,128]{1,0:T(8,128)S(1)}, u32[]{:S(2)}, u32[]{:S(2)}) %collective-permute-start.12) | collective-permute-done | bytes 40992 | tf_op jit(solution)/shard_map/ppermute | solution.py:402
  45.1 0.7 collective-permute-done.11
  45.8 0.3 collective-permute-done.10
  46.1 1.8 %collective-permute-start.15 = (f32[320,128]{1,0:T(8,128)S(1)}, f32[320,128]{1,0:T(8,128)S(1)}, u32[]{:S(2)}, u32[]{:S(2)}) collective-permute-start(f32[320,128]{1,0:T(8,128)S(1)} %pad_maximum_fusion.refs_0_), channel_id=1, source_target_pairs={{0,17},{1,16},{2,19},{3,18},{4,21},{5,20},{6,23},{7,22},{8,25},{9,... | collective-permute-start | bytes 491528 | tf_op jit(solution)/shard_map/ppermute | solution.py:402
  47.9 1.1 %collective-permute-start.14 = (f32[320,128]{1,0:T(8,128)S(1)}, f32[320,128]{1,0:T(8,128)S(1)}, u32[]{:S(2)}, u32[]{:S(2)}) collective-permute-start(f32[320,128]{1,0:T(8,128)S(1)} %pad_maximum_fusion.refs_0_), channel_id=1, source_target_pairs={{0,1},{1,0},{2,3},{3,2},{4,5},{5,4},{6,7},{7,6},{8,9},{9,8},{10,11... | collective-permute-start | bytes 491528 | tf_op jit(solution)/shard_map/ppermute | solution.py:402
  49.1 0.6 collective-permute-start.13
  49.6 0.0 collective-permute-start.16
  49.6 3.5 %collective-permute-done.15.refs_3_ = f32[320,128]{1,0:T(8,128)S(1)} collective-permute-done((f32[320,128]{1,0:T(8,128)S(1)}, f32[320,128]{1,0:T(8,128)S(1)}, u32[]{:S(2)}, u32[]{:S(2)}) %collective-permute-start.15) | collective-permute-done | bytes 163872 | tf_op jit(solution)/shard_map/ppermute | solution.py:402
  53.1 0.0 collective-permute-start.19
  53.2 1.6 %collective-permute-done.14.refs_2_ = f32[320,128]{1,0:T(8,128)S(1)} collective-permute-done((f32[320,128]{1,0:T(8,128)S(1)}, f32[320,128]{1,0:T(8,128)S(1)}, u32[]{:S(2)}, u32[]{:S(2)}) %collective-permute-start.14) | collective-permute-done | bytes 163872 | tf_op jit(solution)/shard_map/ppermute | solution.py:402
  54.8 0.0 collective-permute-start.18
  54.8 0.1 collective-permute-done.13.refs_1_
  54.9 0.4 collective-permute-start.17
  55.3 0.0 collective-permute-done.16.refs_4_
  55.3 0.0 collective-permute-done.19.refs_7_
  55.3 0.9 %collective-permute-done.18.refs_6_ = f32[320,128]{1,0:T(8,128)S(1)} collective-permute-done((f32[320,128]{1,0:T(8,128)S(1)}, f32[320,128]{1,0:T(8,128)S(1)}, u32[]{:S(2)}, u32[]{:S(2)}) %collective-permute-start.18) | collective-permute-done | bytes 163872 | tf_op jit(solution)/shard_map/ppermute | solution.py:402
  56.2 0.2 collective-permute-done.17.refs_5_
  56.4 17.9 %first_section.1 = f32[96,768]{1,0:T(8,128)} custom-call(f32[320,128]{1,0:T(8,128)S(1)} %pad_maximum_fusion.refs_0_, f32[320,128]{1,0:T(8,128)S(1)} %collective-permute-done.13.refs_1_, f32[320,128]{1,0:T(8,128)S(1)} %collective-permute-done.14.refs_2_, f32[320,128]{1,0:T(8,128)S(1)} %collective-permute-done.15.refs_3_, ...), custom_call_target="tpu_custom_call" | custom-call | tf_op jit(solution)/shard_map/first_section/pallas_call | solution.py:380
  (6 shorter events, 0.1 us)
Async XLA Ops:
  16.7 1.6 %collective-permute-start.1 = (f32[320,128]{1,0:T(8,128)S(1)}, f32[320,128]{1,0:T(8,128)S(1)}, u32[]{:S(2)}, u32[]{:S(2)}) collective-permute-start(f32[320,128]{1,0:T(8,128)S(1)} %get-tuple-element.15), channel_id=1, source_target_pairs={{0,8},{1,9},{2,10},{3,11},{4,12},{5,13},{6,14},{7,15},{8,0},{9,1},... | collective-permute-start | bytes 491528 | tf_op jit(solution)/shard_map/ppermute | solution.py:402
  17.3 4.9 %collective-permute-start.3 = (f32[320,128]{1,0:T(8,128)S(1)}, f32[320,128]{1,0:T(8,128)S(1)}, u32[]{:S(2)}, u32[]{:S(2)}) collective-permute-start(f32[320,128]{1,0:T(8,128)S(1)} %get-tuple-element.17), channel_id=1, source_target_pairs={{0,8},{1,9},{2,10},{3,11},{4,12},{5,13},{6,14},{7,15},{8,0},{9,1},... | collective-permute-start | bytes 491528 | tf_op jit(solution)/shard_map/ppermute | solution.py:402
  17.4 5.4 %collective-permute-start.5 = (f32[320,128]{1,0:T(8,128)S(1)}, f32[320,128]{1,0:T(8,128)S(1)}, u32[]{:S(2)}, u32[]{:S(2)}) collective-permute-start(f32[320,128]{1,0:T(8,128)S(1)} %get-tuple-element.19), channel_id=1, source_target_pairs={{0,8},{1,9},{2,10},{3,11},{4,12},{5,13},{6,14},{7,15},{8,0},{9,1},... | collective-permute-start | bytes 491528 | tf_op jit(solution)/shard_map/ppermute | solution.py:402
  17.8 5.3 %collective-permute-start = (f32[320,128]{1,0:T(8,128)S(1)}, f32[320,128]{1,0:T(8,128)S(1)}, u32[]{:S(2)}, u32[]{:S(2)}) collective-permute-start(f32[320,128]{1,0:T(8,128)S(1)} %get-tuple-element.13), channel_id=1, source_target_pairs={{0,8},{1,9},{2,10},{3,11},{4,12},{5,13},{6,14},{7,15},{8,0},{9,1},... | collective-permute-start | bytes 491528 | tf_op jit(solution)/shard_map/ppermute | solution.py:402
  18.3 8.9 %collective-permute-start.2 = (f32[320,128]{1,0:T(8,128)S(1)}, f32[320,128]{1,0:T(8,128)S(1)}, u32[]{:S(2)}, u32[]{:S(2)}) collective-permute-start(f32[320,128]{1,0:T(8,128)S(1)} %add.31), channel_id=1, source_target_pairs={{0,17},{1,16},{2,19},{3,18},{4,21},{5,20},{6,23},{7,22},{8,25},{9,... | collective-permute-start | bytes 491528 | tf_op jit(solution)/shard_map/ppermute | solution.py:402
  22.2 8.0 %collective-permute-start.4 = (f32[320,128]{1,0:T(8,128)S(1)}, f32[320,128]{1,0:T(8,128)S(1)}, u32[]{:S(2)}, u32[]{:S(2)}) collective-permute-start(f32[320,128]{1,0:T(8,128)S(1)} %add.33), channel_id=1, source_target_pairs={{0,1},{1,0},{2,3},{3,2},{4,5},{5,4},{6,7},{7,6},{8,9},{9,8},{10,11... | collective-permute-start | bytes 491528 | tf_op jit(solution)/shard_map/ppermute | solution.py:402
  22.8 7.7 %collective-permute-start.6 = (f32[320,128]{1,0:T(8,128)S(1)}, f32[320,128]{1,0:T(8,128)S(1)}, u32[]{:S(2)}, u32[]{:S(2)}) collective-permute-start(f32[320,128]{1,0:T(8,128)S(1)} %add.35), channel_id=1, source_target_pairs={{0,16},{1,17},{2,18},{3,19},{4,20},{5,21},{6,22},{7,23},{8,24},{9,... | collective-permute-start | bytes 491528 | tf_op jit(solution)/shard_map/ppermute | solution.py:402
  30.6 5.9 %collective-permute-start.7 = (f32[80,128]{1,0:T(8,128)S(1)}, f32[80,128]{1,0:T(8,128)S(1)}, u32[]{:S(2)}, u32[]{:S(2)}) collective-permute-start(f32[80,128]{1,0:T(8,128)S(1)} %get-tuple-element.20), channel_id=1, source_target_pairs={{0,6},{1,7},{2,4},{3,5},{4,2},{5,3},{6,0},{7,1},{8,14},{9,15},{10,... | collective-permute-start | bytes 122888 | tf_op jit(solution)/shard_map/ppermute | solution.py:402
  34.3 4.9 %collective-permute-start.9 = (f32[80,128]{1,0:T(8,128)S(1)}, f32[80,128]{1,0:T(8,128)S(1)}, u32[]{:S(2)}, u32[]{:S(2)}) collective-permute-start(f32[80,128]{1,0:T(8,128)S(1)} %get-tuple-element.21), channel_id=1, source_target_pairs={{0,4},{1,5},{2,6},{3,7},{4,0},{5,1},{6,2},{7,3},{8,12},{9,13},{10,... | collective-permute-start | bytes 122888 | tf_op jit(solution)/shard_map/ppermute | solution.py:402
  34.3 4.9 %collective-permute-start.8 = (f32[80,128]{1,0:T(8,128)S(1)}, f32[80,128]{1,0:T(8,128)S(1)}, u32[]{:S(2)}, u32[]{:S(2)}) collective-permute-start(f32[80,128]{1,0:T(8,128)S(1)} %get-tuple-element.22), channel_id=1, source_target_pairs={{0,2},{1,3},{2,0},{3,1},{4,6},{5,7},{6,4},{7,5},{8,10},{9,11},{10,... | collective-permute-start | bytes 122888 | tf_op jit(solution)/shard_map/ppermute | solution.py:402
  39.2 5.9 %collective-permute-start.12 = (f32[80,128]{1,0:T(8,128)S(1)}, f32[80,128]{1,0:T(8,128)S(1)}, u32[]{:S(2)}, u32[]{:S(2)}) collective-permute-start(f32[80,128]{1,0:T(8,128)S(1)} %fusion.1), channel_id=1, source_target_pairs={{0,6},{1,7},{2,4},{3,5},{4,2},{5,3},{6,0},{7,1},{8,14},{9,15},{10,... | collective-permute-start | bytes 122888 | tf_op jit(solution)/shard_map/ppermute | solution.py:402
  40.9 4.9 %collective-permute-start.11 = (f32[80,128]{1,0:T(8,128)S(1)}, f32[80,128]{1,0:T(8,128)S(1)}, u32[]{:S(2)}, u32[]{:S(2)}) collective-permute-start(f32[80,128]{1,0:T(8,128)S(1)} %fusion.1), channel_id=1, source_target_pairs={{0,4},{1,5},{2,6},{3,7},{4,0},{5,1},{6,2},{7,3},{8,12},{9,13},{10,... | collective-permute-start | bytes 122888 | tf_op jit(solution)/shard_map/ppermute | solution.py:402
  41.4 4.7 %collective-permute-start.10 = (f32[80,128]{1,0:T(8,128)S(1)}, f32[80,128]{1,0:T(8,128)S(1)}, u32[]{:S(2)}, u32[]{:S(2)}) collective-permute-start(f32[80,128]{1,0:T(8,128)S(1)} %fusion.1), channel_id=1, source_target_pairs={{0,2},{1,3},{2,0},{3,1},{4,6},{5,7},{6,4},{7,5},{8,10},{9,11},{10,... | collective-permute-start | bytes 122888 | tf_op jit(solution)/shard_map/ppermute | solution.py:402
  46.1 7.1 %collective-permute-start.15 = (f32[320,128]{1,0:T(8,128)S(1)}, f32[320,128]{1,0:T(8,128)S(1)}, u32[]{:S(2)}, u32[]{:S(2)}) collective-permute-start(f32[320,128]{1,0:T(8,128)S(1)} %pad_maximum_fusion.refs_0_), channel_id=1, source_target_pairs={{0,17},{1,16},{2,19},{3,18},{4,21},{5,20},{6,23},{7,22},{8,25},{9,... | collective-permute-start | bytes 491528 | tf_op jit(solution)/shard_map/ppermute | solution.py:402
  47.9 6.8 %collective-permute-start.14 = (f32[320,128]{1,0:T(8,128)S(1)}, f32[320,128]{1,0:T(8,128)S(1)}, u32[]{:S(2)}, u32[]{:S(2)}) collective-permute-start(f32[320,128]{1,0:T(8,128)S(1)} %pad_maximum_fusion.refs_0_), channel_id=1, source_target_pairs={{0,1},{1,0},{2,3},{3,2},{4,5},{5,4},{6,7},{7,6},{8,9},{9,8},{10,11... | collective-permute-start | bytes 491528 | tf_op jit(solution)/shard_map/ppermute | solution.py:402
  49.1 5.8 %collective-permute-start.13 = (f32[320,128]{1,0:T(8,128)S(1)}, f32[320,128]{1,0:T(8,128)S(1)}, u32[]{:S(2)}, u32[]{:S(2)}) collective-permute-start(f32[320,128]{1,0:T(8,128)S(1)} %pad_maximum_fusion.refs_0_), channel_id=1, source_target_pairs={{0,16},{1,17},{2,18},{3,19},{4,20},{5,21},{6,22},{7,23},{8,24},{9,... | collective-permute-start | bytes 491528 | tf_op jit(solution)/shard_map/ppermute | solution.py:402
  49.6 5.7 %collective-permute-start.16 = (f32[320,128]{1,0:T(8,128)S(1)}, f32[320,128]{1,0:T(8,128)S(1)}, u32[]{:S(2)}, u32[]{:S(2)}) collective-permute-start(f32[320,128]{1,0:T(8,128)S(1)} %pad_maximum_fusion.refs_0_), channel_id=1, source_target_pairs={{0,8},{1,9},{2,10},{3,11},{4,12},{5,13},{6,14},{7,15},{8,0},{9,1},... | collective-permute-start | bytes 491528 | tf_op jit(solution)/shard_map/ppermute | solution.py:402
  53.1 2.1 %collective-permute-start.19 = (f32[320,128]{1,0:T(8,128)S(1)}, f32[320,128]{1,0:T(8,128)S(1)}, u32[]{:S(2)}, u32[]{:S(2)}) collective-permute-start(f32[320,128]{1,0:T(8,128)S(1)} %collective-permute-done.15.refs_3_), channel_id=1, source_target_pairs={{0,8},{1,9},{2,10},{3,11},{4,12},{5,13},{6,14},{7,15},{8,0},{9,1},... | collective-permute-start | bytes 491528 | tf_op jit(solution)/shard_map/ppermute | solution.py:402
  54.8 1.4 %collective-permute-start.18 = (f32[320,128]{1,0:T(8,128)S(1)}, f32[320,128]{1,0:T(8,128)S(1)}, u32[]{:S(2)}, u32[]{:S(2)}) collective-permute-start(f32[320,128]{1,0:T(8,128)S(1)} %collective-permute-done.14.refs_2_), channel_id=1, source_target_pairs={{0,8},{1,9},{2,10},{3,11},{4,12},{5,13},{6,14},{7,15},{8,0},{9,1},... | collective-permute-start | bytes 491528 | tf_op jit(solution)/shard_map/ppermute | solution.py:402
  54.9 1.5 %collective-permute-start.17 = (f32[320,128]{1,0:T(8,128)S(1)}, f32[320,128]{1,0:T(8,128)S(1)}, u32[]{:S(2)}, u32[]{:S(2)}) collective-permute-start(f32[320,128]{1,0:T(8,128)S(1)} %collective-permute-done.13.refs_1_), channel_id=1, source_target_pairs={{0,8},{1,9},{2,10},{3,11},{4,12},{5,13},{6,14},{7,15},{8,0},{9,1},... | collective-permute-start | bytes 491528 | tf_op jit(solution)/shard_map/ppermute | solution.py:402
